TPU v7x, 128 devices: a whole 4x4x4 slice. The times are simulated.
128 devices in a mesh: seq: 4 (over x), tp: 32 (over z, y, core).
Axes of the slice: x: 4, y: 4, z: 4, core: 2. Of those that a mesh axis runs over, the one named last changes fastest.
Arguments:
- hidden_in: bfloat16 [96, 4, 1024], P('tp'), may hold values from -6 to 6
- new_query: bfloat16 [96, 4, 1024], P('tp'), may hold values from -70 to 70
- new_key: bfloat16 [96, 4, 1024], P('tp'), may hold values from -15 to 15
- new_value: bfloat16 [96, 4, 1024], P('tp'), may hold values from -6 to 6
- key_cache: bfloat16 [96, 4096, 1024], P('tp', 'seq'), may hold values from -16 to 16
- value_cache: bfloat16 [96, 4096, 1024], P('tp', 'seq'), may hold values from -6 to 6
- lengths: int32 [96], P('tp'), may hold values from 64 to 4096, as said below
- out_weight: bfloat16 [1024, 1024], replicated, may hold values from -0.1875 to 0.1875
- norm_gain: float32 [1024], replicated, may hold values from 0.5 to 1.5
- router_weight: bfloat16 [1024, 16], replicated, may hold values from -0.1875 to 0.1875
- expert_ids: int32 [96, 4, 2], P('tp'), may hold values from 0 to 15, all different within a row
- gate_weight: bfloat16 [45056, 1024], P(('seq', 'tp')), may hold values from -0.1875 to 0.1875
- up_weight: bfloat16 [45056, 1024], P(('seq', 'tp')), may hold values from -0.1875 to 0.1875
- down_weight: bfloat16 [45056, 1024], P(('seq', 'tp')), may hold values from -0.109375 to 0.109375
Outputs:
- attn_out: bfloat16 [96, 4, 1024], P('tp', None, 'seq')
- layer_out: bfloat16 [96, 4, 1024], P('tp', None, 'seq')
Inputs may be any that keep to these rules, and one draw needn't show every extreme that they name: `lengths`: each length is 4096 or between 64 and 128; some request has 4096.
All inputs are finite; a program needn't handle non-finite values.
Results may differ from a plain program's by a relative error of at most 0.014.
Values may be sent and summed in bfloat16 or wider, within the bound.
A program may use at most 64 MiB of HBM per device.

v0:
```python
import jax
import jax.numpy as jnp
from jax import lax
from jax.sharding import PartitionSpec as P

HEADS = 16


masked_score = -1e30
norm_epsilon = 1e-06


def entering(part, axis, combine, identity):
    place = lax.axis_index(axis)
    gathered = lax.all_gather(part, axis)
    state = jnp.zeros_like(part) + jnp.asarray(identity, part.dtype)

    def one(turn, state):
        return combine(state, lax.dynamic_index_in_dim(gathered, turn, 0, False))

    return lax.fori_loop(0, place, one, state)


def add_counts(former, latter):
    return former + latter


def pick_slot(chosen_ids, earlier):
    onehot = chosen_ids[..., None] == jnp.arange(earlier.shape[2], dtype=jnp.int32)
    return jnp.sum(jnp.where(onehot, earlier[:, :, None, :], 0), axis=3)


def body(
    hidden_in,
    new_query,
    new_key,
    new_value,
    key_cache,
    value_cache,
    lengths,
    out_weight,
    norm_gain,
    router_weight,
    expert_ids,
    gate_weight,
    up_weight,
    down_weight,
):
    req_dev, steps, width = hidden_in.shape
    block = key_cache.shape[1]
    head_size = width // HEADS
    scale = head_size ** (-0.5)
    seq_index = lax.axis_index("seq")
    tp_index = lax.axis_index("tp")
    seq_size = lax.axis_size("seq")
    tp_size = lax.axis_size("tp")
    queries = new_query.reshape(req_dev, steps, HEADS, head_size)
    cache_keys = key_cache.reshape(req_dev, block, HEADS, head_size)
    cache_values = value_cache.reshape(req_dev, block, HEADS, head_size)
    fresh_keys = new_key.reshape(req_dev, steps, HEADS, head_size)
    fresh_values = new_value.reshape(req_dev, steps, HEADS, head_size)
    scores = (
        jnp.einsum("rthe,rphe->rhtp", queries, cache_keys, preferred_element_type=jnp.float32)
        * scale
    )
    positions = seq_index * block + jnp.arange(block, dtype=jnp.int32)
    usable = (positions[None, :] < lengths[:, None])[:, None, None, :]
    scores = jnp.where(usable, scores, masked_score)
    fresh_scores = (
        jnp.einsum("rthe,rshe->rhts", queries, fresh_keys, preferred_element_type=jnp.float32)
        * scale
    )
    causal = (jnp.arange(steps)[:, None] >= jnp.arange(steps)[None, :]) & (seq_index == 0)
    fresh_scores = jnp.where(causal, fresh_scores, masked_score)
    local_max = jnp.maximum(jnp.max(scores, axis=3), jnp.max(fresh_scores, axis=3))
    weights = jnp.where(usable, jnp.exp(scores - local_max[..., None]), 0.0)
    fresh_weights = jnp.where(causal, jnp.exp(fresh_scores - local_max[..., None]), 0.0)
    totals = jnp.sum(weights, axis=3) + jnp.sum(fresh_weights, axis=3)
    gathered_values = jnp.einsum(
        "rhtp,rphe->rhte",
        weights.astype(jnp.bfloat16),
        cache_values,
        preferred_element_type=jnp.float32,
    )
    gathered_values = gathered_values + jnp.einsum(
        "rhts,rshe->rhte",
        fresh_weights.astype(jnp.bfloat16),
        fresh_values,
        preferred_element_type=jnp.float32,
    )
    overall = lax.pmax(local_max, "seq")
    factors = jnp.exp(local_max - overall)
    totals, gathered_values = (
        lax.psum((totals * factors).astype(jnp.bfloat16), "seq").astype(jnp.float32),
        lax.psum((gathered_values * factors[..., None]).astype(jnp.bfloat16), "seq").astype(
            jnp.float32
        ),
    )
    context = (
        (gathered_values / totals[..., None])
        .transpose(0, 2, 1, 3)
        .reshape(req_dev, steps, width)
        .astype(jnp.bfloat16)
    )
    attention = jnp.einsum("rtd,de->rte", context, out_weight, preferred_element_type=jnp.float32)
    feature_block = width // seq_size
    attn_out = lax.dynamic_slice_in_dim(
        attention, seq_index * feature_block, feature_block, 2
    ).astype(jnp.bfloat16)
    residual = hidden_in.astype(jnp.float32) + attention
    normed = (
        residual
        * lax.rsqrt(jnp.mean(residual * residual, axis=-1, keepdims=True) + norm_epsilon)
        * norm_gain
    ).astype(jnp.bfloat16)
    experts = router_weight.shape[1]
    topk = expert_ids.shape[2]
    requests = req_dev * tp_size
    capacity = (5 * requests * topk + 4 * experts - 1) // (4 * experts)
    expert_range = jnp.arange(experts, dtype=jnp.int32)
    local_hits = jnp.sum((expert_ids[..., None] == expert_range).astype(jnp.int32), axis=2)
    counts = jnp.sum(local_hits, axis=0)
    before = entering(counts, "tp", add_counts, jnp.zeros_like(counts))
    earlier = (before[None] + jnp.cumsum(local_hits, axis=0) - local_hits).astype(jnp.int32)
    routing = jnp.concatenate([expert_ids, pick_slot(expert_ids, earlier)], axis=2)
    all_routing = lax.all_gather(routing, "tp", axis=0, tiled=True)
    all_ids = all_routing[:, :, :topk]
    all_slots = all_routing[:, :, topk:]
    all_normed = lax.all_gather(normed, "tp", axis=0, tiled=True)
    logits = jnp.einsum(
        "rtd,de->rte", all_normed, router_weight, preferred_element_type=jnp.float32
    )
    onehot = all_ids[..., None] == expert_range
    chosen = jnp.sum(jnp.where(onehot, logits[:, :, None, :], 0.0), axis=3)
    share = 1.0 / (1.0 + jnp.exp(chosen[:, :, ::-1] - chosen))
    slices = seq_size * tp_size // experts
    mine = (seq_index * tp_size + tp_index) // slices
    match = all_ids == mine
    slot_mine = jnp.sum(jnp.where(match, all_slots, 0), axis=2)
    share_mine = jnp.sum(jnp.where(match, share, 0.0), axis=2)
    kept = jnp.any(match, axis=2) & (slot_mine < capacity)
    select = kept[None] & (slot_mine[None] == jnp.arange(capacity, dtype=jnp.int32)[:, None, None])
    buffer = (
        jnp.einsum(
            "crt,rtd->tcd",
            select.astype(jnp.bfloat16),
            all_normed,
            preferred_element_type=jnp.float32,
        )
        .astype(jnp.bfloat16)
        .reshape(steps * capacity, width)
    )
    contract = (((1,), (1,)), ((), ()))
    gate = lax.dot_general(buffer, gate_weight, contract, preferred_element_type=jnp.float32)
    upward = lax.dot_general(buffer, up_weight, contract, preferred_element_type=jnp.float32)
    inner = (jax.nn.gelu(gate) * upward).astype(jnp.bfloat16)
    produced = jnp.dot(inner, down_weight, preferred_element_type=jnp.float32)
    placed = select.astype(jnp.float32) * share_mine[None]
    term = jnp.einsum(
        "crt,tcd->rtd",
        placed,
        produced.reshape(steps, capacity, width),
        precision=lax.Precision.HIGHEST,
    )
    row_sums = lax.psum_scatter(term.astype(jnp.bfloat16), "tp", scatter_dimension=0, tiled=True)
    mixture = lax.psum_scatter(row_sums, "seq", scatter_dimension=2, tiled=True).astype(jnp.float32)
    own_residual = lax.dynamic_slice_in_dim(residual, seq_index * feature_block, feature_block, 2)
    layer_out = (own_residual + mixture).astype(jnp.bfloat16)
    return (attn_out, layer_out)


def solution(mesh):
    return jax.shard_map(
        body,
        mesh=mesh,
        in_specs=(
            P("tp", None, None),
            P("tp", None, None),
            P("tp", None, None),
            P("tp", None, None),
            P("tp", "seq", None),
            P("tp", "seq", None),
            P("tp"),
            P(),
            P(),
            P(),
            P("tp", None, None),
            P(("seq", "tp"), None),
            P(("seq", "tp"), None),
            P(("seq", "tp"), None),
        ),
        out_specs=(P("tp", None, "seq"), P("tp", None, "seq")),
        check_vma=False,
    )
```

profile of v0, /device:TPU:1, one launch (start us, length us, event | category | flops | bytes accessed | tf_op | source)
XLA Modules:
  0.0 283.4 jit_solution(4095929092177931425)
XLA Ops:
  7.2 1.0 reshape.92
  8.2 8.7 %copy.131 = bf16[3,1024,1024]{1,2,0:T(8,128)(2,1)} copy(bf16[3,1024,1024]{2,1,0:T(8,128)(2,1)} %param.20) | data formatting | bytes 12582912 | tf_op args[4]
  17.0 0.2 fusion.30
  17.6 3.8 %fusion.61 = (f32[3,16,4]{2,1,0:T(8,128)S(1)}, f32[3,16,4,1024]{3,2,1,0:T(4,128)S(1)}) fusion(bf16[3,1024,16,64]{1,3,2,0:T(8,128)(2,1)} %bitcast.35, bf16[3,4,16,64]{3,2,1,0:T(8,128)(2,1)S(1)} %reshape.92, pred[3,1024]{1,0:T(4,128)(4,1)S(1)} %broadcast_compare_fusion), kind=kOutput, calls=%fused_computation.93 | convolution fusion | flops 25755456 | bytes 7106304 | tf_op jit(solution)/shard_map/rthe,rphe->rhtp/dot_general | solution.py:63
  21.5 14.1 %pmax.7 = f32[3,16,4]{2,1,0:T(8,128)S(1)} all-reduce(f32[3,16,4]{2,1,0:T(8,128)S(1)} %max.9), channel_id=1, replica_groups=mesh['seq'=4,'tp'=32] {'seq'}, use_global_device_ids=true, to_apply=%region_2.3 | all-reduce | flops 192 | bytes 1536 | tf_op jit(solution)/shard_map/pmax | solution.py:91
  35.6 0.5 fusion.12
  36.3 8.6 %copy.137 = bf16[3,1024,1024]{1,2,0:T(8,128)(2,1)} copy(bf16[3,1024,1024]{2,1,0:T(8,128)(2,1)} %param.21) | data formatting | bytes 12582912 | tf_op args[5]
  45.0 4.6 %fusion.14 = f32[3,16,4,64]{3,2,1,0:T(4,128)S(1)} fusion(bf16[3,1024,16,64]{1,3,2,0:T(8,128)(2,1)} %bitcast.36, f32[3,16,4,1024]{3,2,1,0:T(4,128)S(1)} %get-tuple-element.49, f32[3,16,4]{2,1,0:T(8,128)S(1)} %max.9, pred[3,1024]{1,0:T(4,128)(4,1)S(1)} %broadcast_compare_fusion), kind=kOutput, calls=%fused_computation.22 | convolution fusion | flops 25755648 | bytes 7130880 | tf_op jit(solution)/shard_map/rhtp,rphe->rhte/dot_general | solution.py:79
  49.6 0.2 copy.139
  49.9 0.2 fusion.5
  50.1 11.4 %all-reduce.1 = (bf16[3,16,4,64]{3,2,1,0:T(4,128)(2,1)S(1)}, bf16[3,16,4]{2,1,0:T(8,128)(2,1)S(1)}) all-reduce(bf16[3,16,4,64]{3,2,1,0:T(4,128)(2,1)S(1)} %fusion.5, bf16[3,16,4]{2,1,0:T(8,128)(2,1)S(1)} %get-tuple-element.42), channel_id=1, replica_groups=mesh['seq'=4,'tp'=32] {'seq'}, use_global_device_ids=true, to_apply=%region_3.4 | all-reduce | flops 12480 | bytes 49920 | tf_op jit(solution)/shard_map/psum | solution.py:95
  61.8 0.5 multiply_reduce_fusion
  62.4 34.1 %all_gather.15 = bf16[96,4,1024]{2,1,0:T(4,128)(2,1)S(1)} all-gather(bf16[3,4,1024]{2,1,0:T(4,128)(2,1)S(1)} %multiply_convert_fusion), channel_id=1, replica_groups=mesh['seq'=4,'tp'=32] {'tp'}, dimensions={0}, use_global_device_ids=true | all-gather | bytes 811008 | tf_op jit(solution)/shard_map/all_gather | solution.py:129
  96.6 23.6 %all-gather.1 = s32[32,4,16]{2,1,0:T(4,128)S(1)} all-gather(s32[1,4,16]{2,1,0:T(4,128)S(1)} %bitcast.39), channel_id=2, replica_groups=mesh['seq'=4,'tp'=32] {'tp'}, dimensions={0}, use_global_device_ids=true | all-gather | bytes 8448 | tf_op jit(solution)/shard_map/all_gather | solution.py:15
  120.3 0.3 select_reduce_fusion.1
  120.6 23.5 %all_gather.14 = s32[96,4,4]{2,1,0:T(4,128)S(1)} all-gather(s32[3,4,4]{2,1,0:T(4,128)S(1)} %copy.143), channel_id=1, replica_groups=mesh['seq'=4,'tp'=32] {'tp'}, dimensions={0}, use_global_device_ids=true | all-gather | bytes 6336 | tf_op jit(solution)/shard_map/all_gather | solution.py:126
  144.1 0.2 fusion.60
  144.4 0.4 fusion.9
  145.1 0.5 convolution_convert_fusion.1
  145.7 1.5 fusion.62
  147.2 2.0 fusion.7
  149.2 1.4 fusion.2
  150.7 1.5 copy.155
  152.3 0.6 dynamic-slice
  153.5 100.6 %all-reduce.4.cloned.1.call-done = bf16[96,4,1024]{2,1,0:T(4,128)(2,1)} async-done(((bf16[96,4,1024]{2,1,0:T(4,128)(2,1)}), bf16[96,4,1024]{2,1,0:T(4,128)(2,1)}) %all-reduce.4.cloned.1.call-update) | async-done | bytes 786448
  254.1 0.7 constant_dynamic-slice_fusion
  254.9 0.7 copy.156
  255.6 1.2 reshape.105
  256.8 0.6 dynamic-slice_convert_fusion
  257.4 17.4 %reduce-scatter.4.cloned.1.call-done = bf16[256,12]{1,0:T(8,128)(2,1)} async-done(((bf16[1024,12]{1,0:T(8,128)(2,1)}), bf16[256,12]{1,0:T(8,128)(2,1)}) %reduce-scatter.4.cloned.1.call-update) | async-done | bytes 6160
  274.8 1.0 reshape.106
  275.9 0.6 add_convert_fusion
  (59 shorter events, 2.3 us)
Async XLA Ops:
  7.2 54.6 %copy-start = (bf16[1024,1024]{1,0:T(8,128)(2,1)S(1)}, bf16[1024,1024]{1,0:T(8,128)(2,1)}, u32[]{:S(2)}) copy-start(bf16[1024,1024]{1,0:T(8,128)(2,1)} %param.23) | copy-start | bytes 6291460
  7.2 246.9 %all-reduce.4.cloned.1.call-start = ((), (), s32[]{:S(2)}) async-start(), calls=%async_computation.2 | async-start | bytes 1572864
  8.2 8.7 %copy-start.3 = (bf16[3,4,1024]{2,1,0:T(4,128)(2,1)S(1)}, bf16[3,4,1024]{2,1,0:T(4,128)(2,1)}, u32[]{:S(2)}) copy-start(bf16[3,4,1024]{2,1,0:T(4,128)(2,1)} %param.18) | copy-start | bytes 73732
  8.2 9.3 %copy-start.6 = (s32[3]{0:T(128)S(1)}, s32[3]{0:T(128)}, u32[]{:S(2)}) copy-start(s32[3]{0:T(128)} %param.22) | copy-start | bytes 40
  45.0 4.8 %copy-start.4 = (bf16[3,4,1024]{2,1,0:T(4,128)(2,1)S(1)}, bf16[3,4,1024]{2,1,0:T(4,128)(2,1)}, u32[]{:S(2)}) copy-start(bf16[3,4,1024]{2,1,0:T(4,128)(2,1)} %param.19) | copy-start | bytes 73732
  45.0 16.8 %copy-start.2 = (bf16[3,4,1024]{2,1,0:T(4,128)(2,1)S(1)}, bf16[3,4,1024]{2,1,0:T(4,128)(2,1)}, u32[]{:S(2)}) copy-start(bf16[3,4,1024]{2,1,0:T(4,128)(2,1)} %param.16) | copy-start | bytes 73732
  45.0 17.3 %copy-start.5 = (f32[1024]{0:T(1024)S(1)}, f32[1024]{0:T(1024)}, u32[]{:S(2)}) copy-start(f32[1024]{0:T(1024)} %param.24) | copy-start | bytes 12292
  45.0 51.6 %copy-start.1 = (s32[3,4,2]{1,2,0:T(2,128)S(1)}, s32[3,4,2]{1,2,0:T(2,128)}, u32[]{:S(2)}) copy-start(s32[3,4,2]{1,2,0:T(2,128)} %param.26) | copy-start | bytes 292
  45.0 99.5 %copy-start.7 = (bf16[1024,16]{0,1:T(8,128)(2,1)S(1)}, bf16[1024,16]{0,1:T(8,128)(2,1)}, u32[]{:S(2)}) copy-start(bf16[1024,16]{0,1:T(8,128)(2,1)} %param.25) | copy-start | bytes 98308
  62.3 90.0 %copy-start.8 = (u32[128]{0:T(128)S(1)}, u32[128]{0:T(128)}, u32[]{:S(2)}) copy-start(u32[128]{0:T(128)} %constant.85) | copy-start | bytes 1540
  152.2 122.6 %reduce-scatter.4.cloned.1.call-start = ((), (), s32[]{:S(2)}) async-start(), calls=%async_computation.1 | async-start | bytes 327680
Sparse Core Ops, SparseCore 0:
  152.3 101.7 all-reduce.3
  256.9 17.8 reduce-scatter.3
where the time goes:
time: 286 us; the launch traced here: 283 us
  waiting for transfers between devices  118 us (41%)
  blocking collectives  107 us (37%)
  local copies, waits for them, and re-layouts  26.3 us (9%)
  matrix products  15.1 us (5%)
  between operations  15 us (5%)
    unnamed x4, waiting for transfers between devices  118 us
    all_gather x1, blocking collectives, body(): all_normed = lax.all_gather(normed, 'tp', axis=0, tiled=True)  34.1 us
    all_gather x1, blocking collectives, entering(): gathered = lax.all_gather(part, axis)  23.6 us
    all_gather x1, blocking collectives, body(): all_routing = lax.all_gather(routing, 'tp', axis=0, tiled=True)  23.5 us
    unnamed x28, local copies, waits for them, and re-layouts  21.9 us
    pmax x1, blocking collectives, body(): overall = lax.pmax(local_max, 'seq')  14.1 us
    psum x1, blocking collectives, body(): lax.psum((gathered_values * factors[..., None]).astype(jnp.bfloat16), 'seq')  11.4 us
  transfers between devices with their start and end apart: 2, of which 2 were waited for; matrix products, arithmetic and copies ran while one was open for 0% of the time, Pallas kernels for 0%

commit v1 on v0

v1 whole, which is shorter than its diff:
```python
import jax
import jax.numpy as jnp
from jax import lax
from jax.sharding import PartitionSpec as P

HEADS = 16


masked_score = -1e30
norm_epsilon = 1e-06


def body(
    hidden_in,
    new_query,
    new_key,
    new_value,
    key_cache,
    value_cache,
    lengths,
    out_weight,
    norm_gain,
    router_weight,
    expert_ids,
    gate_weight,
    up_weight,
    down_weight,
):
    req_dev, steps, width = hidden_in.shape
    block = key_cache.shape[1]
    head_size = width // HEADS
    scale = head_size ** (-0.5)
    seq_index = lax.axis_index("seq")
    tp_index = lax.axis_index("tp")
    seq_size = lax.axis_size("seq")
    tp_size = lax.axis_size("tp")
    rows = steps * HEADS

    head_mask = (jnp.arange(width) // head_size)[None, :] == jnp.arange(HEADS)[:, None]
    q_wide = jnp.where(head_mask[None, None], new_query[:, :, None, :], 0).reshape(
        req_dev, rows, width
    )
    with jax.named_scope("cache_scores"):
        scores = (
            jnp.einsum("rqd,rpd->rqp", q_wide, key_cache, preferred_element_type=jnp.float32)
            * scale
        )
    positions = seq_index * block + jnp.arange(block, dtype=jnp.int32)
    usable = (positions[None, :] < lengths[:, None])[:, None, :]
    scores = jnp.where(usable, scores, masked_score)
    fresh_scores = (
        jnp.einsum("rqd,rsd->rqs", q_wide, new_key, preferred_element_type=jnp.float32) * scale
    )
    causal = (
        (jnp.arange(rows)[:, None] // HEADS) >= jnp.arange(steps)[None, :]
    ) & (seq_index == 0)
    fresh_scores = jnp.where(causal, fresh_scores, masked_score)
    local_max = jnp.maximum(jnp.max(scores, axis=2), jnp.max(fresh_scores, axis=2))
    weights = jnp.where(usable, jnp.exp(scores - local_max[..., None]), 0.0)
    fresh_weights = jnp.where(causal, jnp.exp(fresh_scores - local_max[..., None]), 0.0)
    totals = jnp.sum(weights, axis=2) + jnp.sum(fresh_weights, axis=2)
    with jax.named_scope("cache_values"):
        wide_values = jnp.einsum(
            "rqp,rpd->rqd",
            weights.astype(jnp.bfloat16),
            value_cache,
            preferred_element_type=jnp.float32,
        )
    wide_values = wide_values + jnp.einsum(
        "rqs,rsd->rqd",
        fresh_weights.astype(jnp.bfloat16),
        new_value,
        preferred_element_type=jnp.float32,
    )
    partial = jnp.sum(
        jnp.where(head_mask[None, None], wide_values.reshape(req_dev, steps, HEADS, width), 0.0),
        axis=2,
    )
    stats = jnp.concatenate(
        [
            partial,
            local_max.reshape(req_dev, steps, HEADS),
            totals.reshape(req_dev, steps, HEADS),
        ],
        axis=2,
    )
    every = lax.all_gather(stats, "seq")
    block_sums = every[..., :width]
    block_max = every[..., width : width + HEADS]
    block_totals = every[..., width + HEADS :]
    overall = jnp.max(block_max, axis=0)
    factors = jnp.exp(block_max - overall[None])
    numer = jnp.sum(jnp.repeat(factors, head_size, axis=-1) * block_sums, axis=0)
    denom = jnp.sum(factors * block_totals, axis=0)
    context = (numer / jnp.repeat(denom, head_size, axis=-1)).astype(jnp.bfloat16)
    attention = jnp.einsum("rtd,de->rte", context, out_weight, preferred_element_type=jnp.float32)
    feature_block = width // seq_size
    attn_out = lax.dynamic_slice_in_dim(
        attention, seq_index * feature_block, feature_block, 2
    ).astype(jnp.bfloat16)
    residual = hidden_in.astype(jnp.float32) + attention
    normed = (
        residual
        * lax.rsqrt(jnp.mean(residual * residual, axis=-1, keepdims=True) + norm_epsilon)
        * norm_gain
    ).astype(jnp.bfloat16)
    experts = router_weight.shape[1]
    topk = expert_ids.shape[2]
    requests = req_dev * tp_size
    capacity = (5 * requests * topk + 4 * experts - 1) // (4 * experts)
    expert_range = jnp.arange(experts, dtype=jnp.int32)
    packed = jnp.concatenate([normed, expert_ids.astype(jnp.bfloat16)], axis=2)
    all_packed = lax.all_gather(packed, "tp", axis=0, tiled=True)
    all_normed = all_packed[:, :, :width]
    all_ids = all_packed[:, :, width:].astype(jnp.int32)
    onehot = all_ids[..., None] == expert_range
    hits = jnp.sum(onehot.astype(jnp.int32), axis=2)
    earlier = jnp.cumsum(hits, axis=0) - hits
    all_slots = jnp.sum(jnp.where(onehot, earlier[:, :, None, :], 0), axis=3)
    logits = jnp.einsum(
        "rtd,de->rte", all_normed, router_weight, preferred_element_type=jnp.float32
    )
    chosen = jnp.sum(jnp.where(onehot, logits[:, :, None, :], 0.0), axis=3)
    share = 1.0 / (1.0 + jnp.exp(chosen[:, :, ::-1] - chosen))
    slices = seq_size * tp_size // experts
    mine = (seq_index * tp_size + tp_index) // slices
    match = all_ids == mine
    slot_mine = jnp.sum(jnp.where(match, all_slots, 0), axis=2)
    share_mine = jnp.sum(jnp.where(match, share, 0.0), axis=2)
    kept = jnp.any(match, axis=2) & (slot_mine < capacity)
    select = kept[None] & (slot_mine[None] == jnp.arange(capacity, dtype=jnp.int32)[:, None, None])
    buffer = (
        jnp.einsum(
            "crt,rtd->tcd",
            select.astype(jnp.bfloat16),
            all_normed,
            preferred_element_type=jnp.float32,
        )
        .astype(jnp.bfloat16)
        .reshape(steps * capacity, width)
    )
    contract = (((1,), (1,)), ((), ()))
    gate = lax.dot_general(buffer, gate_weight, contract, preferred_element_type=jnp.float32)
    upward = lax.dot_general(buffer, up_weight, contract, preferred_element_type=jnp.float32)
    inner = (jax.nn.gelu(gate) * upward).astype(jnp.bfloat16)
    produced = jnp.dot(inner, down_weight, preferred_element_type=jnp.float32)
    placed = select.astype(jnp.float32) * share_mine[None]
    term = jnp.einsum(
        "crt,tcd->rtd",
        placed,
        produced.reshape(steps, capacity, width),
        precision=lax.Precision.HIGHEST,
    )
    term = (
        term.astype(jnp.bfloat16)
        .reshape(tp_size, req_dev, steps, seq_size, feature_block)
        .transpose(0, 3, 1, 2, 4)
        .reshape(tp_size * seq_size, req_dev, steps, feature_block)
    )
    term = term.reshape(tp_size * seq_size, req_dev * steps, feature_block).transpose(1, 0, 2)
    term = term.reshape(req_dev * steps, tp_size * seq_size * feature_block)
    mixture = lax.psum_scatter(term, ("tp", "seq"), scatter_dimension=1, tiled=True)
    mixture = mixture.reshape(req_dev, steps, feature_block).astype(jnp.float32)
    own_residual = lax.dynamic_slice_in_dim(residual, seq_index * feature_block, feature_block, 2)
    layer_out = (own_residual + mixture).astype(jnp.bfloat16)
    return (attn_out, layer_out)


def solution(mesh):
    return jax.shard_map(
        body,
        mesh=mesh,
        in_specs=(
            P("tp", None, None),
            P("tp", None, None),
            P("tp", None, None),
            P("tp", None, None),
            P("tp", "seq", None),
            P("tp", "seq", None),
            P("tp"),
            P(),
            P(),
            P(),
            P("tp", None, None),
            P(("seq", "tp"), None),
            P(("seq", "tp"), None),
            P(("seq", "tp"), None),
        ),
        out_specs=(P("tp", None, "seq"), P("tp", None, "seq")),
        check_vma=False,
    )
```

time: 286 us -> 722 us (2.52)
  waiting for transfers between devices: 118 us -> 629 us
  blocking collectives: 107 us -> 40.3 us
  local copies, waits for them, and re-layouts: 26.3 us -> 9.41 us
    reduce_scatter x0 -> x1, waiting for transfers between devices: none -> 629 us  [body(): lax.psum_scatter(term, ('tp', 'seq'), scatter_dimension=1, tiled=True)]
    unnamed x4 -> x1, waiting for transfers between devices: 118 us -> 0.02 us
    all_gather x3 -> x2, blocking collectives: 81.2 us -> 40.3 us  [the longest x1 29.7 us: body(): all_packed = lax.all_gather(packed, 'tp', axis=0, tiled=True)]
    unnamed x28 -> x13, local copies, waits for them, and re-layouts: 21.9 us -> 1.8 us
    pmax x1 -> x0, blocking collectives: 14.1 us -> none  [body(): overall = lax.pmax(local_max, 'seq')]
    psum x1 -> x0, blocking collectives: 11.4 us -> none  [body(): lax.psum((gathered_values * factors[..., None]).astype(jnp.bfloat16), 'seq')]
  transfers between devices with their start and end apart: 2 -> 1, of which waited for: 2 -> 1; matrix products, arithmetic and copies ran while one was open for 0% -> 0% of each run, Pallas kernels for 0% -> 0%
where the time goes in v1:
time: 722 us; the launch traced here: 714 us
  waiting for transfers between devices  629 us (87%)
  blocking collectives  40.3 us (6%)
  matrix products  17.6 us (2%)
  between operations  14.3 us (2%)
  local copies, waits for them, and re-layouts  9.41 us (1%)
    reduce_scatter x1, waiting for transfers between devices, body(): lax.psum_scatter(term, ('tp', 'seq'), scatter_dimension=1, tiled=True)  629 us
    all_gather x1, blocking collectives, body(): all_packed = lax.all_gather(packed, 'tp', axis=0, tiled=True)  29.7 us
  transfers between devices with their start and end apart: 1, of which 1 were waited for; matrix products, arithmetic and copies ran while one was open for 0% of the time, Pallas kernels for 0%

profile of v1, /device:TPU:1, one launch (start us, length us, event | category | flops | bytes accessed | tf_op | source)
XLA Modules:
  0.0 714.3 jit_solution(15507271383634190996)
XLA Ops:
  7.3 0.8 convert_element_type.58
  8.1 0.1 copy.45
  8.2 0.7 broadcast_compare_fusion
  9.0 0.8 bitcast_select_fusion
  9.8 1.0 fusion.62
  10.8 4.9 fusion.61
  15.8 0.3 fusion.10
  16.2 0.3 fusion.47
  16.5 4.2 select_reduce_fusion
  20.8 10.5 %all-gather = f32[12,4,1056]{2,1,0:T(4,128)S(1)} all-gather(f32[3,4,1056]{2,1,0:T(4,128)S(1)} %concatenate.6), channel_id=2, replica_groups=mesh['seq'=4,'tp'=32] {'seq'}, dimensions={0}, use_global_device_ids=true | all-gather | bytes 253440 | tf_op jit(solution)/shard_map/all_gather | solution.py:87
  31.6 0.1 reshape.173
  31.7 0.2 broadcast_in_dim.143
  31.8 0.2 reshape.172
  32.1 0.5 multiply_reduce_fusion
  32.8 29.7 %all_gather.11 = bf16[96,4,1026]{2,1,0:T(4,128)(2,1)S(1)} all-gather(bf16[3,4,1026]{2,1,0:T(4,128)(2,1)S(1)} %pad_maximum_fusion), channel_id=1, replica_groups=mesh['seq'=4,'tp'=32] {'tp'}, dimensions={0}, use_global_device_ids=true | all-gather | bytes 812592 | tf_op jit(solution)/shard_map/all_gather | solution.py:113
  62.6 0.3 slice.24
  62.8 0.1 copy.62
  63.0 0.4 fusion.7
  63.5 0.1 copy.48
  63.7 0.1 fusion.63
  64.0 0.5 convolution_convert_fusion.1
  64.6 1.5 fusion.64
  66.0 2.0 fusion.5
  68.1 2.3 fusion.3
  70.4 1.9 reshape.176
  72.4 1.2 copy.70
  73.6 1.6 reshape_reshape.3
  75.2 1.6 copy.64
  76.8 0.6 dynamic-slice_convert_fusion
  77.5 628.7 %reduce-scatter.2.cloned.1.call-done = bf16[12,256]{1,0:T(8,128)(2,1)} async-done(((bf16[12,32768]{1,0:T(8,128)(2,1)}), bf16[12,256]{1,0:T(8,128)(2,1)}) %reduce-scatter.2.cloned.1.call-update) | async-done | bytes 6160 | tf_op jit(solution)/shard_map/reduce_scatter | solution.py:162
  706.1 0.7 reshape.178
  706.8 0.6 add_convert_fusion
  (46 shorter events, 1.4 us)
Async XLA Ops:
  7.2 25.0 %copy-start = (bf16[1024,1024]{1,0:T(8,128)(2,1)S(1)}, bf16[1024,1024]{1,0:T(8,128)(2,1)}, u32[]{:S(2)}) copy-start(bf16[1024,1024]{1,0:T(8,128)(2,1)} %param.21) | copy-start | bytes 6291460
  7.2 9.0 %copy-start.2 = (bf16[3,4,1024]{2,1,0:T(4,128)(2,1)S(1)}, bf16[3,4,1024]{2,1,0:T(4,128)(2,1)}, u32[]{:S(2)}) copy-start(bf16[3,4,1024]{2,1,0:T(4,128)(2,1)} %param.17) | copy-start | bytes 73732
  7.2 698.9 %reduce-scatter.2.cloned.1.call-start = ((), (), s32[]{:S(2)}) async-start(), calls=%async_computation.1 | async-start | bytes 1056768 | tf_op jit(solution)/shard_map/reduce_scatter | solution.py:162
  15.7 16.5 %copy-start.1 = (bf16[3,4,1024]{2,1,0:T(4,128)(2,1)S(1)}, bf16[3,4,1024]{2,1,0:T(4,128)(2,1)}, u32[]{:S(2)}) copy-start(bf16[3,4,1024]{2,1,0:T(4,128)(2,1)} %param.14) | copy-start | bytes 73732
  16.5 16.1 %copy-start.3 = (f32[1024]{0:T(1024)S(1)}, f32[1024]{0:T(1024)}, u32[]{:S(2)}) copy-start(f32[1024]{0:T(1024)} %param.22) | copy-start | bytes 12292
  16.5 46.5 %copy-start.4 = (bf16[1024,16]{0,1:T(8,128)(2,1)S(1)}, bf16[1024,16]{0,1:T(8,128)(2,1)}, u32[]{:S(2)}) copy-start(bf16[1024,16]{0,1:T(8,128)(2,1)} %param.23) | copy-start | bytes 98308
Sparse Core Ops, SparseCore 0:
  77.0 629.0 reduce-scatter.1

commit v2 on v1

--- a/solution.py
+++ b/solution.py
@@ -1,6 +1,10 @@
+import functools
+
 import jax
 import jax.numpy as jnp
 from jax import lax
+from jax.experimental import pallas as pl
+from jax.experimental.pallas import tpu as pltpu
 from jax.sharding import PartitionSpec as P
 
 HEADS = 16
@@ -8,6 +12,144 @@
 
 masked_score = -1e30
 norm_epsilon = 1e-06
+
+
+def combine_kernel(seq_size, tp_size, slices, experts, part_ref, out_ref, recv, summed, landing,
+                   send1, recv1, send2, recv2):
+    mesh_type = pl.DeviceIdType.MESH
+    s = lax.axis_index("seq")
+    t = lax.axis_index("tp")
+    groups = tp_size // slices
+    g = t // slices
+    j = t % slices
+    chunk = recv.shape[2]
+    halves = slices // seq_size
+    expert = s * groups + g
+
+    def stage1(i):
+        return pltpu.make_async_remote_copy(
+            part_ref.at[:, pl.ds(i * chunk, chunk)],
+            recv.at[j],
+            send1.at[i],
+            recv1.at[j],
+            device_id=(s, g * slices + i),
+            device_id_type=mesh_type,
+        )
+
+    def stage1_local(i):
+        return pltpu.make_async_copy(part_ref.at[:, pl.ds(i * chunk, chunk)], recv.at[i], recv1.at[i])
+
+    for i in range(slices):
+        @pl.when(j == i)
+        def _():
+            stage1_local(i).start()
+
+        @pl.when(j != i)
+        def _():
+            stage1(i).start()
+
+    for i in range(slices):
+        @pl.when(j == i)
+        def _():
+            stage1_local(i).wait()
+
+        @pl.when(j != i)
+        def _():
+            stage1(i).wait_send()
+            pltpu.make_async_remote_copy(
+                part_ref.at[:, pl.ds(0, chunk)],
+                recv.at[i],
+                send1.at[i],
+                recv1.at[i],
+                device_id=(s, g * slices + i),
+                device_id_type=mesh_type,
+            ).wait_recv()
+
+    total = recv[0]
+    for i in range(1, slices):
+        total = total + recv[i]
+    summed[...] = total
+
+    dest_seq = j // halves
+    half = j % halves
+    slot = expert * halves + half
+
+    def stage2(u):
+        return pltpu.make_async_remote_copy(
+            summed,
+            landing.at[expert, half],
+            send2.at[u],
+            recv2.at[slot],
+            device_id=(dest_seq, u),
+            device_id_type=mesh_type,
+        )
+
+    def stage2_local():
+        return pltpu.make_async_copy(summed, landing.at[expert, half], recv2.at[slot])
+
+    for u in range(tp_size):
+        mine = (dest_seq == s) & (t == u)
+
+        @pl.when(mine)
+        def _():
+            stage2_local().start()
+
+        @pl.when(jnp.logical_not(mine))
+        def _():
+            stage2(u).start()
+
+    for u in range(tp_size):
+        mine = (dest_seq == s) & (t == u)
+
+        @pl.when(jnp.logical_not(mine))
+        def _():
+            stage2(u).wait_send()
+
+    for e in range(experts):
+        for h in range(halves):
+            src_seq = e // groups
+            src_t = (e % groups) * slices + s * halves + h
+            mine = (src_seq == s) & (src_t == t)
+            at = e * halves + h
+
+            @pl.when(mine)
+            def _():
+                pltpu.make_async_copy(summed, landing.at[e, h], recv2.at[at]).wait()
+
+            @pl.when(jnp.logical_not(mine))
+            def _():
+                pltpu.make_async_remote_copy(
+                    summed,
+                    landing.at[e, h],
+                    send2.at[0],
+                    recv2.at[at],
+                    device_id=(src_seq, src_t),
+                    device_id_type=mesh_type,
+                ).wait_recv()
+
+    out_ref[...] = landing[...]
+
+
+def combine_rows(part, seq_size, tp_size, slices, experts):
+    rows, width = part.shape
+    chunk = width // slices
+    halves = slices // seq_size
+    return pl.pallas_call(
+        functools.partial(combine_kernel, seq_size, tp_size, slices, experts),
+        out_shape=jax.ShapeDtypeStruct((experts, halves, rows, chunk), jnp.float32),
+        in_specs=[pl.BlockSpec(memory_space=pltpu.VMEM)],
+        out_specs=pl.BlockSpec(memory_space=pltpu.VMEM),
+        scratch_shapes=[
+            pltpu.VMEM((slices, rows, chunk), jnp.float32),
+            pltpu.VMEM((rows, chunk), jnp.float32),
+            pltpu.VMEM((experts, halves, rows, chunk), jnp.float32),
+            pltpu.SemaphoreType.DMA((slices,)),
+            pltpu.SemaphoreType.DMA((slices,)),
+            pltpu.SemaphoreType.DMA((tp_size,)),
+            pltpu.SemaphoreType.DMA((experts * halves,)),
+        ],
+        compiler_params=pltpu.CompilerParams(has_side_effects=True),
+    )(part)
 
 
 def body(
@@ -144,23 +286,28 @@
     upward = lax.dot_general(buffer, up_weight, contract, preferred_element_type=jnp.float32)
     inner = (jax.nn.gelu(gate) * upward).astype(jnp.bfloat16)
     produced = jnp.dot(inner, down_weight, preferred_element_type=jnp.float32)
-    placed = select.astype(jnp.float32) * share_mine[None]
-    term = jnp.einsum(
-        "crt,tcd->rtd",
-        placed,
-        produced.reshape(steps, capacity, width),
-        precision=lax.Precision.HIGHEST,
-    )
-    term = (
-        term.astype(jnp.bfloat16)
-        .reshape(tp_size, req_dev, steps, seq_size, feature_block)
-        .transpose(0, 3, 1, 2, 4)
-        .reshape(tp_size * seq_size, req_dev, steps, feature_block)
-    )
-    term = term.reshape(tp_size * seq_size, req_dev * steps, feature_block).transpose(1, 0, 2)
-    term = term.reshape(req_dev * steps, tp_size * seq_size * feature_block)
-    mixture = lax.psum_scatter(term, ("tp", "seq"), scatter_dimension=1, tiled=True)
-    mixture = mixture.reshape(req_dev, steps, feature_block).astype(jnp.float32)
+    groups = tp_size // slices
+    padded = 8 * ((steps * capacity + 7) // 8)
+    part = jnp.pad(produced, ((0, padded - steps * capacity), (0, 0)))
+    gathered = combine_rows(part, seq_size, tp_size, slices, experts)
+    gathered = gathered.transpose(0, 2, 1, 3).reshape(experts * padded, feature_block)
+    own_ids = expert_ids
+    own_slots = lax.dynamic_slice_in_dim(all_slots, tp_index * req_dev, req_dev, 0)
+    own_share = lax.dynamic_slice_in_dim(share, tp_index * req_dev, req_dev, 0)
+    own_kept = own_slots < capacity
+    row_of = own_ids * padded + jnp.arange(steps, dtype=jnp.int32)[None, :, None] * capacity + own_slots
+    weight = jnp.where(own_kept, own_share, 0.0)
+    pick = jnp.sum(
+        jnp.where(
+            row_of[..., None] == jnp.arange(experts * padded, dtype=jnp.int32),
+            weight[..., None],
+            0.0,
+        ),
+        axis=2,
+    ).reshape(req_dev * steps, experts * padded)
+    mixture = jnp.dot(pick, gathered, precision=lax.Precision.HIGHEST).reshape(
+        req_dev, steps, feature_block
+    )
     own_residual = lax.dynamic_slice_in_dim(residual, seq_index * feature_block, feature_block, 2)
     layer_out = (own_residual + mixture).astype(jnp.bfloat16)
     return (attn_out, layer_out)

time: 722 us -> 132 us (0.18)
  the two profiles are of different devices: /device:TPU:1 before, /device:TPU:121 now
where the time goes in v2:
time: 132 us
  Pallas kernels  66.7 us (51%)
  blocking collectives  35.6 us (27%)
  matrix products  16.4 us (12%)
  local copies, waits for them, and re-layouts  8.68 us (7%)
  other arithmetic  3.46 us (3%)
    pallas_call x1, Pallas kernels, combine_rows(): pl.pallas_call(functools.partial(combine_kernel, seq_size, tp_size, slice...  66.7 us
    all_gather x1, blocking collectives, body(): all_packed = lax.all_gather(packed, 'tp', axis=0, tiled=True)  25.9 us
    all_gather x1, blocking collectives, body(): every = lax.all_gather(stats, 'seq')  9.71 us
    dot_general x1, matrix products, body(): jnp.einsum('rqd,rpd->rqp', q_wide, key_cache, preferred_element_type=jnp....  4.9 us
    dot_general x1, matrix products, body(): jnp.einsum('rqp,rpd->rqd', weights.astype(jnp.bfloat16), value_cache, pre...  4.2 us
    transpose x1, local copies, waits for them, and re-layouts, body(): gathered.transpose(0, 2, 1, 3).reshape(experts * padded, feature_block)  3.08 us

profile of v2, /device:TPU:121, one launch (start us, length us, event | category | flops | bytes accessed | tf_op | source)
XLA Modules:
  0.0 131.8 jit_solution(13444482479471112795)
XLA Ops:
  0.7 0.8 convert_element_type.47
  1.5 0.1 copy.48
  1.7 0.7 broadcast_compare_fusion
  2.4 0.8 bitcast_select_fusion
  3.2 1.0 fusion.56
  4.2 4.9 %fusion.55 = (f32[3,64]{1,0:T(4,128)S(1)}, f32[3,64,1024]{2,1,0:T(8,128)S(1)}) fusion(bf16[3,64,1024]{2,1,0:T(8,128)(2,1)S(1)} %bitcast_select_fusion, bf16[3,1024,1024]{2,1,0:T(8,128)(2,1)} %param.18, pred[3,1024]{1,0:T(4,128)(4,1)S(1)} %broadcast_compare_fusion), kind=kOutput, calls=%fused_computation.100 | convolution fusion | flops 403242816 | bytes 7474944 | tf_op jit(solution)/shard_map/cache_scores/rqd,rpd->rqp/dot_general | solution.py:187
  9.2 0.3 fusion.10
  9.6 0.3 fusion.40
  10.0 4.2 %select_reduce_fusion = f32[3,4,1024]{2,1,0:T(4,128)S(1)} fusion(pred[16,1024]{1,0:T(8,128)(4,1)S(1)} %iota_compare_fusion.2, f32[3,64,1024]{2,1,0:T(8,128)S(1)} %fusion.40, bf16[3,1024,1024]{2,1,0:T(8,128)(2,1)} %param.19, f32[3,64,1024]{2,1,0:T(8,128)S(1)} %get-tuple-element.7, f32[3,64]{1,0:T(4,128)S(1)} %max.11, ...), kind=kOutput, calls=%fused_computation.13 | convolution fusion | flops 403820544 | bytes 7933696 | tf_op jit(solution)/shard_map/cache_values/rqp,rpd->rqd/dot_general | solution.py:205
  14.3 9.7 %all-gather = f32[12,4,1056]{2,1,0:T(4,128)S(1)} all-gather(f32[3,4,1056]{2,1,0:T(4,128)S(1)} %concatenate.6), channel_id=2, replica_groups=mesh['seq'=4,'tp'=32] {'seq'}, dimensions={0}, use_global_device_ids=true | all-gather | bytes 253440 | tf_op jit(solution)/shard_map/all_gather | solution.py:229
  24.2 0.1 reshape.174
  24.3 0.2 broadcast_in_dim.158
  24.5 0.2 reshape.173
  24.8 0.5 multiply_reduce_fusion
  25.3 0.6 dynamic-slice_convert_fusion
  26.0 25.9 %all_gather.11 = bf16[96,4,1026]{2,1,0:T(4,128)(2,1)S(1)} all-gather(bf16[3,4,1026]{2,1,0:T(4,128)(2,1)S(1)} %pad_maximum_fusion), channel_id=1, replica_groups=mesh['seq'=4,'tp'=32] {'tp'}, dimensions={0}, use_global_device_ids=true | all-gather | bytes 812592 | tf_op jit(solution)/shard_map/all_gather | solution.py:255
  51.9 0.3 slice.24
  52.2 0.1 copy.65
  52.4 0.4 fusion.8
  52.8 0.1 copy.55
  53.0 0.2 rev.3
  53.2 0.1 copy.50
  53.3 0.1 fusion.57
  53.9 0.5 convolution_convert_fusion
  54.5 0.1 select_reduce_fusion.1
  54.6 1.5 %fusion.58 = f32[60,352]{1,0:T(8,128)S(1)} fusion(bf16[60,1024]{1,0:T(8,128)(2,1)S(1)} %reshape.175, bf16[352,1024]{1,0:T(8,128)(2,1)} %param.25), kind=kOutput, calls=%fused_computation.103 | convolution fusion | flops 43253760 | bytes 928256 | tf_op jit(solution)/shard_map/dot_general | solution.py:285
  56.1 2.0 %fusion.4 = f32[60,1024]{1,0:T(8,128)S(1)} fusion(bf16[352,1024]{1,0:T(8,128)(2,1)} %param.27, bf16[60,1024]{1,0:T(8,128)(2,1)S(1)} %reshape.175, bf16[352,1024]{1,0:T(8,128)(2,1)} %param.26, f32[60,352]{1,0:T(8,128)S(1)} %fusion.58), kind=kOutput, calls=%fused_computation.8 | convolution fusion | flops 86718720 | bytes 1894912 | tf_op jit(solution)/shard_map/dot_general | solution.py:288
  58.1 0.7 pad.4.part_ref
  58.8 66.7 %shard_map.149 = f32[16,2,64,128]{3,2,1,0:T(8,128)} custom-call(f32[64,1024]{1,0:T(8,128)} %pad.4.part_ref), custom_call_target="tpu_custom_call" | custom-call | tf_op jit(solution)/shard_map/pallas_call | solution.py:137
  125.5 3.1 %copy.62 = f32[16,64,2,128]{3,2,1,0:T(2,128)} copy(f32[16,64,2,128]{3,1,2,0:T(8,128)} %bitcast.33) | data formatting | bytes 2097152 | tf_op jit(solution)/shard_map/transpose | solution.py:293
  128.6 2.1 %reshape.180 = f32[1024,256,1]{1,0,2:T(8,128)S(1)} reshape(f32[16,64,2,128]{3,2,1,0:T(2,128)} %copy.62) | data formatting | bytes 2097152 | tf_op jit(solution)/shard_map/reshape | solution.py:293
  130.6 1.2 fusion.5
  (47 shorter events, 1.4 us)
Async XLA Ops:
  0.6 24.1 %copy-start = (bf16[1024,1024]{1,0:T(8,128)(2,1)S(1)}, bf16[1024,1024]{1,0:T(8,128)(2,1)}, u32[]{:S(2)}) copy-start(bf16[1024,1024]{1,0:T(8,128)(2,1)} %param.21) | copy-start | bytes 6291460
  0.6 9.0 %copy-start.2 = (bf16[3,4,1024]{2,1,0:T(4,128)(2,1)S(1)}, bf16[3,4,1024]{2,1,0:T(4,128)(2,1)}, u32[]{:S(2)}) copy-start(bf16[3,4,1024]{2,1,0:T(4,128)(2,1)} %param.17) | copy-start | bytes 73732
  9.1 15.6 %copy-start.1 = (bf16[3,4,1024]{2,1,0:T(4,128)(2,1)S(1)}, bf16[3,4,1024]{2,1,0:T(4,128)(2,1)}, u32[]{:S(2)}) copy-start(bf16[3,4,1024]{2,1,0:T(4,128)(2,1)} %param.14) | copy-start | bytes 73732
  10.0 15.9 %copy-start.4 = (f32[1024]{0:T(1024)S(1)}, f32[1024]{0:T(1024)}, u32[]{:S(2)}) copy-start(f32[1024]{0:T(1024)} %param.22) | copy-start | bytes 12292
  10.0 42.4 %copy-start.5 = (bf16[1024,16]{0,1:T(8,128)(2,1)S(1)}, bf16[1024,16]{0,1:T(8,128)(2,1)}, u32[]{:S(2)}) copy-start(bf16[1024,16]{0,1:T(8,128)(2,1)} %param.23) | copy-start | bytes 98308
  14.2 39.7 %copy-start.3 = (s32[3,4,2]{1,2,0:T(2,128)S(1)}, s32[3,4,2]{1,2,0:T(2,128)}, u32[]{:S(2)}) copy-start(s32[3,4,2]{1,2,0:T(2,128)} %param.24) | copy-start | bytes 292

commit v3 on v2

--- a/solution.py
+++ b/solution.py
@@ -14,17 +14,15 @@
 norm_epsilon = 1e-06
 
 
-def combine_kernel(seq_size, tp_size, slices, experts, part_ref, out_ref, recv, summed, landing,
-                   send1, recv1, send2, recv2):
+def combine_kernel(seq_size, tp_size, slices, part_ref, out_ref, recv, summed, middle, landing,
+                   send1, recv1, send2, recv2, send3, recv3):
     mesh_type = pl.DeviceIdType.MESH
     s = lax.axis_index("seq")
     t = lax.axis_index("tp")
-    groups = tp_size // slices
     g = t // slices
     j = t % slices
     chunk = recv.shape[2]
     halves = slices // seq_size
-    expert = s * groups + g
 
     def stage1(i):
         return pltpu.make_async_remote_copy(
@@ -68,85 +66,88 @@
     total = recv[0]
     for i in range(1, slices):
         total = total + recv[i]
-    summed[...] = total
+    summed[...] = total.astype(summed.dtype)
 
     dest_seq = j // halves
     half = j % halves
-    slot = expert * halves + half
-
-    def stage2(u):
+    dest_t = g * slices + s * halves + half
+    to_self = dest_seq == s
+
+    @pl.when(to_self)
+    def _():
+        pltpu.make_async_copy(summed, middle, recv2.at[0]).start()
+        pltpu.make_async_copy(summed, middle, recv2.at[0]).wait()
+
+    @pl.when(jnp.logical_not(to_self))
+    def _():
+        copy = pltpu.make_async_remote_copy(
+            summed, middle, send2.at[0], recv2.at[0],
+            device_id=(dest_seq, dest_t), device_id_type=mesh_type,
+        )
+        copy.start()
+        copy.wait_send()
+
+    src_seq = (t % slices) // halves
+    src_t = g * slices + s * halves + t % halves
+    from_self = src_seq == s
+
+    @pl.when(jnp.logical_not(from_self))
+    def _():
+        pltpu.make_async_remote_copy(
+            summed, middle, send2.at[0], recv2.at[0],
+            device_id=(src_seq, src_t), device_id_type=mesh_type,
+        ).wait_recv()
+
+    def stage3(u):
         return pltpu.make_async_remote_copy(
-            summed,
-            landing.at[expert, half],
-            send2.at[u],
-            recv2.at[slot],
-            device_id=(dest_seq, u),
-            device_id_type=mesh_type,
-        )
-
-    def stage2_local():
-        return pltpu.make_async_copy(summed, landing.at[expert, half], recv2.at[slot])
+            middle, landing.at[t], send3.at[u], recv3.at[t],
+            device_id=(s, u), device_id_type=mesh_type,
+        )
 
     for u in range(tp_size):
-        mine = (dest_seq == s) & (t == u)
-
-        @pl.when(mine)
-        def _():
-            stage2_local().start()
-
-        @pl.when(jnp.logical_not(mine))
-        def _():
-            stage2(u).start()
+        @pl.when(t == u)
+        def _():
+            pltpu.make_async_copy(middle, landing.at[u], recv3.at[u]).start()
+
+        @pl.when(t != u)
+        def _():
+            stage3(u).start()
 
     for u in range(tp_size):
-        mine = (dest_seq == s) & (t == u)
-
-        @pl.when(jnp.logical_not(mine))
-        def _():
-            stage2(u).wait_send()
-
-    for e in range(experts):
-        for h in range(halves):
-            src_seq = e // groups
-            src_t = (e % groups) * slices + s * halves + h
-            mine = (src_seq == s) & (src_t == t)
-            at = e * halves + h
-
-            @pl.when(mine)
-            def _():
-                pltpu.make_async_copy(summed, landing.at[e, h], recv2.at[at]).wait()
-
-            @pl.when(jnp.logical_not(mine))
-            def _():
-                pltpu.make_async_remote_copy(
-                    summed,
-                    landing.at[e, h],
-                    send2.at[0],
-                    recv2.at[at],
-                    device_id=(src_seq, src_t),
-                    device_id_type=mesh_type,
-                ).wait_recv()
+        @pl.when(t == u)
+        def _():
+            pltpu.make_async_copy(middle, landing.at[u], recv3.at[u]).wait()
+
+        @pl.when(t != u)
+        def _():
+            stage3(u).wait_send()
+            pltpu.make_async_remote_copy(
+                middle, landing.at[u], send3.at[u], recv3.at[u],
+                device_id=(s, u), device_id_type=mesh_type,
+            ).wait_recv()
 
     out_ref[...] = landing[...]
 
 
-def combine_rows(part, seq_size, tp_size, slices, experts):
+def combine_rows(part, seq_size, tp_size, slices):
     rows, width = part.shape
     chunk = width // slices
-    halves = slices // seq_size
     return pl.pallas_call(
-        functools.partial(combine_kernel, seq_size, tp_size, slices, experts),
-        out_shape=jax.ShapeDtypeStruct((experts, halves, rows, chunk), jnp.float32),
+        functools.partial(combine_kernel, seq_size, tp_size, slices),
+        out_shape=jax.ShapeDtypeStruct((tp_size, rows, chunk), jnp.bfloat16),
         in_specs=[pl.BlockSpec(memory_space=pltpu.VMEM)],
         out_specs=pl.BlockSpec(memory_space=pltpu.VMEM),
         scratch_shapes=[
             pltpu.VMEM((slices, rows, chunk), jnp.float32),
-            pltpu.VMEM((rows, chunk), jnp.float32),
-            pltpu.VMEM((experts, halves, rows, chunk), jnp.float32),
+            pltpu.VMEM((rows, chunk), jnp.bfloat16),
+            pltpu.VMEM((rows, chunk), jnp.bfloat16),
+            pltpu.VMEM((tp_size, rows, chunk), jnp.bfloat16),
             pltpu.SemaphoreType.DMA((slices,)),
             pltpu.SemaphoreType.DMA((slices,)),
+            pltpu.SemaphoreType.DMA((1,)),
+            pltpu.SemaphoreType.DMA((1,)),
             pltpu.SemaphoreType.DMA((tp_size,)),
-            pltpu.SemaphoreType.DMA((experts * halves,)),
+            pltpu.SemaphoreType.DMA((tp_size,)),
         ],
         compiler_params=pltpu.CompilerParams(has_side_effects=True),
     )(part)
@@ -289,25 +290,22 @@
     groups = tp_size // slices
     padded = 8 * ((steps * capacity + 7) // 8)
     part = jnp.pad(produced, ((0, padded - steps * capacity), (0, 0)))
-    gathered = combine_rows(part, seq_size, tp_size, slices, experts)
-    gathered = gathered.transpose(0, 2, 1, 3).reshape(experts * padded, feature_block)
-    own_ids = expert_ids
+    gathered = combine_rows(part, seq_size, tp_size, slices)
+    halves = slices // seq_size
+    gathered = gathered.astype(jnp.float32).reshape(groups, tp_size // (groups * halves), halves, padded, width // slices)
     own_slots = lax.dynamic_slice_in_dim(all_slots, tp_index * req_dev, req_dev, 0)
     own_share = lax.dynamic_slice_in_dim(share, tp_index * req_dev, req_dev, 0)
-    own_kept = own_slots < capacity
-    row_of = own_ids * padded + jnp.arange(steps, dtype=jnp.int32)[None, :, None] * capacity + own_slots
-    weight = jnp.where(own_kept, own_share, 0.0)
-    pick = jnp.sum(
-        jnp.where(
-            row_of[..., None] == jnp.arange(experts * padded, dtype=jnp.int32),
-            weight[..., None],
-            0.0,
-        ),
-        axis=2,
-    ).reshape(req_dev * steps, experts * padded)
-    mixture = jnp.dot(pick, gathered, precision=lax.Precision.HIGHEST).reshape(
-        req_dev, steps, feature_block
-    )
+    weight = jnp.where(own_slots < capacity, own_share, 0.0)
+    row_of = jnp.arange(steps, dtype=jnp.int32)[None, :, None] * capacity + own_slots
+    hit = (
+        (expert_ids[..., None, None, None] % groups == jnp.arange(groups)[:, None, None])
+        & (expert_ids[..., None, None, None] // groups == jnp.arange(tp_size // (groups * halves))[None, :, None])
+        & (row_of[..., None, None, None] == jnp.arange(padded)[None, None, :])
+    )
+    pick = jnp.sum(jnp.where(hit, weight[..., None, None, None], 0.0), axis=2)
+    mixture = jnp.einsum(
+        "rtzyp,zyhpf->rthf", pick, gathered, precision=lax.Precision.HIGHEST
+    ).reshape(req_dev, steps, feature_block)
     own_residual = lax.dynamic_slice_in_dim(residual, seq_index * feature_block, feature_block, 2)
     layer_out = (own_residual + mixture).astype(jnp.bfloat16)
     return (attn_out, layer_out)

time: 132 us -> 95.4 us (0.72)
  the two profiles are of different devices: /device:TPU:121 before, /device:TPU:1 now
where the time goes in v3:
time: 95.4 us; the launch traced here: 94.9 us
  blocking collectives  40.3 us (42%)
  Pallas kernels  27.6 us (29%)
  matrix products  16.3 us (17%)
  local copies, waits for them, and re-layouts  5.85 us (6%)
  other arithmetic  3.93 us (4%)
  between operations  0.97 us (1%)
    all_gather x1, blocking collectives, body(): all_packed = lax.all_gather(packed, 'tp', axis=0, tiled=True)  29.7 us
    pallas_call x1, Pallas kernels, combine_rows(): pl.pallas_call(functools.partial(combine_kernel, seq_size, tp_size, slice...  27.6 us
    all_gather x1, blocking collectives, body(): every = lax.all_gather(stats, 'seq')  10.5 us
    dot_general x1, matrix products, body(): jnp.einsum('rqd,rpd->rqp', q_wide, key_cache, preferred_element_type=jnp....  4.9 us
    dot_general x1, matrix products, body(): jnp.einsum('rqp,rpd->rqd', weights.astype(jnp.bfloat16), value_cache, pre...  4.19 us
    dot_general x1, matrix products, body(): produced = jnp.dot(inner, down_weight, preferred_element_type=jnp.float32)  2.02 us
    dot_general x2, local copies, waits for them, and re-layouts, body(): jnp.einsum('rtzyp,zyhpf->rthf', pick, gathered, precision=lax.Precision.H...  1.92 us

profile of v3, /device:TPU:1, one launch (start us, length us, event | category | flops | bytes accessed | tf_op | source)
XLA Modules:
  0.0 94.9 jit_solution(1411664602153632275)
XLA Ops:
  0.7 0.9 broadcast_compare_fusion
  1.6 0.8 and_select_fusion.1
  2.4 0.1 copy.54
  2.5 0.1 copy.56
  3.0 0.8 bitcast_select_fusion
  3.7 1.0 %fusion.58 = (f32[3,64]{1,0:T(4,128)S(1)}, f32[3,64,4]{1,2,0:T(4,128)S(1)}) fusion(bf16[3,64,1024]{2,1,0:T(8,128)(2,1)S(1)} %bitcast_select_fusion, bf16[3,4,1024]{2,1,0:T(4,128)(2,1)} %param.16, pred[64,4]{0,1:T(4,128)(4,1)S(1)} %fusion.49), kind=kOutput, calls=%fused_computation.113 | convolution fusion | flops 1574976 | bytes 421888 | tf_op jit(solution)/shard_map/rqd,rsd->rqs/dot_general | solution.py:195
  4.7 4.9 %fusion.57 = (f32[3,64]{1,0:T(4,128)S(1)}, f32[3,64,1024]{2,1,0:T(8,128)S(1)}) fusion(bf16[3,64,1024]{2,1,0:T(8,128)(2,1)S(1)} %bitcast_select_fusion, bf16[3,1024,1024]{2,1,0:T(8,128)(2,1)} %param.18, pred[3,1024]{1,0:T(4,128)(4,1)S(1)} %broadcast_compare_fusion), kind=kOutput, calls=%fused_computation.112 | convolution fusion | flops 403242816 | bytes 7474944 | tf_op jit(solution)/shard_map/cache_scores/rqd,rpd->rqp/dot_general | solution.py:188
  9.7 0.3 fusion.11
  10.1 0.3 fusion.42
  10.5 4.2 %select_reduce_fusion = f32[3,4,1024]{2,1,0:T(4,128)S(1)} fusion(pred[16,1024]{1,0:T(8,128)(4,1)S(1)} %iota_compare_fusion.1, f32[3,64,1024]{2,1,0:T(8,128)S(1)} %fusion.42, bf16[3,1024,1024]{2,1,0:T(8,128)(2,1)} %param.19, f32[3,64,1024]{2,1,0:T(8,128)S(1)} %get-tuple-element.10, f32[3,64]{1,0:T(4,128)S(1)} %max.11, ...), kind=kOutput, calls=%fused_computation.14 | convolution fusion | flops 403820544 | bytes 7933696 | tf_op jit(solution)/shard_map/cache_values/rqp,rpd->rqd/dot_general | solution.py:206
  14.8 10.5 %all-gather = f32[12,4,1056]{2,1,0:T(4,128)S(1)} all-gather(f32[3,4,1056]{2,1,0:T(4,128)S(1)} %concatenate.6), channel_id=2, replica_groups=mesh['seq'=4,'tp'=32] {'seq'}, dimensions={0}, use_global_device_ids=true | all-gather | bytes 253440 | tf_op jit(solution)/shard_map/all_gather | solution.py:230
  25.6 0.2 broadcast_in_dim.159
  25.8 0.2 reshape.224
  26.1 0.5 multiply_reduce_fusion
  26.6 0.6 dynamic-slice_convert_fusion
  27.3 29.7 %all_gather.11 = bf16[96,4,1026]{2,1,0:T(4,128)(2,1)S(1)} all-gather(bf16[3,4,1026]{2,1,0:T(4,128)(2,1)S(1)} %pad_maximum_fusion), channel_id=1, replica_groups=mesh['seq'=4,'tp'=32] {'tp'}, dimensions={0}, use_global_device_ids=true | all-gather | bytes 812592 | tf_op jit(solution)/shard_map/all_gather | solution.py:256
  57.1 0.3 slice.24
  57.4 0.1 copy.77
  57.6 0.4 fusion.9
  58.0 0.1 copy.64
  58.1 0.2 rev.3
  58.4 0.1 copy.58
  59.1 0.5 convolution_convert_fusion
  59.6 0.1 copy.62
  59.9 0.2 select_reduce_fusion.1
  60.2 1.5 %fusion.60 = f32[60,352]{1,0:T(8,128)S(1)} fusion(bf16[60,1024]{1,0:T(8,128)(2,1)S(1)} %reshape.226, bf16[352,1024]{1,0:T(8,128)(2,1)} %param.25), kind=kOutput, calls=%fused_computation.115 | convolution fusion | flops 43253760 | bytes 928256 | tf_op jit(solution)/shard_map/dot_general | solution.py:286
  61.6 2.0 %fusion.4 = f32[60,1024]{1,0:T(8,128)S(1)} fusion(bf16[352,1024]{1,0:T(8,128)(2,1)} %param.27, bf16[60,1024]{1,0:T(8,128)(2,1)S(1)} %reshape.226, bf16[352,1024]{1,0:T(8,128)(2,1)} %param.26, f32[60,352]{1,0:T(8,128)S(1)} %fusion.60), kind=kOutput, calls=%fused_computation.8 | convolution fusion | flops 86718720 | bytes 1894912 | tf_op jit(solution)/shard_map/dot_general | solution.py:289
  63.6 0.7 pad.4.part_ref
  64.4 27.6 %shard_map.149 = bf16[32,64,128]{2,1,0:T(8,128)(2,1)} custom-call(f32[64,1024]{1,0:T(8,128)} %pad.4.part_ref), custom_call_target="tpu_custom_call" | custom-call | tf_op jit(solution)/shard_map/pallas_call | solution.py:135
  92.0 1.6 %copy.72 = bf16[2,128,64,4,4]{1,0,2,4,3:T(2,128)(2,1)S(1)} copy(bf16[2,128,64,4,4]{1,2,0,3,4:T(8,128)(2,1)} %bitcast.44) | data formatting | bytes 1048576 | tf_op jit(solution)/shard_map/rtzyp,zyhpf->rthf/dot_general | solution.py:306
  93.6 0.3 reshape.231
  93.9 1.0 %fusion.6 = bf16[3,4,256]{2,1,0:T(4,128)(2,1)} fusion(bf16[256,64,4,4,1]{0,1,3,2,4:T(8,128)(2,1)S(1)} %reshape.231, f32[3,4,4,4,64]{4,3,2,1,0:T(4,128)S(1)} %select_reduce_fusion.1, f32[3,4,1024]{2,1,0:T(4,128)S(1)} %get-tuple-element.3, s32[]{:T(128)S(6)} %select_n.98), kind=kOutput, calls=%fused_computation.11 | convolution fusion | flops 37754880 | bytes 591876 | tf_op jit(solution)/shard_map/rtzyp,zyhpf->rthf/dot_general | solution.py:306
  (52 shorter events, 2.0 us)
Async XLA Ops:
  0.6 25.4 %copy-start = (bf16[1024,1024]{1,0:T(8,128)(2,1)S(1)}, bf16[1024,1024]{1,0:T(8,128)(2,1)}, u32[]{:S(2)}) copy-start(bf16[1024,1024]{1,0:T(8,128)(2,1)} %param.21) | copy-start | bytes 6291460
  0.6 9.5 %copy-start.2 = (bf16[3,4,1024]{2,1,0:T(4,128)(2,1)S(1)}, bf16[3,4,1024]{2,1,0:T(4,128)(2,1)}, u32[]{:S(2)}) copy-start(bf16[3,4,1024]{2,1,0:T(4,128)(2,1)} %param.17) | copy-start | bytes 73732
  9.6 16.5 %copy-start.1 = (bf16[3,4,1024]{2,1,0:T(4,128)(2,1)S(1)}, bf16[3,4,1024]{2,1,0:T(4,128)(2,1)}, u32[]{:S(2)}) copy-start(bf16[3,4,1024]{2,1,0:T(4,128)(2,1)} %param.14) | copy-start | bytes 73732
  10.5 16.7 %copy-start.3 = (f32[1024]{0:T(1024)S(1)}, f32[1024]{0:T(1024)}, u32[]{:S(2)}) copy-start(f32[1024]{0:T(1024)} %param.22) | copy-start | bytes 12292
  10.5 47.1 %copy-start.4 = (bf16[1024,16]{0,1:T(8,128)(2,1)S(1)}, bf16[1024,16]{0,1:T(8,128)(2,1)}, u32[]{:S(2)}) copy-start(bf16[1024,16]{0,1:T(8,128)(2,1)} %param.23) | copy-start | bytes 98308

commit v4 on v3

--- a/solution.py
+++ b/solution.py
@@ -127,6 +127,57 @@
             ).wait_recv()
 
     out_ref[...] = landing[...]
+
+
+def gather_kernel(axis, size, piece_ref, out_ref, landing, send, recv):
+    mesh_type = pl.DeviceIdType.MESH
+    me = lax.axis_index(axis)
+    other = lax.axis_index("tp" if axis == "seq" else "seq")
+
+    def peer(u):
+        return (u, other) if axis == "seq" else (other, u)
+
+    def remote(u, slot):
+        return pltpu.make_async_remote_copy(
+            piece_ref, landing.at[slot], send.at[u], recv.at[slot],
+            device_id=peer(u), device_id_type=mesh_type,
+        )
+
+    for u in range(size):
+        @pl.when(me == u)
+        def _():
+            pltpu.make_async_copy(piece_ref, landing.at[u], recv.at[u]).start()
+
+        @pl.when(me != u)
+        def _():
+            remote(u, me).start()
+
+    for u in range(size):
+        @pl.when(me == u)
+        def _():
+            pltpu.make_async_copy(piece_ref, landing.at[u], recv.at[u]).wait()
+
+        @pl.when(me != u)
+        def _():
+            remote(u, me).wait_send()
+            remote(u, u).wait_recv()
+
+    out_ref[...] = landing[...]
+
+
+def gather_axis(piece, axis, size):
+    return pl.pallas_call(
+        functools.partial(gather_kernel, axis, size),
+        out_shape=jax.ShapeDtypeStruct((size,) + piece.shape, piece.dtype),
+        in_specs=[pl.BlockSpec(memory_space=pltpu.VMEM)],
+        out_specs=pl.BlockSpec(memory_space=pltpu.VMEM),
+        scratch_shapes=[
+            pltpu.VMEM((size,) + piece.shape, piece.dtype),
+            pltpu.SemaphoreType.DMA((size,)),
+            pltpu.SemaphoreType.DMA((size,)),
+        ],
+        compiler_params=pltpu.CompilerParams(has_side_effects=True),
+    )(piece)
 
 
 def combine_rows(part, seq_size, tp_size, slices):
@@ -227,7 +278,9 @@
         ],
         axis=2,
     )
-    every = lax.all_gather(stats, "seq")
+    every = gather_axis(stats.reshape(req_dev * steps, -1), "seq", seq_size).reshape(
+        (seq_size,) + stats.shape
+    )
     block_sums = every[..., :width]
     block_max = every[..., width : width + HEADS]
     block_totals = every[..., width + HEADS :]
@@ -253,7 +306,9 @@
     capacity = (5 * requests * topk + 4 * experts - 1) // (4 * experts)
     expert_range = jnp.arange(experts, dtype=jnp.int32)
     packed = jnp.concatenate([normed, expert_ids.astype(jnp.bfloat16)], axis=2)
-    all_packed = lax.all_gather(packed, "tp", axis=0, tiled=True)
+    all_packed = gather_axis(packed.reshape(req_dev * steps, -1), "tp", tp_size).reshape(
+        requests, steps, -1
+    )
     all_normed = all_packed[:, :, :width]
     all_ids = all_packed[:, :, width:].astype(jnp.int32)
     onehot = all_ids[..., None] == expert_range

time: 95.4 us -> 112 us (1.17)
  Pallas kernels: 27.6 us -> 79 us
  blocking collectives: 40.3 us -> 0 us
  local copies, waits for them, and re-layouts: 5.85 us -> 12.7 us
  matrix products: 16.3 us -> 14.9 us
    pallas_call x0 -> x2, Pallas kernels: none -> 46 us  [gather_axis(): pl.pallas_call(functools.partial(gather_kernel, axis, size), out_shape=ja...]
    all_gather x2 -> x0, blocking collectives: 40.3 us -> none  [the longest x1 29.7 us: body(): all_packed = lax.all_gather(packed, 'tp', axis=0, tiled=True)]
    pallas_call x1, Pallas kernels: 27.6 us -> 33 us  [combine_rows(): pl.pallas_call(functools.partial(combine_kernel, seq_size, tp_size, slice...]
    dot_general x1, matrix products: 4.19 us -> 1.47 us  [body(): jnp.einsum('rqp,rpd->rqd', weights.astype(jnp.bfloat16), value_cache, pre...]
    reshape x0 -> x2, local copies, waits for them, and re-layouts: none -> 2.46 us  [the longest x1 1.83 us: body(): gather_axis(packed.reshape(req_dev * steps, -1), 'tp', tp_size)]
    dot_general x2, local copies, waits for them, and re-layouts: 1.92 us -> 3.79 us  [body(): jnp.einsum('rtzyp,zyhpf->rthf', pick, gathered, precision=lax.Precision.H...]
    dot_general x1, matrix products: 0.53 us -> 1.67 us  [body(): jnp.einsum('crt,rtd->tcd', select.astype(jnp.bfloat16), all_normed, prefe...]
where the time goes in v4:
time: 112 us; the launch traced here: 111 us
  Pallas kernels  79 us (71%)
  matrix products  14.9 us (13%)
  local copies, waits for them, and re-layouts  12.7 us (11%)
  other arithmetic  3.41 us (3%)
    pallas_call x2, Pallas kernels, gather_axis(): pl.pallas_call(functools.partial(gather_kernel, axis, size), out_shape=ja...  46 us
    pallas_call x1, Pallas kernels, combine_rows(): pl.pallas_call(functools.partial(combine_kernel, seq_size, tp_size, slice...  33 us
    dot_general x1, matrix products, body(): jnp.einsum('rqd,rpd->rqp', q_wide, key_cache, preferred_element_type=jnp....  5.06 us
    dot_general x2, local copies, waits for them, and re-layouts, body(): jnp.einsum('rtzyp,zyhpf->rthf', pick, gathered, precision=lax.Precision.H...  3.79 us

profile of v4, /device:TPU:1, one launch (start us, length us, event | category | flops | bytes accessed | tf_op | source)
XLA Modules:
  0.0 111.1 jit_solution(12211033331119984059)
XLA Ops:
  0.7 0.9 bitcast_select_fusion
  1.7 1.0 fusion.63
  2.7 0.9 broadcast_compare_fusion
  3.6 5.1 %fusion.62 = (f32[3,64]{1,0:T(4,128)S(1)}, f32[3,64,1024]{2,1,0:T(8,128)S(1)}) fusion(bf16[3,64,1024]{2,1,0:T(8,128)(2,1)S(1)} %bitcast_select_fusion, bf16[3,1024,1024]{2,1,0:T(8,128)(2,1)} %param.18, pred[3,1024]{1,0:T(4,128)(4,1)S(1)} %broadcast_compare_fusion), kind=kOutput, calls=%fused_computation.116 | convolution fusion | flops 403242816 | bytes 7474944 | tf_op jit(solution)/shard_map/cache_scores/rqd,rpd->rqp/dot_general | solution.py:239
  8.6 0.3 fusion.43
  9.0 1.5 %select_reduce_fusion = f32[3,4,1024]{2,1,0:T(4,128)S(1)} fusion(pred[16,1024]{1,0:T(8,128)(4,1)S(1)} %iota_compare_fusion.1, f32[3,64,1024]{2,1,0:T(8,128)S(1)} %fusion.43, bf16[3,1024,1024]{2,1,0:T(8,128)(2,1)S(1)} %copy-done.1, f32[3,64,1024]{2,1,0:T(8,128)S(1)} %get-tuple-element.10, f32[3,64]{1,0:T(4,128)S(1)} %max.12, ...), kind=kOutput, calls=%fused_computation.14 | convolution fusion | flops 403820544 | bytes 7933696 | tf_op jit(solution)/shard_map/cache_values/rqp,rpd->rqd/dot_general | solution.py:257
  10.6 0.3 fusion.11
  11.0 0.7 concatenate.10.piece_ref
  11.7 19.0 %shard_map.149 = f32[4,12,1056]{2,1,0:T(8,128)} custom-call(f32[12,1056]{1,0:T(8,128)} %concatenate.10.piece_ref), custom_call_target="tpu_custom_call" | custom-call | tf_op jit(solution)/shard_map/pallas_call | solution.py:169
  30.7 1.0 copy.55
  31.8 0.2 broadcast_in_dim.159
  32.0 0.2 reshape.242
  32.2 0.2 fusion.17
  32.6 0.5 multiply_reduce_fusion
  33.1 0.6 dynamic-slice_convert_fusion
  33.9 0.6 reshape.244.piece_ref
  34.6 27.0 %shard_map.150 = bf16[32,12,1026]{2,1,0:T(8,128)(2,1)} custom-call(bf16[12,1026]{1,0:T(8,128)(2,1)} %reshape.244.piece_ref), custom_call_target="tpu_custom_call" | custom-call | tf_op jit(solution)/shard_map/pallas_call | solution.py:169
  61.6 1.8 %reshape.245 = bf16[96,4,1026]{2,1,0:T(4,128)(2,1)S(1)} reshape(bf16[32,12,1026]{2,1,0:T(8,128)(2,1)} %shard_map.150) | data formatting | bytes 1575936 | tf_op jit(solution)/shard_map/reshape | solution.py:309
  63.5 1.1 %slice.24 = bf16[96,4,1024]{2,1,0:T(4,128)(2,1)} slice(bf16[96,4,1026]{2,1,0:T(4,128)(2,1)S(1)} %reshape.245), slice={[0:96], [0:4], [0:1024]} | slice | bytes 1572864 | tf_op jit(solution)/shard_map/slice | solution.py:312
  64.8 0.1 copy.60
  65.3 1.7 %convolution_convert_fusion = bf16[4,15,1024]{2,1,0:T(8,128)(2,1)S(1)} fusion(bf16[96,4,1024]{2,1,0:T(4,128)(2,1)} %slice.24, s32[96,4]{0,1:T(4,128)S(1)} %select_reduce_fusion.4, pred[96,4]{0,1:T(4,128)(4,1)S(1)} %compare_and_fusion), kind=kOutput, calls=%fused_computation.5 | convolution fusion | flops 11869440 | bytes 911232 | tf_op jit(solution)/shard_map/crt,rtd->tcd/dot_general | solution.py:331
  67.0 1.5 %fusion.65 = f32[60,352]{1,0:T(8,128)S(1)} fusion(bf16[60,1024]{1,0:T(8,128)(2,1)S(1)} %reshape.246, bf16[352,1024]{1,0:T(8,128)(2,1)} %param.25), kind=kOutput, calls=%fused_computation.119 | convolution fusion | flops 43253760 | bytes 928256 | tf_op jit(solution)/shard_map/dot_general | solution.py:341
  68.5 2.0 %fusion.4 = f32[60,1024]{1,0:T(8,128)S(1)} fusion(bf16[352,1024]{1,0:T(8,128)(2,1)} %param.27, bf16[60,1024]{1,0:T(8,128)(2,1)S(1)} %reshape.246, bf16[352,1024]{1,0:T(8,128)(2,1)} %param.26, f32[60,352]{1,0:T(8,128)S(1)} %fusion.65), kind=kOutput, calls=%fused_computation.8 | convolution fusion | flops 86718720 | bytes 1894912 | tf_op jit(solution)/shard_map/dot_general | solution.py:344
  70.5 0.7 pad.4.part_ref
  71.3 33.0 %shard_map.151 = bf16[32,64,128]{2,1,0:T(8,128)(2,1)} custom-call(f32[64,1024]{1,0:T(8,128)} %pad.4.part_ref), custom_call_target="tpu_custom_call" | custom-call | tf_op jit(solution)/shard_map/pallas_call | solution.py:186
  104.3 2.4 %copy.74 = bf16[2,128,64,4,4]{1,0,2,4,3:T(2,128)(2,1)} copy(bf16[2,128,64,4,4]{1,2,0,3,4:T(8,128)(2,1)} %bitcast.46) | data formatting | bytes 1048576 | tf_op jit(solution)/shard_map/rtzyp,zyhpf->rthf/dot_general | solution.py:361
  106.7 1.4 %reshape.250 = bf16[256,64,4,4,1]{0,1,3,2,4:T(8,128)(2,1)S(1)} reshape(bf16[2,128,64,4,4]{1,0,2,4,3:T(2,128)(2,1)} %copy.74) | data formatting | bytes 1048576 | tf_op jit(solution)/shard_map/rtzyp,zyhpf->rthf/dot_general | solution.py:361
  108.3 0.4 fusion.9
  108.7 0.1 copy.66
  108.8 0.2 rev.3
  109.8 0.2 select_reduce_fusion.1
  110.1 1.0 fusion.6
  (61 shorter events, 2.3 us)
Async XLA Ops:
  0.6 31.9 %copy-start = (bf16[1024,1024]{1,0:T(8,128)(2,1)S(1)}, bf16[1024,1024]{1,0:T(8,128)(2,1)}, u32[]{:S(2)}) copy-start(bf16[1024,1024]{1,0:T(8,128)(2,1)} %param.21) | copy-start | bytes 6291460
  0.6 8.0 %copy-start.4 = (bf16[3,4,1024]{2,1,0:T(4,128)(2,1)S(1)}, bf16[3,4,1024]{2,1,0:T(4,128)(2,1)}, u32[]{:S(2)}) copy-start(bf16[3,4,1024]{2,1,0:T(4,128)(2,1)} %param.17) | copy-start | bytes 73732
  2.7 6.3 %copy-start.1 = (bf16[3,1024,1024]{2,1,0:T(8,128)(2,1)S(1)}, bf16[3,1024,1024]{2,1,0:T(8,128)(2,1)}, u32[]{:S(2)}) copy-start(bf16[3,1024,1024]{2,1,0:T(8,128)(2,1)} %param.19) | copy-start | bytes 18874372
  8.6 23.9 %copy-start.3 = (bf16[3,4,1024]{2,1,0:T(4,128)(2,1)S(1)}, bf16[3,4,1024]{2,1,0:T(4,128)(2,1)}, u32[]{:S(2)}) copy-start(bf16[3,4,1024]{2,1,0:T(4,128)(2,1)} %param.14) | copy-start | bytes 73732
  9.0 24.7 %copy-start.6 = (s32[3,4,2]{1,2,0:T(2,128)S(1)}, s32[3,4,2]{1,2,0:T(2,128)}, u32[]{:S(2)}) copy-start(s32[3,4,2]{1,2,0:T(2,128)} %param.24) | copy-start | bytes 292
  9.0 24.8 %copy-start.5 = (f32[1024]{0:T(1024)S(1)}, f32[1024]{0:T(1024)}, u32[]{:S(2)}) copy-start(f32[1024]{0:T(1024)} %param.22) | copy-start | bytes 12292
  61.6 46.7 %copy-start.7 = (bf16[1024,16]{0,1:T(8,128)(2,1)S(1)}, bf16[1024,16]{0,1:T(8,128)(2,1)}, u32[]{:S(2)}) copy-start(bf16[1024,16]{0,1:T(8,128)(2,1)} %param.23) | copy-start | bytes 98308
  64.6 43.6 %copy-start.2 = (bf16[96,4,1024]{2,1,0:T(4,128)(2,1)S(1)}, bf16[96,4,1024]{2,1,0:T(4,128)(2,1)}, u32[]{:S(2)}) copy-start(bf16[96,4,1024]{2,1,0:T(4,128)(2,1)} %slice.24) | copy-start | bytes 2359300

commit v5 on v4

--- a/solution.py
+++ b/solution.py
@@ -23,6 +23,27 @@
     j = t % slices
     chunk = recv.shape[2]
     halves = slices // seq_size
+    dest_seq = j // halves
+    half = j % halves
+    dest_t = g * slices + s * halves + half
+    to_self = dest_seq == s
+
+    barrier = pltpu.get_barrier_semaphore()
+    for u in range(tp_size):
+        @pl.when(t != u)
+        def _():
+            pl.semaphore_signal(barrier, inc=1, device_id=(s, u), device_id_type=mesh_type)
+
+    @pl.when(to_self)
+    def _():
+        pl.semaphore_wait(barrier, tp_size - 1)
+
+    @pl.when(jnp.logical_not(to_self))
+    def _():
+        pl.semaphore_signal(
+            barrier, inc=1, device_id=(dest_seq, dest_t), device_id_type=mesh_type
+        )
+        pl.semaphore_wait(barrier, tp_size)
 
     def stage1(i):
         return pltpu.make_async_remote_copy(
@@ -68,10 +89,6 @@
         total = total + recv[i]
     summed[...] = total.astype(summed.dtype)
 
-    dest_seq = j // halves
-    half = j % halves
-    dest_t = g * slices + s * halves + half
-    to_self = dest_seq == s
 
     @pl.when(to_self)
     def _():
@@ -143,6 +160,13 @@
             device_id=peer(u), device_id_type=mesh_type,
         )
 
+    barrier = pltpu.get_barrier_semaphore()
+    for u in range(size):
+        @pl.when(me != u)
+        def _():
+            pl.semaphore_signal(barrier, inc=1, device_id=peer(u), device_id_type=mesh_type)
+    pl.semaphore_wait(barrier, size - 1)
+
     for u in range(size):
         @pl.when(me == u)
         def _():
@@ -165,7 +189,7 @@
     out_ref[...] = landing[...]
 
 
-def gather_axis(piece, axis, size):
+def gather_axis(piece, axis, size, key):
     return pl.pallas_call(
         functools.partial(gather_kernel, axis, size),
         out_shape=jax.ShapeDtypeStruct((size,) + piece.shape, piece.dtype),
@@ -176,7 +200,7 @@
             pltpu.SemaphoreType.DMA((size,)),
             pltpu.SemaphoreType.DMA((size,)),
         ],
-        compiler_params=pltpu.CompilerParams(has_side_effects=True),
+        compiler_params=pltpu.CompilerParams(collective_id=key, has_side_effects=True),
     )(piece)
 
 
@@ -200,7 +224,7 @@
             pltpu.SemaphoreType.DMA((tp_size,)),
             pltpu.SemaphoreType.DMA((tp_size,)),
         ],
-        compiler_params=pltpu.CompilerParams(has_side_effects=True),
+        compiler_params=pltpu.CompilerParams(collective_id=2, has_side_effects=True),
     )(part)
 
 
@@ -278,7 +302,7 @@
         ],
         axis=2,
     )
-    every = gather_axis(stats.reshape(req_dev * steps, -1), "seq", seq_size).reshape(
+    every = gather_axis(stats.reshape(req_dev * steps, -1), "seq", seq_size, 0).reshape(
         (seq_size,) + stats.shape
     )
     block_sums = every[..., :width]
@@ -306,7 +330,7 @@
     capacity = (5 * requests * topk + 4 * experts - 1) // (4 * experts)
     expert_range = jnp.arange(experts, dtype=jnp.int32)
     packed = jnp.concatenate([normed, expert_ids.astype(jnp.bfloat16)], axis=2)
-    all_packed = gather_axis(packed.reshape(req_dev * steps, -1), "tp", tp_size).reshape(
+    all_packed = gather_axis(packed.reshape(req_dev * steps, -1), "tp", tp_size, 1).reshape(
         requests, steps, -1
     )
     all_normed = all_packed[:, :, :width]

time: 112 us -> 94.6 us (0.84)
  Pallas kernels: 79 us -> 61.8 us
    pallas_call x2, Pallas kernels: 46 us -> 37 us  [gather_axis(): pl.pallas_call(functools.partial(gather_kernel, axis, size), out_shape=ja...]
    pallas_call x1, Pallas kernels: 33 us -> 24.8 us  [combine_rows(): pl.pallas_call(functools.partial(combine_kernel, seq_size, tp_size, slice...]
where the time goes in v5:
time: 94.6 us; the launch traced here: 93.8 us
  Pallas kernels  61.8 us (65%)
  matrix products  14.9 us (16%)
  local copies, waits for them, and re-layouts  12.7 us (13%)
  other arithmetic  3.41 us (4%)
  between operations  1.02 us (1%)
    pallas_call x2, Pallas kernels, gather_axis(): pl.pallas_call(functools.partial(gather_kernel, axis, size), out_shape=ja...  37 us
    pallas_call x1, Pallas kernels, combine_rows(): pl.pallas_call(functools.partial(combine_kernel, seq_size, tp_size, slice...  24.8 us
    dot_general x1, matrix products, body(): jnp.einsum('rqd,rpd->rqp', q_wide, key_cache, preferred_element_type=jnp....  5.06 us
    dot_general x2, local copies, waits for them, and re-layouts, body(): jnp.einsum('rtzyp,zyhpf->rthf', pick, gathered, precision=lax.Precision.H...  3.79 us
    dot_general x1, matrix products, body(): produced = jnp.dot(inner, down_weight, preferred_element_type=jnp.float32)  2.02 us

profile of v5, /device:TPU:1, one launch (start us, length us, event | category | flops | bytes accessed | tf_op | source)
XLA Modules:
  0.0 93.8 jit_solution(183356219995528741)
XLA Ops:
  0.7 0.9 bitcast_select_fusion
  1.7 1.0 %fusion.63 = (f32[3,64]{1,0:T(4,128)S(1)}, f32[3,64,4]{1,2,0:T(4,128)S(1)}) fusion(bf16[3,64,1024]{2,1,0:T(8,128)(2,1)S(1)} %bitcast_select_fusion, bf16[3,4,1024]{2,1,0:T(4,128)(2,1)} %param.16, pred[64,4]{0,1:T(4,128)(4,1)S(1)} %fusion.50), kind=kOutput, calls=%fused_computation.117 | convolution fusion | flops 1574976 | bytes 421888 | tf_op jit(solution)/shard_map/rqd,rsd->rqs/dot_general | solution.py:270
  2.7 0.9 broadcast_compare_fusion
  3.6 5.1 %fusion.62 = (f32[3,64]{1,0:T(4,128)S(1)}, f32[3,64,1024]{2,1,0:T(8,128)S(1)}) fusion(bf16[3,64,1024]{2,1,0:T(8,128)(2,1)S(1)} %bitcast_select_fusion, bf16[3,1024,1024]{2,1,0:T(8,128)(2,1)} %param.18, pred[3,1024]{1,0:T(4,128)(4,1)S(1)} %broadcast_compare_fusion), kind=kOutput, calls=%fused_computation.116 | convolution fusion | flops 403242816 | bytes 7474944 | tf_op jit(solution)/shard_map/cache_scores/rqd,rpd->rqp/dot_general | solution.py:263
  8.6 0.3 fusion.43
  9.0 1.5 %select_reduce_fusion = f32[3,4,1024]{2,1,0:T(4,128)S(1)} fusion(pred[16,1024]{1,0:T(8,128)(4,1)S(1)} %iota_compare_fusion.1, f32[3,64,1024]{2,1,0:T(8,128)S(1)} %fusion.43, bf16[3,1024,1024]{2,1,0:T(8,128)(2,1)S(1)} %copy-done.1, f32[3,64,1024]{2,1,0:T(8,128)S(1)} %get-tuple-element.10, f32[3,64]{1,0:T(4,128)S(1)} %max.12, ...), kind=kOutput, calls=%fused_computation.14 | convolution fusion | flops 403820544 | bytes 7933696 | tf_op jit(solution)/shard_map/cache_values/rqp,rpd->rqd/dot_general | solution.py:281
  10.6 0.3 fusion.11
  11.0 0.7 concatenate.10.piece_ref
  11.7 10.2 %shard_map.149 = f32[4,12,1056]{2,1,0:T(8,128)} custom-call(f32[12,1056]{1,0:T(8,128)} %concatenate.10.piece_ref), custom_call_target="tpu_custom_call" | custom-call | tf_op jit(solution)/shard_map/pallas_call | solution.py:193
  21.9 1.0 %copy.55 = f32[4,12,1056]{2,0,1:T(4,128)S(1)} copy(f32[4,12,1056]{2,1,0:T(8,128)} %shard_map.149) | data formatting | bytes 405504 | tf_op jit(solution)/shard_map/pallas_call | solution.py:193
  23.0 0.2 broadcast_in_dim.159
  23.2 0.2 reshape.242
  23.4 0.2 fusion.17
  23.8 0.5 multiply_reduce_fusion
  24.3 0.6 dynamic-slice_convert_fusion
  25.1 0.6 reshape.244.piece_ref
  25.8 26.8 %shard_map.150 = bf16[32,12,1026]{2,1,0:T(8,128)(2,1)} custom-call(bf16[12,1026]{1,0:T(8,128)(2,1)} %reshape.244.piece_ref), custom_call_target="tpu_custom_call" | custom-call | tf_op jit(solution)/shard_map/pallas_call | solution.py:193
  52.6 1.8 %reshape.245 = bf16[96,4,1026]{2,1,0:T(4,128)(2,1)S(1)} reshape(bf16[32,12,1026]{2,1,0:T(8,128)(2,1)} %shard_map.150) | data formatting | bytes 1575936 | tf_op jit(solution)/shard_map/reshape | solution.py:333
  54.4 1.1 %slice.24 = bf16[96,4,1024]{2,1,0:T(4,128)(2,1)} slice(bf16[96,4,1026]{2,1,0:T(4,128)(2,1)S(1)} %reshape.245), slice={[0:96], [0:4], [0:1024]} | slice | bytes 1572864 | tf_op jit(solution)/shard_map/slice | solution.py:336
  55.8 0.1 copy.60
  56.3 1.7 %convolution_convert_fusion = bf16[4,15,1024]{2,1,0:T(8,128)(2,1)S(1)} fusion(bf16[96,4,1024]{2,1,0:T(4,128)(2,1)} %slice.24, s32[96,4]{0,1:T(4,128)S(1)} %select_reduce_fusion.4, pred[96,4]{0,1:T(4,128)(4,1)S(1)} %compare_and_fusion), kind=kOutput, calls=%fused_computation.5 | convolution fusion | flops 11869440 | bytes 911232 | tf_op jit(solution)/shard_map/crt,rtd->tcd/dot_general | solution.py:355
  58.0 1.5 %fusion.65 = f32[60,352]{1,0:T(8,128)S(1)} fusion(bf16[60,1024]{1,0:T(8,128)(2,1)S(1)} %reshape.246, bf16[352,1024]{1,0:T(8,128)(2,1)} %param.25), kind=kOutput, calls=%fused_computation.119 | convolution fusion | flops 43253760 | bytes 928256 | tf_op jit(solution)/shard_map/dot_general | solution.py:365
  59.5 2.0 %fusion.4 = f32[60,1024]{1,0:T(8,128)S(1)} fusion(bf16[352,1024]{1,0:T(8,128)(2,1)} %param.27, bf16[60,1024]{1,0:T(8,128)(2,1)S(1)} %reshape.246, bf16[352,1024]{1,0:T(8,128)(2,1)} %param.26, f32[60,352]{1,0:T(8,128)S(1)} %fusion.65), kind=kOutput, calls=%fused_computation.8 | convolution fusion | flops 86718720 | bytes 1894912 | tf_op jit(solution)/shard_map/dot_general | solution.py:368
  61.5 0.7 pad.4.part_ref
  62.2 24.8 %shard_map.151 = bf16[32,64,128]{2,1,0:T(8,128)(2,1)} custom-call(f32[64,1024]{1,0:T(8,128)} %pad.4.part_ref), custom_call_target="tpu_custom_call" | custom-call | tf_op jit(solution)/shard_map/pallas_call | solution.py:210
  87.0 2.4 %copy.74 = bf16[2,128,64,4,4]{1,0,2,4,3:T(2,128)(2,1)} copy(bf16[2,128,64,4,4]{1,2,0,3,4:T(8,128)(2,1)} %bitcast.46) | data formatting | bytes 1048576 | tf_op jit(solution)/shard_map/rtzyp,zyhpf->rthf/dot_general | solution.py:385
  89.5 1.4 %reshape.250 = bf16[256,64,4,4,1]{0,1,3,2,4:T(8,128)(2,1)S(1)} reshape(bf16[2,128,64,4,4]{1,0,2,4,3:T(2,128)(2,1)} %copy.74) | data formatting | bytes 1048576 | tf_op jit(solution)/shard_map/rtzyp,zyhpf->rthf/dot_general | solution.py:385
  91.0 0.4 fusion.9
  91.4 0.1 copy.66
  91.6 0.2 rev.3
  92.6 0.2 select_reduce_fusion.1
  92.8 1.0 %fusion.6 = bf16[3,4,256]{2,1,0:T(4,128)(2,1)} fusion(bf16[256,64,4,4,1]{0,1,3,2,4:T(8,128)(2,1)S(1)} %reshape.250, f32[3,4,4,4,64]{4,3,2,1,0:T(4,128)S(1)} %select_reduce_fusion.1, f32[3,4,1024]{2,1,0:T(4,128)S(1)} %get-tuple-element.3, s32[]{:T(128)S(6)} %select_n.98), kind=kOutput, calls=%fused_computation.11 | convolution fusion | flops 37754880 | bytes 591876 | tf_op jit(solution)/shard_map/rtzyp,zyhpf->rthf/dot_general | solution.py:385
  (61 shorter events, 2.3 us)
Async XLA Ops:
  0.6 23.1 %copy-start = (bf16[1024,1024]{1,0:T(8,128)(2,1)S(1)}, bf16[1024,1024]{1,0:T(8,128)(2,1)}, u32[]{:S(2)}) copy-start(bf16[1024,1024]{1,0:T(8,128)(2,1)} %param.21) | copy-start | bytes 6291460
  0.6 8.0 %copy-start.4 = (bf16[3,4,1024]{2,1,0:T(4,128)(2,1)S(1)}, bf16[3,4,1024]{2,1,0:T(4,128)(2,1)}, u32[]{:S(2)}) copy-start(bf16[3,4,1024]{2,1,0:T(4,128)(2,1)} %param.17) | copy-start | bytes 73732
  2.7 6.3 %copy-start.1 = (bf16[3,1024,1024]{2,1,0:T(8,128)(2,1)S(1)}, bf16[3,1024,1024]{2,1,0:T(8,128)(2,1)}, u32[]{:S(2)}) copy-start(bf16[3,1024,1024]{2,1,0:T(8,128)(2,1)} %param.19) | copy-start | bytes 18874372
  8.6 15.1 %copy-start.3 = (bf16[3,4,1024]{2,1,0:T(4,128)(2,1)S(1)}, bf16[3,4,1024]{2,1,0:T(4,128)(2,1)}, u32[]{:S(2)}) copy-start(bf16[3,4,1024]{2,1,0:T(4,128)(2,1)} %param.14) | copy-start | bytes 73732
  9.0 15.9 %copy-start.6 = (s32[3,4,2]{1,2,0:T(2,128)S(1)}, s32[3,4,2]{1,2,0:T(2,128)}, u32[]{:S(2)}) copy-start(s32[3,4,2]{1,2,0:T(2,128)} %param.24) | copy-start | bytes 292
  9.0 16.0 %copy-start.5 = (f32[1024]{0:T(1024)S(1)}, f32[1024]{0:T(1024)}, u32[]{:S(2)}) copy-start(f32[1024]{0:T(1024)} %param.22) | copy-start | bytes 12292
  52.6 38.5 %copy-start.7 = (bf16[1024,16]{0,1:T(8,128)(2,1)S(1)}, bf16[1024,16]{0,1:T(8,128)(2,1)}, u32[]{:S(2)}) copy-start(bf16[1024,16]{0,1:T(8,128)(2,1)} %param.23) | copy-start | bytes 98308
  55.6 35.4 %copy-start.2 = (bf16[96,4,1024]{2,1,0:T(4,128)(2,1)S(1)}, bf16[96,4,1024]{2,1,0:T(4,128)(2,1)}, u32[]{:S(2)}) copy-start(bf16[96,4,1024]{2,1,0:T(4,128)(2,1)} %slice.24) | copy-start | bytes 2359300

commit v6 on v5

--- a/solution.py
+++ b/solution.py
@@ -14,8 +14,8 @@
 norm_epsilon = 1e-06
 
 
-def combine_kernel(seq_size, tp_size, slices, part_ref, out_ref, recv, summed, middle, landing,
-                   send1, recv1, send2, recv2, send3, recv3):
+def combine_kernel(seq_size, tp_size, slices, part_ref, select_ref, out_ref, recv, summed, middle,
+                   outgoing, landing, send1, recv1, send2, recv2, send3, recv3):
     mesh_type = pl.DeviceIdType.MESH
     s = lax.axis_index("seq")
     t = lax.axis_index("tp")
@@ -115,16 +115,24 @@
             device_id=(src_seq, src_t), device_id_type=mesh_type,
         ).wait_recv()
 
+    picked = jnp.dot(
+        select_ref[...].reshape(-1, select_ref.shape[2]),
+        middle[...].astype(jnp.float32),
+        precision=lax.Precision.HIGHEST,
+        preferred_element_type=jnp.float32,
+    )
+    outgoing[...] = picked.reshape(outgoing.shape).astype(outgoing.dtype)
+
     def stage3(u):
         return pltpu.make_async_remote_copy(
-            middle, landing.at[t], send3.at[u], recv3.at[t],
+            outgoing.at[u], landing.at[t], send3.at[u], recv3.at[t],
             device_id=(s, u), device_id_type=mesh_type,
         )
 
     for u in range(tp_size):
         @pl.when(t == u)
         def _():
-            pltpu.make_async_copy(middle, landing.at[u], recv3.at[u]).start()
+            pltpu.make_async_copy(outgoing.at[u], landing.at[u], recv3.at[u]).start()
 
         @pl.when(t != u)
         def _():
@@ -133,13 +141,13 @@
     for u in range(tp_size):
         @pl.when(t == u)
         def _():
-            pltpu.make_async_copy(middle, landing.at[u], recv3.at[u]).wait()
+            pltpu.make_async_copy(outgoing.at[u], landing.at[u], recv3.at[u]).wait()
 
         @pl.when(t != u)
         def _():
             stage3(u).wait_send()
             pltpu.make_async_remote_copy(
-                middle, landing.at[u], send3.at[u], recv3.at[u],
+                outgoing.at[u], landing.at[u], send3.at[u], recv3.at[u],
                 device_id=(s, u), device_id_type=mesh_type,
             ).wait_recv()
 
@@ -204,19 +212,21 @@
     )(piece)
 
 
-def combine_rows(part, seq_size, tp_size, slices):
+def combine_rows(part, select, seq_size, tp_size, slices):
     rows, width = part.shape
     chunk = width // slices
+    tokens = select.shape[1]
     return pl.pallas_call(
         functools.partial(combine_kernel, seq_size, tp_size, slices),
-        out_shape=jax.ShapeDtypeStruct((tp_size, rows, chunk), jnp.bfloat16),
-        in_specs=[pl.BlockSpec(memory_space=pltpu.VMEM)],
+        out_shape=jax.ShapeDtypeStruct((tp_size, tokens, chunk), jnp.bfloat16),
+        in_specs=[pl.BlockSpec(memory_space=pltpu.VMEM)] * 2,
         out_specs=pl.BlockSpec(memory_space=pltpu.VMEM),
         scratch_shapes=[
             pltpu.VMEM((slices, rows, chunk), jnp.float32),
             pltpu.VMEM((rows, chunk), jnp.bfloat16),
             pltpu.VMEM((rows, chunk), jnp.bfloat16),
-            pltpu.VMEM((tp_size, rows, chunk), jnp.bfloat16),
+            pltpu.VMEM((tp_size, tokens, chunk), jnp.bfloat16),
+            pltpu.VMEM((tp_size, tokens, chunk), jnp.bfloat16),
             pltpu.SemaphoreType.DMA((slices,)),
             pltpu.SemaphoreType.DMA((slices,)),
             pltpu.SemaphoreType.DMA((1,)),
@@ -225,7 +235,7 @@
             pltpu.SemaphoreType.DMA((tp_size,)),
         ],
         compiler_params=pltpu.CompilerParams(collective_id=2, has_side_effects=True),
-    )(part)
+    )(part, select)
 
 
 def body(
@@ -369,22 +379,27 @@
     groups = tp_size // slices
     padded = 8 * ((steps * capacity + 7) // 8)
     part = jnp.pad(produced, ((0, padded - steps * capacity), (0, 0)))
-    gathered = combine_rows(part, seq_size, tp_size, slices)
     halves = slices // seq_size
-    gathered = gathered.astype(jnp.float32).reshape(groups, tp_size // (groups * halves), halves, padded, width // slices)
-    own_slots = lax.dynamic_slice_in_dim(all_slots, tp_index * req_dev, req_dev, 0)
-    own_share = lax.dynamic_slice_in_dim(share, tp_index * req_dev, req_dev, 0)
-    weight = jnp.where(own_slots < capacity, own_share, 0.0)
-    row_of = jnp.arange(steps, dtype=jnp.int32)[None, :, None] * capacity + own_slots
-    hit = (
-        (expert_ids[..., None, None, None] % groups == jnp.arange(groups)[:, None, None])
-        & (expert_ids[..., None, None, None] // groups == jnp.arange(tp_size // (groups * halves))[None, :, None])
-        & (row_of[..., None, None, None] == jnp.arange(padded)[None, None, :])
-    )
-    pick = jnp.sum(jnp.where(hit, weight[..., None, None, None], 0.0), axis=2)
-    mixture = jnp.einsum(
-        "rtzyp,zyhpf->rthf", pick, gathered, precision=lax.Precision.HIGHEST
-    ).reshape(req_dev, steps, feature_block)
+    held = ((tp_index % slices) // halves) * groups + tp_index // slices
+    held_match = (all_ids == held) & (all_slots < capacity)
+    held_row = jnp.arange(steps, dtype=jnp.int32)[None, :, None] * capacity + all_slots
+    select_rows = jnp.sum(
+        jnp.where(
+            held_match[..., None] & (held_row[..., None] == jnp.arange(padded)),
+            share[..., None],
+            0.0,
+        ),
+        axis=2,
+    ).reshape(tp_size, req_dev * steps, padded)
+    tokens = 16 * ((req_dev * steps + 15) // 16)
+    select_rows = jnp.pad(select_rows, ((0, 0), (0, tokens - req_dev * steps), (0, 0)))
+    landed = combine_rows(part, select_rows, seq_size, tp_size, slices)
+    landed = landed.astype(jnp.float32).reshape(tp_size // halves, halves, tokens, width // slices)
+    mixture = (
+        jnp.sum(landed, axis=0)[:, : req_dev * steps]
+        .transpose(1, 0, 2)
+        .reshape(req_dev, steps, feature_block)
+    )
     own_residual = lax.dynamic_slice_in_dim(residual, seq_index * feature_block, feature_block, 2)
     layer_out = (own_residual + mixture).astype(jnp.bfloat16)
     return (attn_out, layer_out)

time: 94.6 us -> 89.9 us (0.950)
  local copies, waits for them, and re-layouts: 12.7 us -> 8.97 us
  other arithmetic: 3.41 us -> 4.54 us
  matrix products: 14.9 us -> 13.8 us
    dot_general x2 -> x0, local copies, waits for them, and re-layouts: 3.79 us -> none  [body(): jnp.einsum('rtzyp,zyhpf->rthf', pick, gathered, precision=lax.Precision.H...]
    dot_general x1 -> x0, matrix products: 1.03 us -> none  [body(): jnp.einsum('rtzyp,zyhpf->rthf', pick, gathered, precision=lax.Precision.H...]
where the time goes in v6:
time: 89.9 us; the launch traced here: 89.5 us
  Pallas kernels  61.1 us (68%)
  matrix products  13.8 us (15%)
  local copies, waits for them, and re-layouts  8.97 us (10%)
  other arithmetic  4.54 us (5%)
  between operations  1.01 us (1%)
    pallas_call x2, Pallas kernels, gather_axis(): pl.pallas_call(functools.partial(gather_kernel, axis, size), out_shape=ja...  37 us
    pallas_call x1, Pallas kernels, combine_rows(): pl.pallas_call(functools.partial(combine_kernel, seq_size, tp_size, slice...  24.2 us
    dot_general x1, matrix products, body(): jnp.einsum('rqd,rpd->rqp', q_wide, key_cache, preferred_element_type=jnp....  5.06 us
    dot_general x1, matrix products, body(): produced = jnp.dot(inner, down_weight, preferred_element_type=jnp.float32)  2.02 us
    reshape x1, local copies, waits for them, and re-layouts, body(): gather_axis(packed.reshape(req_dev * steps, -1), 'tp', tp_size, 1)  1.83 us

profile of v6, /device:TPU:1, one launch (start us, length us, event | category | flops | bytes accessed | tf_op | source)
XLA Modules:
  0.0 89.5 jit_solution(2251128836796977813)
XLA Ops:
  0.7 0.9 %bitcast_select_fusion = bf16[3,64,1024]{2,1,0:T(8,128)(2,1)S(1)} fusion(pred[64,1024]{1,0:T(8,128)(4,1)S(1)} %bitcast.39, bf16[3,4,1024]{2,1,0:T(4,128)(2,1)} %param.15), kind=kLoop, calls=%fused_computation.18 | loop fusion | flops 196608 | bytes 483328 | tf_op jit(solution)/shard_map/jit(_where)/select_n | solution.py:268
  1.7 1.0 %fusion.59 = (f32[3,64]{1,0:T(4,128)S(1)}, f32[3,64,4]{1,2,0:T(4,128)S(1)}) fusion(bf16[3,64,1024]{2,1,0:T(8,128)(2,1)S(1)} %bitcast_select_fusion, bf16[3,4,1024]{2,1,0:T(4,128)(2,1)} %param.16, pred[64,4]{0,1:T(4,128)(4,1)S(1)} %fusion.47), kind=kOutput, calls=%fused_computation.104 | convolution fusion | flops 1574976 | bytes 421888 | tf_op jit(solution)/shard_map/rqd,rsd->rqs/dot_general | solution.py:280
  2.7 0.9 broadcast_compare_fusion
  3.6 5.1 %fusion.58 = (f32[3,64]{1,0:T(4,128)S(1)}, f32[3,64,1024]{2,1,0:T(8,128)S(1)}) fusion(bf16[3,64,1024]{2,1,0:T(8,128)(2,1)S(1)} %bitcast_select_fusion, bf16[3,1024,1024]{2,1,0:T(8,128)(2,1)} %param.18, pred[3,1024]{1,0:T(4,128)(4,1)S(1)} %broadcast_compare_fusion), kind=kOutput, calls=%fused_computation.103 | convolution fusion | flops 403242816 | bytes 7474944 | tf_op jit(solution)/shard_map/cache_scores/rqd,rpd->rqp/dot_general | solution.py:273
  8.6 0.3 fusion.41
  9.0 1.5 %select_reduce_fusion = f32[3,4,1024]{2,1,0:T(4,128)S(1)} fusion(pred[16,1024]{1,0:T(8,128)(4,1)S(1)} %iota_compare_fusion.2, f32[3,64,1024]{2,1,0:T(8,128)S(1)} %fusion.41, bf16[3,1024,1024]{2,1,0:T(8,128)(2,1)S(1)} %copy-done.1, f32[3,64,1024]{2,1,0:T(8,128)S(1)} %get-tuple-element.11, f32[3,64]{1,0:T(4,128)S(1)} %max.12, ...), kind=kOutput, calls=%fused_computation.11 | convolution fusion | flops 403820544 | bytes 7933696 | tf_op jit(solution)/shard_map/cache_values/rqp,rpd->rqd/dot_general | solution.py:291
  10.6 0.3 fusion.9
  11.0 0.7 concatenate.10.piece_ref
  11.7 10.2 %shard_map.149 = f32[4,12,1056]{2,1,0:T(8,128)} custom-call(f32[12,1056]{1,0:T(8,128)} %concatenate.10.piece_ref), custom_call_target="tpu_custom_call" | custom-call | tf_op jit(solution)/shard_map/pallas_call | solution.py:201
  21.9 1.0 %copy.43 = f32[4,12,1056]{2,0,1:T(4,128)S(1)} copy(f32[4,12,1056]{2,1,0:T(8,128)} %shard_map.149) | data formatting | bytes 405504 | tf_op jit(solution)/shard_map/pallas_call | solution.py:201
  23.0 0.2 broadcast_in_dim.155
  23.2 0.2 reshape.199
  23.4 0.2 fusion.16
  23.8 0.5 multiply_reduce_fusion
  24.3 0.6 dynamic-slice_convert_fusion
  24.9 0.1 copy.44
  25.1 0.6 reshape.201.piece_ref
  25.8 26.8 %shard_map.150 = bf16[32,12,1026]{2,1,0:T(8,128)(2,1)} custom-call(bf16[12,1026]{1,0:T(8,128)(2,1)} %reshape.201.piece_ref), custom_call_target="tpu_custom_call" | custom-call | tf_op jit(solution)/shard_map/pallas_call | solution.py:201
  52.6 1.8 %reshape.202 = bf16[96,4,1026]{2,1,0:T(4,128)(2,1)S(1)} reshape(bf16[32,12,1026]{2,1,0:T(8,128)(2,1)} %shard_map.150) | data formatting | bytes 1575936 | tf_op jit(solution)/shard_map/reshape | solution.py:343
  54.4 1.1 %slice.28 = bf16[96,4,1024]{2,1,0:T(4,128)(2,1)} slice(bf16[96,4,1026]{2,1,0:T(4,128)(2,1)S(1)} %reshape.202), slice={[0:96], [0:4], [0:1024]} | slice | bytes 1572864 | tf_op jit(solution)/shard_map/slice | solution.py:346
  55.6 0.1 copy.59
  55.7 0.1 copy.47
  56.3 1.7 %convolution_convert_fusion = bf16[4,15,1024]{2,1,0:T(8,128)(2,1)S(1)} fusion(bf16[96,4,1024]{2,1,0:T(4,128)(2,1)} %slice.28, s32[96,4]{0,1:T(4,128)S(1)} %get-tuple-element.7, pred[96,4]{0,1:T(4,128)(4,1)S(1)} %compare_and_fusion.1), kind=kOutput, calls=%fused_computation.5 | convolution fusion | flops 11869440 | bytes 911232 | tf_op jit(solution)/shard_map/crt,rtd->tcd/dot_general | solution.py:365
  58.0 1.5 %fusion.61 = f32[60,352]{1,0:T(8,128)S(1)} fusion(bf16[60,1024]{1,0:T(8,128)(2,1)S(1)} %reshape.203, bf16[352,1024]{1,0:T(8,128)(2,1)} %param.25), kind=kOutput, calls=%fused_computation.106 | convolution fusion | flops 43253760 | bytes 928256 | tf_op jit(solution)/shard_map/dot_general | solution.py:375
  59.5 2.0 %fusion.4 = f32[60,1024]{1,0:T(8,128)S(1)} fusion(bf16[352,1024]{1,0:T(8,128)(2,1)} %param.27, bf16[60,1024]{1,0:T(8,128)(2,1)S(1)} %reshape.203, bf16[352,1024]{1,0:T(8,128)(2,1)} %param.26, f32[60,352]{1,0:T(8,128)S(1)} %fusion.61), kind=kOutput, calls=%fused_computation.8 | convolution fusion | flops 86718720 | bytes 1894912 | tf_op jit(solution)/shard_map/dot_general | solution.py:378
  61.5 0.7 pad.8.part_ref
  62.3 0.4 fusion.6
  62.8 0.1 copy.55
  63.0 0.7 pad.9.select_ref
  63.7 24.2 %shard_map.151 = bf16[32,16,128]{2,1,0:T(8,128)(2,1)} custom-call(f32[64,1024]{1,0:T(8,128)} %pad.8.part_ref, f32[32,16,64]{2,1,0:T(8,128)} %pad.9.select_ref), custom_call_target="tpu_custom_call" | custom-call | tf_op jit(solution)/shard_map/pallas_call | solution.py:219
  87.9 0.9 %convert_reduce_fusion = f32[2,16,128]{2,1,0:T(8,128)S(1)} fusion(bf16[16,2,16,128]{3,2,1,0:T(8,128)(2,1)} %bitcast.38), kind=kLoop, calls=%fused_computation.22 | loop fusion | flops 126976 | bytes 147456 | tf_op jit(solution)/shard_map/reduce_sum | solution.py:399
  88.9 0.6 add_convert_fusion
  (55 shorter events, 1.5 us)
Async XLA Ops:
  0.6 23.1 %copy-start = (bf16[1024,1024]{1,0:T(8,128)(2,1)S(1)}, bf16[1024,1024]{1,0:T(8,128)(2,1)}, u32[]{:S(2)}) copy-start(bf16[1024,1024]{1,0:T(8,128)(2,1)} %param.21) | copy-start | bytes 6291460
  0.6 8.0 %copy-start.4 = (bf16[3,4,1024]{2,1,0:T(4,128)(2,1)S(1)}, bf16[3,4,1024]{2,1,0:T(4,128)(2,1)}, u32[]{:S(2)}) copy-start(bf16[3,4,1024]{2,1,0:T(4,128)(2,1)} %param.17) | copy-start | bytes 73732
  2.7 6.3 %copy-start.1 = (bf16[3,1024,1024]{2,1,0:T(8,128)(2,1)S(1)}, bf16[3,1024,1024]{2,1,0:T(8,128)(2,1)}, u32[]{:S(2)}) copy-start(bf16[3,1024,1024]{2,1,0:T(8,128)(2,1)} %param.19) | copy-start | bytes 18874372
  8.6 15.1 %copy-start.3 = (bf16[3,4,1024]{2,1,0:T(4,128)(2,1)S(1)}, bf16[3,4,1024]{2,1,0:T(4,128)(2,1)}, u32[]{:S(2)}) copy-start(bf16[3,4,1024]{2,1,0:T(4,128)(2,1)} %param.14) | copy-start | bytes 73732
  9.0 15.9 %copy-start.6 = (s32[3,4,2]{1,2,0:T(2,128)S(1)}, s32[3,4,2]{1,2,0:T(2,128)}, u32[]{:S(2)}) copy-start(s32[3,4,2]{1,2,0:T(2,128)} %param.24) | copy-start | bytes 292
  9.0 16.0 %copy-start.5 = (f32[1024]{0:T(1024)S(1)}, f32[1024]{0:T(1024)}, u32[]{:S(2)}) copy-start(f32[1024]{0:T(1024)} %param.22) | copy-start | bytes 12292
  24.3 38.0 %copy-start.7 = (bf16[1024,16]{0,1:T(8,128)(2,1)S(1)}, bf16[1024,16]{0,1:T(8,128)(2,1)}, u32[]{:S(2)}) copy-start(bf16[1024,16]{0,1:T(8,128)(2,1)} %param.23) | copy-start | bytes 98308
  55.6 6.7 %copy-start.2 = (bf16[96,4,1024]{2,1,0:T(4,128)(2,1)S(1)}, bf16[96,4,1024]{2,1,0:T(4,128)(2,1)}, u32[]{:S(2)}) copy-start(bf16[96,4,1024]{2,1,0:T(4,128)(2,1)} %slice.28) | copy-start | bytes 2359300

commit v7 on v6

--- a/solution.py
+++ b/solution.py
@@ -14,8 +14,8 @@
 norm_epsilon = 1e-06
 
 
-def combine_kernel(seq_size, tp_size, slices, part_ref, select_ref, out_ref, recv, summed, middle,
-                   outgoing, landing, send1, recv1, send2, recv2, send3, recv3):
+def combine_kernel(seq_size, tp_size, slices, part_ref, select_ref, out_ref, recv, middle,
+                   outgoing, landing, send1, recv1, send3, recv3):
     mesh_type = pl.DeviceIdType.MESH
     s = lax.axis_index("seq")
     t = lax.axis_index("tp")
@@ -23,27 +23,39 @@
     j = t % slices
     chunk = recv.shape[2]
     halves = slices // seq_size
-    dest_seq = j // halves
-    half = j % halves
-    dest_t = g * slices + s * halves + half
-    to_self = dest_seq == s
+    src_seq = j // halves
+
+    def dest(i):
+        return (i // halves, g * slices + s * halves + i % halves)
+
+    def is_self(i):
+        return (i // halves == s) & (g * slices + s * halves + i % halves == t)
 
     barrier = pltpu.get_barrier_semaphore()
     for u in range(tp_size):
         @pl.when(t != u)
         def _():
             pl.semaphore_signal(barrier, inc=1, device_id=(s, u), device_id_type=mesh_type)
-
-    @pl.when(to_self)
+    for i in range(slices):
+        @pl.when(i // halves != s)
+        def _():
+            pl.semaphore_signal(barrier, inc=1, device_id=dest(i), device_id_type=mesh_type)
+    for k in range(slices):
+        @pl.when((src_seq != s) & (k // halves != s))
+        def _():
+            pl.semaphore_signal(
+                barrier, inc=1, device_id=(src_seq, g * slices + k), device_id_type=mesh_type
+            )
+    far = (seq_size - 1) * halves
+    near = tp_size - 1 + far
+
+    @pl.when(src_seq == s)
     def _():
-        pl.semaphore_wait(barrier, tp_size - 1)
-
-    @pl.when(jnp.logical_not(to_self))
+        pl.semaphore_wait(barrier, near)
+
+    @pl.when(src_seq != s)
     def _():
-        pl.semaphore_signal(
-            barrier, inc=1, device_id=(dest_seq, dest_t), device_id_type=mesh_type
-        )
-        pl.semaphore_wait(barrier, tp_size)
+        pl.semaphore_wait(barrier, near + slices - halves)
 
     def stage1(i):
         return pltpu.make_async_remote_copy(
@@ -51,73 +63,54 @@
             recv.at[j],
             send1.at[i],
             recv1.at[j],
-            device_id=(s, g * slices + i),
+            device_id=dest(i),
             device_id_type=mesh_type,
         )
 
-    def stage1_local(i):
-        return pltpu.make_async_copy(part_ref.at[:, pl.ds(i * chunk, chunk)], recv.at[i], recv1.at[i])
-
     for i in range(slices):
-        @pl.when(j == i)
-        def _():
-            stage1_local(i).start()
-
-        @pl.when(j != i)
+        @pl.when(is_self(i))
+        def _():
+            pltpu.make_async_copy(
+                part_ref.at[:, pl.ds(i * chunk, chunk)], recv.at[j], recv1.at[j]
+            ).start()
+
+        @pl.when(jnp.logical_not(is_self(i)))
         def _():
             stage1(i).start()
 
     for i in range(slices):
-        @pl.when(j == i)
-        def _():
-            stage1_local(i).wait()
-
-        @pl.when(j != i)
+        @pl.when(jnp.logical_not(is_self(i)))
         def _():
             stage1(i).wait_send()
+
+    for k in range(slices):
+        from_self = (src_seq == s) & (k == j)
+
+        @pl.when(from_self)
+        def _():
+            pltpu.make_async_copy(
+                part_ref.at[:, pl.ds(0, chunk)], recv.at[k], recv1.at[k]
+            ).wait()
+
+        @pl.when(jnp.logical_not(from_self))
+        def _():
             pltpu.make_async_remote_copy(
                 part_ref.at[:, pl.ds(0, chunk)],
-                recv.at[i],
-                send1.at[i],
-                recv1.at[i],
-                device_id=(s, g * slices + i),
+                recv.at[k],
+                send1.at[0],
+                recv1.at[k],
+                device_id=(src_seq, g * slices + k),
                 device_id_type=mesh_type,
             ).wait_recv()
 
     total = recv[0]
-    for i in range(1, slices):
-        total = total + recv[i]
-    summed[...] = total.astype(summed.dtype)
-
-
-    @pl.when(to_self)
-    def _():
-        pltpu.make_async_copy(summed, middle, recv2.at[0]).start()
-        pltpu.make_async_copy(summed, middle, recv2.at[0]).wait()
-
-    @pl.when(jnp.logical_not(to_self))
-    def _():
-        copy = pltpu.make_async_remote_copy(
-            summed, middle, send2.at[0], recv2.at[0],
-            device_id=(dest_seq, dest_t), device_id_type=mesh_type,
-        )
-        copy.start()
-        copy.wait_send()
-
-    src_seq = (t % slices) // halves
-    src_t = g * slices + s * halves + t % halves
-    from_self = src_seq == s
-
-    @pl.when(jnp.logical_not(from_self))
-    def _():
-        pltpu.make_async_remote_copy(
-            summed, middle, send2.at[0], recv2.at[0],
-            device_id=(src_seq, src_t), device_id_type=mesh_type,
-        ).wait_recv()
+    for k in range(1, slices):
+        total = total + recv[k]
+    middle[...] = total.astype(middle.dtype)
 
     picked = jnp.dot(
         select_ref[...].reshape(-1, select_ref.shape[2]),
-        middle[...].astype(jnp.float32),
+        middle[...],
         precision=lax.Precision.HIGHEST,
         preferred_element_type=jnp.float32,
     )
@@ -223,14 +216,11 @@
         out_specs=pl.BlockSpec(memory_space=pltpu.VMEM),
         scratch_shapes=[
             pltpu.VMEM((slices, rows, chunk), jnp.float32),
-            pltpu.VMEM((rows, chunk), jnp.bfloat16),
-            pltpu.VMEM((rows, chunk), jnp.bfloat16),
+            pltpu.VMEM((rows, chunk), jnp.float32),
             pltpu.VMEM((tp_size, tokens, chunk), jnp.bfloat16),
             pltpu.VMEM((tp_size, tokens, chunk), jnp.bfloat16),
             pltpu.SemaphoreType.DMA((slices,)),
             pltpu.SemaphoreType.DMA((slices,)),
-            pltpu.SemaphoreType.DMA((1,)),
-            pltpu.SemaphoreType.DMA((1,)),
             pltpu.SemaphoreType.DMA((tp_size,)),
             pltpu.SemaphoreType.DMA((tp_size,)),
         ],

time: 89.9 us -> 87.7 us (0.976)
  Pallas kernels: 61.1 us -> 58.9 us
    pallas_call x1, Pallas kernels: 24.2 us -> 21.9 us  [combine_rows(): pl.pallas_call(functools.partial(combine_kernel, seq_size, tp_size, slice...]
where the time goes in v7:
time: 87.7 us; the launch traced here: 87.3 us
  Pallas kernels  58.9 us (67%)
  matrix products  13.8 us (16%)
  local copies, waits for them, and re-layouts  8.97 us (10%)
  other arithmetic  4.54 us (5%)
  between operations  1.01 us (1%)
    pallas_call x2, Pallas kernels, gather_axis(): pl.pallas_call(functools.partial(gather_kernel, axis, size), out_shape=ja...  37 us
    pallas_call x1, Pallas kernels, combine_rows(): pl.pallas_call(functools.partial(combine_kernel, seq_size, tp_size, slice...  21.9 us
    dot_general x1, matrix products, body(): jnp.einsum('rqd,rpd->rqp', q_wide, key_cache, preferred_element_type=jnp....  5.06 us
    dot_general x1, matrix products, body(): produced = jnp.dot(inner, down_weight, preferred_element_type=jnp.float32)  2.02 us
    reshape x1, local copies, waits for them, and re-layouts, body(): gather_axis(packed.reshape(req_dev * steps, -1), 'tp', tp_size, 1)  1.83 us

profile of v7, /device:TPU:1, one launch (start us, length us, event | category | flops | bytes accessed | tf_op | source)
XLA Modules:
  0.0 87.3 jit_solution(5163629187370949654)
XLA Ops:
  0.7 0.9 %bitcast_select_fusion = bf16[3,64,1024]{2,1,0:T(8,128)(2,1)S(1)} fusion(pred[64,1024]{1,0:T(8,128)(4,1)S(1)} %bitcast.39, bf16[3,4,1024]{2,1,0:T(4,128)(2,1)} %param.15), kind=kLoop, calls=%fused_computation.18 | loop fusion | flops 196608 | bytes 483328 | tf_op jit(solution)/shard_map/jit(_where)/select_n | solution.py:258
  1.7 1.0 %fusion.59 = (f32[3,64]{1,0:T(4,128)S(1)}, f32[3,64,4]{1,2,0:T(4,128)S(1)}) fusion(bf16[3,64,1024]{2,1,0:T(8,128)(2,1)S(1)} %bitcast_select_fusion, bf16[3,4,1024]{2,1,0:T(4,128)(2,1)} %param.16, pred[64,4]{0,1:T(4,128)(4,1)S(1)} %fusion.47), kind=kOutput, calls=%fused_computation.104 | convolution fusion | flops 1574976 | bytes 421888 | tf_op jit(solution)/shard_map/rqd,rsd->rqs/dot_general | solution.py:270
  2.7 0.9 %broadcast_compare_fusion = pred[3,1024]{1,0:T(4,128)(4,1)S(1)} fusion(s32[1024]{0:T(1024)S(1)} %iota_add_fusion, s32[3]{0:T(128)} %param.20), kind=kLoop, calls=%fused_computation.62 | loop fusion | flops 3072 | bytes 7180 | tf_op jit(solution)/shard_map/lt | solution.py:267
  3.6 5.1 %fusion.58 = (f32[3,64]{1,0:T(4,128)S(1)}, f32[3,64,1024]{2,1,0:T(8,128)S(1)}) fusion(bf16[3,64,1024]{2,1,0:T(8,128)(2,1)S(1)} %bitcast_select_fusion, bf16[3,1024,1024]{2,1,0:T(8,128)(2,1)} %param.18, pred[3,1024]{1,0:T(4,128)(4,1)S(1)} %broadcast_compare_fusion), kind=kOutput, calls=%fused_computation.103 | convolution fusion | flops 403242816 | bytes 7474944 | tf_op jit(solution)/shard_map/cache_scores/rqd,rpd->rqp/dot_general | solution.py:263
  8.6 0.3 fusion.41
  9.0 1.5 %select_reduce_fusion = f32[3,4,1024]{2,1,0:T(4,128)S(1)} fusion(pred[16,1024]{1,0:T(8,128)(4,1)S(1)} %iota_compare_fusion.2, f32[3,64,1024]{2,1,0:T(8,128)S(1)} %fusion.41, bf16[3,1024,1024]{2,1,0:T(8,128)(2,1)S(1)} %copy-done.1, f32[3,64,1024]{2,1,0:T(8,128)S(1)} %get-tuple-element.11, f32[3,64]{1,0:T(4,128)S(1)} %max.12, ...), kind=kOutput, calls=%fused_computation.11 | convolution fusion | flops 403820544 | bytes 7933696 | tf_op jit(solution)/shard_map/cache_values/rqp,rpd->rqd/dot_general | solution.py:281
  10.6 0.3 fusion.9
  11.0 0.7 concatenate.10.piece_ref
  11.7 10.2 %shard_map.149 = f32[4,12,1056]{2,1,0:T(8,128)} custom-call(f32[12,1056]{1,0:T(8,128)} %concatenate.10.piece_ref), custom_call_target="tpu_custom_call" | custom-call | tf_op jit(solution)/shard_map/pallas_call | solution.py:194
  21.9 1.0 %copy.43 = f32[4,12,1056]{2,0,1:T(4,128)S(1)} copy(f32[4,12,1056]{2,1,0:T(8,128)} %shard_map.149) | data formatting | bytes 405504 | tf_op jit(solution)/shard_map/pallas_call | solution.py:194
  23.0 0.2 broadcast_in_dim.155
  23.2 0.2 reshape.199
  23.4 0.2 fusion.16
  23.8 0.5 multiply_reduce_fusion
  24.3 0.6 dynamic-slice_convert_fusion
  24.9 0.1 copy.44
  25.1 0.6 reshape.201.piece_ref
  25.8 26.8 %shard_map.150 = bf16[32,12,1026]{2,1,0:T(8,128)(2,1)} custom-call(bf16[12,1026]{1,0:T(8,128)(2,1)} %reshape.201.piece_ref), custom_call_target="tpu_custom_call" | custom-call | tf_op jit(solution)/shard_map/pallas_call | solution.py:194
  52.6 1.8 %reshape.202 = bf16[96,4,1026]{2,1,0:T(4,128)(2,1)S(1)} reshape(bf16[32,12,1026]{2,1,0:T(8,128)(2,1)} %shard_map.150) | data formatting | bytes 1575936 | tf_op jit(solution)/shard_map/reshape | solution.py:333
  54.4 1.1 %slice.28 = bf16[96,4,1024]{2,1,0:T(4,128)(2,1)} slice(bf16[96,4,1026]{2,1,0:T(4,128)(2,1)S(1)} %reshape.202), slice={[0:96], [0:4], [0:1024]} | slice | bytes 1572864 | tf_op jit(solution)/shard_map/slice | solution.py:336
  55.6 0.1 copy.59
  55.7 0.1 copy.47
  56.3 1.7 %convolution_convert_fusion = bf16[4,15,1024]{2,1,0:T(8,128)(2,1)S(1)} fusion(bf16[96,4,1024]{2,1,0:T(4,128)(2,1)} %slice.28, s32[96,4]{0,1:T(4,128)S(1)} %get-tuple-element.7, pred[96,4]{0,1:T(4,128)(4,1)S(1)} %compare_and_fusion.1), kind=kOutput, calls=%fused_computation.5 | convolution fusion | flops 11869440 | bytes 911232 | tf_op jit(solution)/shard_map/crt,rtd->tcd/dot_general | solution.py:355
  58.0 1.5 %fusion.61 = f32[60,352]{1,0:T(8,128)S(1)} fusion(bf16[60,1024]{1,0:T(8,128)(2,1)S(1)} %reshape.203, bf16[352,1024]{1,0:T(8,128)(2,1)} %param.25), kind=kOutput, calls=%fused_computation.106 | convolution fusion | flops 43253760 | bytes 928256 | tf_op jit(solution)/shard_map/dot_general | solution.py:365
  59.5 2.0 %fusion.4 = f32[60,1024]{1,0:T(8,128)S(1)} fusion(bf16[352,1024]{1,0:T(8,128)(2,1)} %param.27, bf16[60,1024]{1,0:T(8,128)(2,1)S(1)} %reshape.203, bf16[352,1024]{1,0:T(8,128)(2,1)} %param.26, f32[60,352]{1,0:T(8,128)S(1)} %fusion.61), kind=kOutput, calls=%fused_computation.8 | convolution fusion | flops 86718720 | bytes 1894912 | tf_op jit(solution)/shard_map/dot_general | solution.py:368
  61.5 0.7 pad.8.part_ref
  62.3 0.4 fusion.6
  62.8 0.1 copy.55
  63.0 0.7 pad.9.select_ref
  63.7 21.9 %shard_map.151 = bf16[32,16,128]{2,1,0:T(8,128)(2,1)} custom-call(f32[64,1024]{1,0:T(8,128)} %pad.8.part_ref, f32[32,16,64]{2,1,0:T(8,128)} %pad.9.select_ref), custom_call_target="tpu_custom_call" | custom-call | tf_op jit(solution)/shard_map/pallas_call | solution.py:212
  85.7 0.9 %convert_reduce_fusion = f32[2,16,128]{2,1,0:T(8,128)S(1)} fusion(bf16[16,2,16,128]{3,2,1,0:T(8,128)(2,1)} %bitcast.38), kind=kLoop, calls=%fused_computation.22 | loop fusion | flops 126976 | bytes 147456 | tf_op jit(solution)/shard_map/reduce_sum | solution.py:389
  86.7 0.6 add_convert_fusion
  (55 shorter events, 1.5 us)
Async XLA Ops:
  0.6 23.1 %copy-start = (bf16[1024,1024]{1,0:T(8,128)(2,1)S(1)}, bf16[1024,1024]{1,0:T(8,128)(2,1)}, u32[]{:S(2)}) copy-start(bf16[1024,1024]{1,0:T(8,128)(2,1)} %param.21) | copy-start | bytes 6291460
  0.6 8.0 %copy-start.4 = (bf16[3,4,1024]{2,1,0:T(4,128)(2,1)S(1)}, bf16[3,4,1024]{2,1,0:T(4,128)(2,1)}, u32[]{:S(2)}) copy-start(bf16[3,4,1024]{2,1,0:T(4,128)(2,1)} %param.17) | copy-start | bytes 73732
  2.7 6.3 %copy-start.1 = (bf16[3,1024,1024]{2,1,0:T(8,128)(2,1)S(1)}, bf16[3,1024,1024]{2,1,0:T(8,128)(2,1)}, u32[]{:S(2)}) copy-start(bf16[3,1024,1024]{2,1,0:T(8,128)(2,1)} %param.19) | copy-start | bytes 18874372
  8.6 15.1 %copy-start.3 = (bf16[3,4,1024]{2,1,0:T(4,128)(2,1)S(1)}, bf16[3,4,1024]{2,1,0:T(4,128)(2,1)}, u32[]{:S(2)}) copy-start(bf16[3,4,1024]{2,1,0:T(4,128)(2,1)} %param.14) | copy-start | bytes 73732
  9.0 15.9 %copy-start.6 = (s32[3,4,2]{1,2,0:T(2,128)S(1)}, s32[3,4,2]{1,2,0:T(2,128)}, u32[]{:S(2)}) copy-start(s32[3,4,2]{1,2,0:T(2,128)} %param.24) | copy-start | bytes 292
  9.0 16.0 %copy-start.5 = (f32[1024]{0:T(1024)S(1)}, f32[1024]{0:T(1024)}, u32[]{:S(2)}) copy-start(f32[1024]{0:T(1024)} %param.22) | copy-start | bytes 12292
  24.3 38.0 %copy-start.7 = (bf16[1024,16]{0,1:T(8,128)(2,1)S(1)}, bf16[1024,16]{0,1:T(8,128)(2,1)}, u32[]{:S(2)}) copy-start(bf16[1024,16]{0,1:T(8,128)(2,1)} %param.23) | copy-start | bytes 98308
  55.6 6.7 %copy-start.2 = (bf16[96,4,1024]{2,1,0:T(4,128)(2,1)S(1)}, bf16[96,4,1024]{2,1,0:T(4,128)(2,1)}, u32[]{:S(2)}) copy-start(bf16[96,4,1024]{2,1,0:T(4,128)(2,1)} %slice.28) | copy-start | bytes 2359300

commit v8 on v7

v8 whole, which is shorter than its diff:
```python
import functools

import jax
import jax.numpy as jnp
from jax import lax
from jax.experimental import pallas as pl
from jax.experimental.pallas import tpu as pltpu
from jax.sharding import PartitionSpec as P

HEADS = 16


masked_score = -1e30
norm_epsilon = 1e-06


def exchange_kernel(seq_size, tp_size, stats_ref, ids_ref, stats_out, ids_out, stats_land,
                    ids_land, send_a, recv_a, send_b, recv_b):
    mesh_type = pl.DeviceIdType.MESH
    s = lax.axis_index("seq")
    t = lax.axis_index("tp")

    barrier = pltpu.get_barrier_semaphore()
    for u in range(seq_size):
        @pl.when(s != u)
        def _():
            pl.semaphore_signal(barrier, inc=1, device_id=(u, t), device_id_type=mesh_type)
    for u in range(tp_size):
        @pl.when(t != u)
        def _():
            pl.semaphore_signal(barrier, inc=1, device_id=(s, u), device_id_type=mesh_type)
    pl.semaphore_wait(barrier, seq_size - 1 + tp_size - 1)

    def along_seq(u, slot):
        return pltpu.make_async_remote_copy(
            stats_ref, stats_land.at[slot], send_a.at[u], recv_a.at[slot],
            device_id=(u, t), device_id_type=mesh_type,
        )

    def along_tp(u, slot):
        return pltpu.make_async_remote_copy(
            ids_ref, ids_land.at[slot], send_b.at[u], recv_b.at[slot],
            device_id=(s, u), device_id_type=mesh_type,
        )

    for u in range(seq_size):
        @pl.when(s == u)
        def _():
            pltpu.make_async_copy(stats_ref, stats_land.at[u], recv_a.at[u]).start()

        @pl.when(s != u)
        def _():
            along_seq(u, s).start()
    for u in range(tp_size):
        @pl.when(t == u)
        def _():
            pltpu.make_async_copy(ids_ref, ids_land.at[u], recv_b.at[u]).start()

        @pl.when(t != u)
        def _():
            along_tp(u, t).start()

    for u in range(seq_size):
        @pl.when(s == u)
        def _():
            pltpu.make_async_copy(stats_ref, stats_land.at[u], recv_a.at[u]).wait()

        @pl.when(s != u)
        def _():
            along_seq(u, s).wait_send()
            along_seq(u, u).wait_recv()
    for u in range(tp_size):
        @pl.when(t == u)
        def _():
            pltpu.make_async_copy(ids_ref, ids_land.at[u], recv_b.at[u]).wait()

        @pl.when(t != u)
        def _():
            along_tp(u, t).wait_send()
            along_tp(u, u).wait_recv()

    stats_out[...] = stats_land[...]
    ids_out[...] = ids_land[...]


def exchange(stats, ids, seq_size, tp_size):
    return pl.pallas_call(
        functools.partial(exchange_kernel, seq_size, tp_size),
        out_shape=(
            jax.ShapeDtypeStruct((seq_size,) + stats.shape, stats.dtype),
            jax.ShapeDtypeStruct((tp_size,) + ids.shape, ids.dtype),
        ),
        in_specs=[pl.BlockSpec(memory_space=pltpu.VMEM)] * 2,
        out_specs=(pl.BlockSpec(memory_space=pltpu.VMEM), pl.BlockSpec(memory_space=pltpu.VMEM)),
        scratch_shapes=[
            pltpu.VMEM((seq_size,) + stats.shape, stats.dtype),
            pltpu.VMEM((tp_size,) + ids.shape, ids.dtype),
            pltpu.SemaphoreType.DMA((seq_size,)),
            pltpu.SemaphoreType.DMA((seq_size,)),
            pltpu.SemaphoreType.DMA((tp_size,)),
            pltpu.SemaphoreType.DMA((tp_size,)),
        ],
        compiler_params=pltpu.CompilerParams(collective_id=0, has_side_effects=True),
    )(stats, ids)


def expert_kernel(seq_size, tp_size, slices, piece_ref, pick_in_ref, gate_ref, up_ref,
                  down_ref, pick_out_ref, out_ref, everyone, part, recv, middle, outgoing,
                  landing, send0, recv0, send1, recv1, send3, recv3):
    mesh_type = pl.DeviceIdType.MESH
    s = lax.axis_index("seq")
    t = lax.axis_index("tp")
    g = t // slices
    j = t % slices
    chunk = recv.shape[2]
    halves = slices // seq_size
    src_seq = j // halves

    def dest(i):
        return (i // halves, g * slices + s * halves + i % halves)

    def is_self(i):
        return (i // halves == s) & (g * slices + s * halves + i % halves == t)

    barrier = pltpu.get_barrier_semaphore()
    for u in range(tp_size):
        @pl.when(t != u)
        def _():
            pl.semaphore_signal(barrier, inc=1, device_id=(s, u), device_id_type=mesh_type)
    for i in range(slices):
        @pl.when(i // halves != s)
        def _():
            pl.semaphore_signal(barrier, inc=1, device_id=dest(i), device_id_type=mesh_type)
    for k in range(slices):
        @pl.when((src_seq != s) & (k // halves != s))
        def _():
            pl.semaphore_signal(
                barrier, inc=1, device_id=(src_seq, g * slices + k), device_id_type=mesh_type
            )
    far = (seq_size - 1) * halves
    near = tp_size - 1 + far

    @pl.when(src_seq == s)
    def _():
        pl.semaphore_wait(barrier, near)

    @pl.when(src_seq != s)
    def _():
        pl.semaphore_wait(barrier, near + slices - halves)

    def gather(u, slot):
        return pltpu.make_async_remote_copy(
            piece_ref, everyone.at[slot], send0.at[u], recv0.at[slot],
            device_id=(s, u), device_id_type=mesh_type,
        )

    for u in range(tp_size):
        @pl.when(t == u)
        def _():
            pltpu.make_async_copy(piece_ref, everyone.at[u], recv0.at[u]).start()

        @pl.when(t != u)
        def _():
            gather(u, t).start()

    for u in range(tp_size):
        @pl.when(t == u)
        def _():
            pltpu.make_async_copy(piece_ref, everyone.at[u], recv0.at[u]).wait()

        @pl.when(t != u)
        def _():
            gather(u, t).wait_send()
            gather(u, u).wait_recv()

    rows_in = everyone[...].reshape(-1, everyone.shape[2])
    buffer = jnp.dot(pick_in_ref[...], rows_in, preferred_element_type=jnp.float32).astype(
        jnp.bfloat16
    )
    contract = (((1,), (1,)), ((), ()))
    gate = lax.dot_general(buffer, gate_ref[...], contract, preferred_element_type=jnp.float32)
    upward = lax.dot_general(buffer, up_ref[...], contract, preferred_element_type=jnp.float32)
    inner = (jax.nn.gelu(gate) * upward).astype(jnp.bfloat16)
    part[...] = jnp.dot(inner, down_ref[...], preferred_element_type=jnp.float32)

    def stage1(i):
        return pltpu.make_async_remote_copy(
            part.at[:, pl.ds(i * chunk, chunk)],
            recv.at[j],
            send1.at[i],
            recv1.at[j],
            device_id=dest(i),
            device_id_type=mesh_type,
        )

    for i in range(slices):
        @pl.when(is_self(i))
        def _():
            pltpu.make_async_copy(part.at[:, pl.ds(i * chunk, chunk)], recv.at[j], recv1.at[j]).start()

        @pl.when(jnp.logical_not(is_self(i)))
        def _():
            stage1(i).start()

    for i in range(slices):
        @pl.when(jnp.logical_not(is_self(i)))
        def _():
            stage1(i).wait_send()

    for k in range(slices):
        from_self = (src_seq == s) & (k == j)

        @pl.when(from_self)
        def _():
            pltpu.make_async_copy(part.at[:, pl.ds(0, chunk)], recv.at[k], recv1.at[k]).wait()

        @pl.when(jnp.logical_not(from_self))
        def _():
            pltpu.make_async_remote_copy(
                part.at[:, pl.ds(0, chunk)],
                recv.at[k],
                send1.at[0],
                recv1.at[k],
                device_id=(src_seq, g * slices + k),
                device_id_type=mesh_type,
            ).wait_recv()

    total = recv[0]
    for k in range(1, slices):
        total = total + recv[k]
    middle[...] = total.astype(middle.dtype)

    picked = jnp.dot(
        pick_out_ref[...].reshape(-1, pick_out_ref.shape[2]),
        middle[...],
        preferred_element_type=jnp.float32,
    )
    outgoing[...] = picked.reshape(outgoing.shape).astype(outgoing.dtype)

    def stage3(u):
        return pltpu.make_async_remote_copy(
            outgoing.at[u], landing.at[t], send3.at[u], recv3.at[t],
            device_id=(s, u), device_id_type=mesh_type,
        )

    for u in range(tp_size):
        @pl.when(t == u)
        def _():
            pltpu.make_async_copy(outgoing.at[u], landing.at[u], recv3.at[u]).start()

        @pl.when(t != u)
        def _():
            stage3(u).start()

    for u in range(tp_size):
        @pl.when(t == u)
        def _():
            pltpu.make_async_copy(outgoing.at[u], landing.at[u], recv3.at[u]).wait()

        @pl.when(t != u)
        def _():
            stage3(u).wait_send()
            pltpu.make_async_remote_copy(
                outgoing.at[u], landing.at[u], send3.at[u], recv3.at[u],
                device_id=(s, u), device_id_type=mesh_type,
            ).wait_recv()

    out_ref[...] = landing[...]


def run_experts(piece, pick_in, gate_weight, up_weight, down_weight, pick_out, seq_size,
                tp_size, slices):
    tokens, width = piece.shape
    rows = pick_in.shape[0]
    chunk = width // slices
    return pl.pallas_call(
        functools.partial(expert_kernel, seq_size, tp_size, slices),
        out_shape=jax.ShapeDtypeStruct((tp_size, tokens, chunk), jnp.bfloat16),
        in_specs=[pl.BlockSpec(memory_space=pltpu.VMEM)] * 6,
        out_specs=pl.BlockSpec(memory_space=pltpu.VMEM),
        scratch_shapes=[
            pltpu.VMEM((tp_size, tokens, width), jnp.bfloat16),
            pltpu.VMEM((rows, width), jnp.float32),
            pltpu.VMEM((slices, rows, chunk), jnp.float32),
            pltpu.VMEM((rows, chunk), jnp.bfloat16),
            pltpu.VMEM((tp_size, tokens, chunk), jnp.bfloat16),
            pltpu.VMEM((tp_size, tokens, chunk), jnp.bfloat16),
            pltpu.SemaphoreType.DMA((tp_size,)),
            pltpu.SemaphoreType.DMA((tp_size,)),
            pltpu.SemaphoreType.DMA((slices,)),
            pltpu.SemaphoreType.DMA((slices,)),
            pltpu.SemaphoreType.DMA((tp_size,)),
            pltpu.SemaphoreType.DMA((tp_size,)),
        ],
        compiler_params=pltpu.CompilerParams(collective_id=1, has_side_effects=True),
    )(piece, pick_in, gate_weight, up_weight, down_weight, pick_out)


def body(
    hidden_in,
    new_query,
    new_key,
    new_value,
    key_cache,
    value_cache,
    lengths,
    out_weight,
    norm_gain,
    router_weight,
    expert_ids,
    gate_weight,
    up_weight,
    down_weight,
):
    req_dev, steps, width = hidden_in.shape
    block = key_cache.shape[1]
    head_size = width // HEADS
    scale = head_size ** (-0.5)
    seq_index = lax.axis_index("seq")
    tp_index = lax.axis_index("tp")
    seq_size = lax.axis_size("seq")
    tp_size = lax.axis_size("tp")
    rows = steps * HEADS
    own = req_dev * steps

    head_mask = (jnp.arange(width) // head_size)[None, :] == jnp.arange(HEADS)[:, None]
    q_wide = jnp.where(head_mask[None, None], new_query[:, :, None, :], 0).reshape(
        req_dev, rows, width
    )
    with jax.named_scope("cache_scores"):
        scores = (
            jnp.einsum("rqd,rpd->rqp", q_wide, key_cache, preferred_element_type=jnp.float32)
            * scale
        )
    positions = seq_index * block + jnp.arange(block, dtype=jnp.int32)
    usable = (positions[None, :] < lengths[:, None])[:, None, :]
    scores = jnp.where(usable, scores, masked_score)
    fresh_scores = (
        jnp.einsum("rqd,rsd->rqs", q_wide, new_key, preferred_element_type=jnp.float32) * scale
    )
    causal = (
        (jnp.arange(rows)[:, None] // HEADS) >= jnp.arange(steps)[None, :]
    ) & (seq_index == 0)
    fresh_scores = jnp.where(causal, fresh_scores, masked_score)
    local_max = jnp.maximum(jnp.max(scores, axis=2), jnp.max(fresh_scores, axis=2))
    weights = jnp.where(usable, jnp.exp(scores - local_max[..., None]), 0.0)
    fresh_weights = jnp.where(causal, jnp.exp(fresh_scores - local_max[..., None]), 0.0)
    totals = jnp.sum(weights, axis=2) + jnp.sum(fresh_weights, axis=2)
    with jax.named_scope("cache_values"):
        wide_values = jnp.einsum(
            "rqp,rpd->rqd",
            weights.astype(jnp.bfloat16),
            value_cache,
            preferred_element_type=jnp.float32,
        )
    wide_values = wide_values + jnp.einsum(
        "rqs,rsd->rqd",
        fresh_weights.astype(jnp.bfloat16),
        new_value,
        preferred_element_type=jnp.float32,
    )
    partial = jnp.sum(
        jnp.where(head_mask[None, None], wide_values.reshape(req_dev, steps, HEADS, width), 0.0),
        axis=2,
    )
    stats = jnp.concatenate(
        [
            partial,
            local_max.reshape(req_dev, steps, HEADS),
            totals.reshape(req_dev, steps, HEADS),
        ],
        axis=2,
    ).reshape(own, -1)
    id_count = expert_ids.size
    id_rows = 8
    id_piece = jnp.pad(expert_ids.reshape(1, id_count), ((0, id_rows - 1), (0, 128 - id_count)))
    every, all_id_pieces = exchange(stats, id_piece, seq_size, tp_size)
    every = every.reshape((seq_size, req_dev, steps, -1))
    all_ids = all_id_pieces[:, 0, :id_count].reshape(tp_size * req_dev, steps, -1)
    block_sums = every[..., :width]
    block_max = every[..., width : width + HEADS]
    block_totals = every[..., width + HEADS :]
    overall = jnp.max(block_max, axis=0)
    factors = jnp.exp(block_max - overall[None])
    numer = jnp.sum(jnp.repeat(factors, head_size, axis=-1) * block_sums, axis=0)
    denom = jnp.sum(factors * block_totals, axis=0)
    context = (numer / jnp.repeat(denom, head_size, axis=-1)).astype(jnp.bfloat16)
    attention = jnp.einsum("rtd,de->rte", context, out_weight, preferred_element_type=jnp.float32)
    feature_block = width // seq_size
    attn_out = lax.dynamic_slice_in_dim(
        attention, seq_index * feature_block, feature_block, 2
    ).astype(jnp.bfloat16)
    residual = hidden_in.astype(jnp.float32) + attention
    normed = (
        residual
        * lax.rsqrt(jnp.mean(residual * residual, axis=-1, keepdims=True) + norm_epsilon)
        * norm_gain
    ).astype(jnp.bfloat16)

    experts = router_weight.shape[1]
    topk = expert_ids.shape[2]
    requests = req_dev * tp_size
    capacity = (5 * requests * topk + 4 * experts - 1) // (4 * experts)
    expert_range = jnp.arange(experts, dtype=jnp.int32)
    slices = seq_size * tp_size // experts
    groups = tp_size // slices
    halves = slices // seq_size
    padded = 8 * ((steps * capacity + 7) // 8)
    tokens = 16 * ((own + 15) // 16)

    onehot = all_ids[..., None] == expert_range
    hits = jnp.sum(onehot.astype(jnp.int32), axis=2)
    earlier = jnp.cumsum(hits, axis=0) - hits
    all_slots = jnp.sum(jnp.where(onehot, earlier[:, :, None, :], 0), axis=3)
    row_of = jnp.arange(steps, dtype=jnp.int32)[None, :, None] * capacity + all_slots

    def rows_for(expert):
        hit = (all_ids == expert) & (all_slots < capacity)
        chosen_rows = jnp.any(
            hit[..., None] & (row_of[..., None] == jnp.arange(padded)), axis=2
        ).reshape(tp_size, own, padded)
        return jnp.pad(chosen_rows, ((0, 0), (0, tokens - own), (0, 0))).astype(jnp.bfloat16)

    mine = (seq_index * tp_size + tp_index) // slices
    pick_in = rows_for(mine).reshape(tp_size * tokens, padded).T
    held = ((tp_index % slices) // halves) * groups + tp_index // slices
    pick_out = rows_for(held)
    piece = jnp.pad(normed.reshape(own, width), ((0, tokens - own), (0, 0)))
    landed = run_experts(
        piece, pick_in, gate_weight, up_weight, down_weight, pick_out, seq_size, tp_size, slices
    )

    logits = jnp.einsum("rtd,de->rte", normed, router_weight, preferred_element_type=jnp.float32)
    own_hot = expert_ids[..., None] == expert_range
    chosen = jnp.sum(jnp.where(own_hot, logits[:, :, None, :], 0.0), axis=3)
    share = 1.0 / (1.0 + jnp.exp(chosen[:, :, ::-1] - chosen))
    own_slots = lax.dynamic_slice_in_dim(all_slots, tp_index * req_dev, req_dev, 0)
    weight = jnp.where(own_slots < capacity, share, 0.0)
    slot_expert = (jnp.arange(tp_size // halves) % (tp_size // (groups * halves))) * groups + (
        jnp.arange(tp_size // halves) // (tp_size // (groups * halves))
    )
    per_slot = jnp.sum(
        jnp.where(expert_ids[..., None] == slot_expert, weight[..., None], 0.0), axis=2
    ).reshape(own, tp_size // halves)
    landed = landed.astype(jnp.float32).reshape(tp_size // halves, halves, tokens, feature_block // halves)
    mixture = jnp.einsum(
        "ia,ahif->ihf", per_slot, landed[:, :, :own], precision=lax.Precision.HIGHEST
    ).reshape(req_dev, steps, feature_block)
    own_residual = lax.dynamic_slice_in_dim(residual, seq_index * feature_block, feature_block, 2)
    layer_out = (own_residual + mixture).astype(jnp.bfloat16)
    return (attn_out, layer_out)


def solution(mesh):

    return jax.shard_map(
        body,
        mesh=mesh,
        in_specs=(
            P("tp", None, None),
            P("tp", None, None),
            P("tp", None, None),
            P("tp", None, None),
            P("tp", "seq", None),
            P("tp", "seq", None),
            P("tp"),
            P(),
            P(),
            P(),
            P("tp", None, None),
            P(("seq", "tp"), None),
            P(("seq", "tp"), None),
            P(("seq", "tp"), None),
        ),
        out_specs=(P("tp", None, "seq"), P("tp", None, "seq")),
        check_vma=False,
    )
```

time: 87.7 us -> 79.2 us (0.903)
  Pallas kernels: 58.9 us -> 54.6 us
  matrix products: 13.8 us -> 11.4 us
  local copies, waits for them, and re-layouts: 8.97 us -> 7.39 us
    pallas_call x3 -> x2, Pallas kernels: 58.9 us -> 54.6 us  [the longest x1 37.8 us: run_experts(): pl.pallas_call(functools.partial(expert_kernel, seq_size, tp_size, slices...]
    dot_general x4 -> x2, matrix products: 5.52 us -> 1.23 us  [the longest x1 1.09 us: body(): jnp.einsum('ia,ahif->ihf', per_slot, landed[:, :, :own], precision=lax.Pr...]
    dot_general x1, matrix products: 1.47 us -> 4.19 us  [body(): jnp.einsum('rqp,rpd->rqd', weights.astype(jnp.bfloat16), value_cache, pre...]
    reshape x5, local copies, waits for them, and re-layouts: 2.59 us -> 0.22 us  [the longest x2 0.1 us: rows_for(): chosen_rows = jnp.any(hit[..., None] & (row_of[..., None] == jnp.arange(p...]
where the time goes in v8:
time: 79.2 us; the launch traced here: 78.9 us
  Pallas kernels  54.6 us (69%)
  matrix products  11.4 us (14%)
  local copies, waits for them, and re-layouts  7.39 us (9%)
  other arithmetic  4.48 us (6%)
  between operations  1.07 us (1%)
    pallas_call x1, Pallas kernels, run_experts(): pl.pallas_call(functools.partial(expert_kernel, seq_size, tp_size, slices...  37.8 us
    pallas_call x1, Pallas kernels, exchange(): pl.pallas_call(functools.partial(exchange_kernel, seq_size, tp_size), out...  16.8 us
    dot_general x1, matrix products, body(): jnp.einsum('rqd,rpd->rqp', q_wide, key_cache, preferred_element_type=jnp....  4.9 us
    dot_general x1, matrix products, body(): jnp.einsum('rqp,rpd->rqd', weights.astype(jnp.bfloat16), value_cache, pre...  4.19 us

profile of v8, /device:TPU:1, one launch (start us, length us, event | category | flops | bytes accessed | tf_op | source)
XLA Modules:
  0.0 78.9 jit_solution(8811936483446877044)
XLA Ops:
  0.7 0.9 %broadcast_compare_fusion = pred[3,1024]{1,0:T(4,128)(4,1)S(1)} fusion(s32[1024]{0:T(1024)S(1)} %iota_add_fusion, s32[3]{0:T(128)} %param.20), kind=kLoop, calls=%fused_computation.46 | loop fusion | flops 3072 | bytes 7180 | tf_op jit(solution)/shard_map/lt | solution.py:336
  1.6 0.8 %bitcast_select_fusion = bf16[3,64,1024]{2,1,0:T(8,128)(2,1)S(1)} fusion(pred[64,1024]{1,0:T(8,128)(4,1)S(1)} %bitcast.44, bf16[3,4,1024]{2,1,0:T(4,128)(2,1)} %param.15), kind=kLoop, calls=%fused_computation.11 | loop fusion | flops 196608 | bytes 483328 | tf_op jit(solution)/shard_map/jit(_where)/select_n | solution.py:327
  2.4 4.9 %fusion.40 = (f32[3,64]{1,0:T(4,128)S(1)}, f32[3,64,1024]{2,1,0:T(8,128)S(1)}) fusion(bf16[3,64,1024]{2,1,0:T(8,128)(2,1)S(1)} %bitcast_select_fusion, bf16[3,1024,1024]{2,1,0:T(8,128)(2,1)} %param.18, pred[3,1024]{1,0:T(4,128)(4,1)S(1)} %broadcast_compare_fusion), kind=kOutput, calls=%fused_computation.87 | convolution fusion | flops 403242816 | bytes 7474944 | tf_op jit(solution)/shard_map/cache_scores/rqd,rpd->rqp/dot_general | solution.py:332
  7.4 0.2 fusion.41
  7.6 0.3 fusion.26
  7.9 4.2 %select_reduce_fusion = f32[3,4,1024]{2,1,0:T(4,128)S(1)} fusion(pred[16,1024]{1,0:T(8,128)(4,1)S(1)} %iota_compare_fusion.2, f32[3,64,1024]{2,1,0:T(8,128)S(1)} %fusion.26, bf16[3,1024,1024]{2,1,0:T(8,128)(2,1)} %param.19, f32[3,64,1024]{2,1,0:T(8,128)S(1)} %get-tuple-element.15, f32[3,64]{1,0:T(4,128)S(1)} %max.12, ...), kind=kOutput, calls=%fused_computation.7 | convolution fusion | flops 403820544 | bytes 7933696 | tf_op jit(solution)/shard_map/cache_values/rqp,rpd->rqd/dot_general | solution.py:350
  12.2 0.3 fusion.4
  12.7 0.7 concatenate.7.stats_ref
  13.4 0.1 copy.36
  13.6 0.6 pad.15.ids_ref
  14.2 16.8 %shard_map.149 = (f32[4,12,1056]{2,1,0:T(8,128)}, s32[32,8,128]{2,1,0:T(8,128)}) custom-call(f32[12,1056]{1,0:T(8,128)} %concatenate.7.stats_ref, s32[8,128]{1,0:T(8,128)} %pad.15.ids_ref), custom_call_target="tpu_custom_call" | custom-call | tf_op jit(solution)/shard_map/pallas_call | solution.py:87
  31.0 0.9 %slice_reduce_fusion = s32[32,24]{1,0:T(8,128)S(1)} fusion(s32[32,8,128]{2,1,0:T(8,128)} %get-tuple-element.5), kind=kLoop, calls=%fused_computation.40 | loop fusion | bytes 6144 | tf_op jit(solution)/shard_map/slice | solution.py:379
  32.0 0.1 eq.116
  32.3 0.1 copy.39
  32.4 0.1 fusion.42
  33.1 0.1 copy.48
  33.3 0.7 copy.49
  34.1 0.1 copy.52
  34.3 0.7 pad_convert_fusion.pick_out_ref
  35.0 1.0 %copy.37 = f32[4,12,1056]{2,0,1:T(4,128)S(1)} copy(f32[4,12,1056]{2,1,0:T(8,128)} %get-tuple-element.4) | data formatting | bytes 405504 | tf_op jit(solution)/shard_map/pallas_call | solution.py:87
  36.1 0.2 broadcast_in_dim.156
  36.3 0.2 reshape.238
  36.5 0.2 fusion.14
  36.7 0.1 reshape.239
  36.8 0.5 multiply_reduce_fusion
  37.5 0.6 pad.16.piece_ref
  38.1 37.8 %shard_map.150 = bf16[32,16,128]{2,1,0:T(8,128)(2,1)} custom-call(bf16[16,1024]{1,0:T(8,128)(2,1)} %pad.16.piece_ref, bf16[64,512]{1,0:T(8,128)(2,1)} %bitcast.43, bf16[352,1024]{1,0:T(8,128)(2,1)} %gate_ref.1, bf16[352,1024]{1,0:T(8,128)(2,1)} %up_ref.1, bf16[352,1024]{1,0:T(8,128)(2,1)} %down_ref.1, bf16[32,16,64]{2,1,0:T(8,128)(2,1)} %pad_convert_fusion.pick_out_ref), custom_call_target="tpu_custom_call" | custom-call | tf_op jit(solution)/shard_map/pallas_call | solution.py:276
  75.8 0.1 fusion.17
  76.0 0.2 select_reduce_fusion.3
  76.6 1.1 %fusion.15 = f32[12,1,2,128]{3,1,2,0:T(1,128)S(1)} fusion(f32[12,16,1,1]{1,2,3,0:T(1,128)S(1)} %bitcast.47, bf16[16,2,12,128]{3,2,1,0:T(8,128)(2,1)} %bitcast.42), kind=kOutput, calls=%fused_computation.24 | convolution fusion | flops 589824 | bytes 111360 | tf_op jit(solution)/shard_map/ia,ahif->ihf/dot_general | solution.py:446
  77.7 0.6 add_convert_fusion
  78.3 0.6 dynamic-slice_convert_fusion
  (55 shorter events, 1.9 us)
Async XLA Ops:
  0.6 36.2 %copy-start = (bf16[1024,1024]{1,0:T(8,128)(2,1)S(1)}, bf16[1024,1024]{1,0:T(8,128)(2,1)}, u32[]{:S(2)}) copy-start(bf16[1024,1024]{1,0:T(8,128)(2,1)} %param.21) | copy-start | bytes 6291460
  0.6 6.7 %copy-start.4 = (bf16[3,4,1024]{2,1,0:T(4,128)(2,1)S(1)}, bf16[3,4,1024]{2,1,0:T(4,128)(2,1)}, u32[]{:S(2)}) copy-start(bf16[3,4,1024]{2,1,0:T(4,128)(2,1)} %param.16) | copy-start | bytes 73732
  0.7 6.9 %copy-start.3 = (bf16[3,4,1024]{2,1,0:T(4,128)(2,1)S(1)}, bf16[3,4,1024]{2,1,0:T(4,128)(2,1)}, u32[]{:S(2)}) copy-start(bf16[3,4,1024]{2,1,0:T(4,128)(2,1)} %param.17) | copy-start | bytes 73732
  7.3 6.1 %copy-start.1 = (s32[3,4,2]{1,2,0:T(2,128)S(1)}, s32[3,4,2]{1,2,0:T(2,128)}, u32[]{:S(2)}) copy-start(s32[3,4,2]{1,2,0:T(2,128)} %param.24) | copy-start | bytes 292
  7.9 28.9 %copy-start.2 = (bf16[3,4,1024]{2,1,0:T(4,128)(2,1)S(1)}, bf16[3,4,1024]{2,1,0:T(4,128)(2,1)}, u32[]{:S(2)}) copy-start(bf16[3,4,1024]{2,1,0:T(4,128)(2,1)} %param.14) | copy-start | bytes 73732
  12.1 25.2 %copy-start.5 = (f32[1024]{0:T(1024)S(1)}, f32[1024]{0:T(1024)}, u32[]{:S(2)}) copy-start(f32[1024]{0:T(1024)} %param.22) | copy-start | bytes 12292
  12.2 63.7 %copy-start.6 = (bf16[1024,16]{0,1:T(8,128)(2,1)S(1)}, bf16[1024,16]{0,1:T(8,128)(2,1)}, u32[]{:S(2)}) copy-start(bf16[1024,16]{0,1:T(8,128)(2,1)} %param.23) | copy-start | bytes 98308

commit v9 on v8

--- a/solution.py
+++ b/solution.py
@@ -14,11 +14,15 @@
 norm_epsilon = 1e-06
 
 
-def exchange_kernel(seq_size, tp_size, stats_ref, ids_ref, stats_out, ids_out, stats_land,
-                    ids_land, send_a, recv_a, send_b, recv_b):
+def exchange_kernel(seq_size, tp_size, scale, query_ref, key_hbm, value_hbm, usable_ref,
+                    fresh_ref, fresh_ok_ref, fresh_value_ref, ids_ref, sums_out, stats_out,
+                    ids_out, keys, values, sums, stats, sums_land, stats_land, ids_land,
+                    load_sem, send_a, recv_a, send_c, recv_c, send_b, recv_b):
     mesh_type = pl.DeviceIdType.MESH
     s = lax.axis_index("seq")
     t = lax.axis_index("tp")
+    req_dev, rows, width = query_ref.shape
+    heads = HEADS
 
     barrier = pltpu.get_barrier_semaphore()
     for u in range(seq_size):
@@ -29,11 +33,58 @@
         @pl.when(t != u)
         def _():
             pl.semaphore_signal(barrier, inc=1, device_id=(s, u), device_id_type=mesh_type)
+
+    loads = []
+    for r in range(req_dev):
+        loads.append(pltpu.make_async_copy(key_hbm.at[r], keys.at[r], load_sem.at[0, r]))
+        loads.append(pltpu.make_async_copy(value_hbm.at[r], values.at[r], load_sem.at[1, r]))
+    for copy in loads:
+        copy.start()
+
+    head_of = lax.broadcasted_iota(jnp.int32, (rows, width), 1) // (width // heads)
+    row_head = lax.broadcasted_iota(jnp.int32, (rows, width), 0) % heads
+    own_head = head_of == row_head
+    lane = lax.broadcasted_iota(jnp.int32, (rows, 128), 1)
+    contract = (((1,), (1,)), ((), ()))
+    for r in range(req_dev):
+        loads[2 * r].wait()
+        scores = lax.dot_general(
+            query_ref[r], keys[r], contract, preferred_element_type=jnp.float32
+        ) * scale
+        usable = usable_ref[r, 0:1, :] > 0.5
+        scores = jnp.where(usable, scores, masked_score)
+        fresh = fresh_ref[r]
+        fresh_ok = fresh_ok_ref[r] > 0.5
+        top = jnp.maximum(
+            jnp.max(scores, axis=1, keepdims=True), jnp.max(fresh, axis=1, keepdims=True)
+        )
+        weights = jnp.where(usable, jnp.exp(scores - top), 0.0)
+        fresh_weights = jnp.where(fresh_ok, jnp.exp(fresh - top), 0.0)
+        total = jnp.sum(weights, axis=1, keepdims=True) + jnp.sum(
+            fresh_weights, axis=1, keepdims=True
+        )
+        loads[2 * r + 1].wait()
+        wide = jnp.dot(
+            weights.astype(jnp.bfloat16), values[r], preferred_element_type=jnp.float32
+        ) + jnp.dot(
+            fresh_weights.astype(jnp.bfloat16), fresh_value_ref[r],
+            preferred_element_type=jnp.float32,
+        )
+        wide = jnp.where(own_head, wide, 0.0)
+        sums[r] = jnp.sum(wide.reshape(rows // heads, heads, width), axis=1)
+        stats[r] = jnp.where(lane < 64, top, total)
+
     pl.semaphore_wait(barrier, seq_size - 1 + tp_size - 1)
 
-    def along_seq(u, slot):
+    def sums_copy(u, slot):
         return pltpu.make_async_remote_copy(
-            stats_ref, stats_land.at[slot], send_a.at[u], recv_a.at[slot],
+            sums, sums_land.at[slot], send_a.at[u], recv_a.at[slot],
+            device_id=(u, t), device_id_type=mesh_type,
+        )
+
+    def stats_copy(u, slot):
+        return pltpu.make_async_remote_copy(
+            stats, stats_land.at[slot], send_c.at[u], recv_c.at[slot],
             device_id=(u, t), device_id_type=mesh_type,
         )
 
@@ -46,11 +97,13 @@
     for u in range(seq_size):
         @pl.when(s == u)
         def _():
-            pltpu.make_async_copy(stats_ref, stats_land.at[u], recv_a.at[u]).start()
+            pltpu.make_async_copy(sums, sums_land.at[u], recv_a.at[u]).start()
+            pltpu.make_async_copy(stats, stats_land.at[u], recv_c.at[u]).start()
 
         @pl.when(s != u)
         def _():
-            along_seq(u, s).start()
+            sums_copy(u, s).start()
+            stats_copy(u, s).start()
     for u in range(tp_size):
         @pl.when(t == u)
         def _():
@@ -63,12 +116,15 @@
     for u in range(seq_size):
         @pl.when(s == u)
         def _():
-            pltpu.make_async_copy(stats_ref, stats_land.at[u], recv_a.at[u]).wait()
+            pltpu.make_async_copy(sums, sums_land.at[u], recv_a.at[u]).wait()
+            pltpu.make_async_copy(stats, stats_land.at[u], recv_c.at[u]).wait()
 
         @pl.when(s != u)
         def _():
-            along_seq(u, s).wait_send()
-            along_seq(u, u).wait_recv()
+            sums_copy(u, s).wait_send()
+            sums_copy(u, u).wait_recv()
+            stats_copy(u, s).wait_send()
+            stats_copy(u, u).wait_recv()
     for u in range(tp_size):
         @pl.when(t == u)
         def _():
@@ -79,29 +135,46 @@
             along_tp(u, t).wait_send()
             along_tp(u, u).wait_recv()
 
+    sums_out[...] = sums_land[...]
     stats_out[...] = stats_land[...]
     ids_out[...] = ids_land[...]
 
 
-def exchange(stats, ids, seq_size, tp_size):
+def exchange(query, key_cache, value_cache, usable, fresh, fresh_ok, fresh_value, ids,
+             seq_size, tp_size, scale):
+    req_dev, rows, width = query.shape
+    steps = rows // HEADS
+    vmem = pl.BlockSpec(memory_space=pltpu.VMEM)
     return pl.pallas_call(
-        functools.partial(exchange_kernel, seq_size, tp_size),
+        functools.partial(exchange_kernel, seq_size, tp_size, scale),
         out_shape=(
-            jax.ShapeDtypeStruct((seq_size,) + stats.shape, stats.dtype),
+            jax.ShapeDtypeStruct((seq_size, req_dev, steps, width), jnp.float32),
+            jax.ShapeDtypeStruct((seq_size, req_dev, rows, 128), jnp.float32),
             jax.ShapeDtypeStruct((tp_size,) + ids.shape, ids.dtype),
         ),
-        in_specs=[pl.BlockSpec(memory_space=pltpu.VMEM)] * 2,
-        out_specs=(pl.BlockSpec(memory_space=pltpu.VMEM), pl.BlockSpec(memory_space=pltpu.VMEM)),
+        in_specs=[vmem, pl.BlockSpec(memory_space=pl.ANY), pl.BlockSpec(memory_space=pl.ANY)]
+        + [vmem] * 5,
+        out_specs=(vmem, vmem, vmem),
         scratch_shapes=[
-            pltpu.VMEM((seq_size,) + stats.shape, stats.dtype),
+            pltpu.VMEM(key_cache.shape, key_cache.dtype),
+            pltpu.VMEM(value_cache.shape, value_cache.dtype),
+            pltpu.VMEM((req_dev, steps, width), jnp.float32),
+            pltpu.VMEM((req_dev, rows, 128), jnp.float32),
+            pltpu.VMEM((seq_size, req_dev, steps, width), jnp.float32),
+            pltpu.VMEM((seq_size, req_dev, rows, 128), jnp.float32),
             pltpu.VMEM((tp_size,) + ids.shape, ids.dtype),
+            pltpu.SemaphoreType.DMA((2, req_dev)),
+            pltpu.SemaphoreType.DMA((seq_size,)),
+            pltpu.SemaphoreType.DMA((seq_size,)),
             pltpu.SemaphoreType.DMA((seq_size,)),
             pltpu.SemaphoreType.DMA((seq_size,)),
             pltpu.SemaphoreType.DMA((tp_size,)),
             pltpu.SemaphoreType.DMA((tp_size,)),
         ],
-        compiler_params=pltpu.CompilerParams(collective_id=0, has_side_effects=True),
-    )(stats, ids)
+        compiler_params=pltpu.CompilerParams(
+            collective_id=0, has_side_effects=True, vmem_limit_bytes=48 * 1024 * 1024
+        ),
+    )(query, key_cache, value_cache, usable, fresh, fresh_ok, fresh_value, ids)
 
 
 def expert_kernel(seq_size, tp_size, slices, piece_ref, pick_in_ref, gate_ref, up_ref,
@@ -327,14 +400,9 @@
     q_wide = jnp.where(head_mask[None, None], new_query[:, :, None, :], 0).reshape(
         req_dev, rows, width
     )
-    with jax.named_scope("cache_scores"):
-        scores = (
-            jnp.einsum("rqd,rpd->rqp", q_wide, key_cache, preferred_element_type=jnp.float32)
-            * scale
-        )
     positions = seq_index * block + jnp.arange(block, dtype=jnp.int32)
-    usable = (positions[None, :] < lengths[:, None])[:, None, :]
-    scores = jnp.where(usable, scores, masked_score)
+    usable = (positions[None, :] < lengths[:, None]).astype(jnp.float32)
+    usable = jnp.broadcast_to(usable[:, None, :], (req_dev, 8, block))
     fresh_scores = (
         jnp.einsum("rqd,rsd->rqs", q_wide, new_key, preferred_element_type=jnp.float32) * scale
     )
@@ -342,44 +410,24 @@
         (jnp.arange(rows)[:, None] // HEADS) >= jnp.arange(steps)[None, :]
     ) & (seq_index == 0)
     fresh_scores = jnp.where(causal, fresh_scores, masked_score)
-    local_max = jnp.maximum(jnp.max(scores, axis=2), jnp.max(fresh_scores, axis=2))
-    weights = jnp.where(usable, jnp.exp(scores - local_max[..., None]), 0.0)
-    fresh_weights = jnp.where(causal, jnp.exp(fresh_scores - local_max[..., None]), 0.0)
-    totals = jnp.sum(weights, axis=2) + jnp.sum(fresh_weights, axis=2)
-    with jax.named_scope("cache_values"):
-        wide_values = jnp.einsum(
-            "rqp,rpd->rqd",
-            weights.astype(jnp.bfloat16),
-            value_cache,
-            preferred_element_type=jnp.float32,
-        )
-    wide_values = wide_values + jnp.einsum(
-        "rqs,rsd->rqd",
-        fresh_weights.astype(jnp.bfloat16),
-        new_value,
-        preferred_element_type=jnp.float32,
-    )
-    partial = jnp.sum(
-        jnp.where(head_mask[None, None], wide_values.reshape(req_dev, steps, HEADS, width), 0.0),
-        axis=2,
-    )
-    stats = jnp.concatenate(
-        [
-            partial,
-            local_max.reshape(req_dev, steps, HEADS),
-            totals.reshape(req_dev, steps, HEADS),
-        ],
-        axis=2,
-    ).reshape(own, -1)
+    fresh_scores = jnp.pad(
+        fresh_scores, ((0, 0), (0, 0), (0, 128 - steps)), constant_values=masked_score
+    )
+    fresh_ok = jnp.pad(
+        jnp.broadcast_to(causal, (req_dev, rows, steps)).astype(jnp.float32),
+        ((0, 0), (0, 0), (0, 128 - steps)),
+    )
+    fresh_value = jnp.pad(new_value, ((0, 0), (0, 128 - steps), (0, 0)))
     id_count = expert_ids.size
     id_rows = 8
     id_piece = jnp.pad(expert_ids.reshape(1, id_count), ((0, id_rows - 1), (0, 128 - id_count)))
-    every, all_id_pieces = exchange(stats, id_piece, seq_size, tp_size)
-    every = every.reshape((seq_size, req_dev, steps, -1))
+    block_sums, every_stats, all_id_pieces = exchange(
+        q_wide, key_cache, value_cache, usable, fresh_scores, fresh_ok, fresh_value, id_piece,
+        seq_size, tp_size, scale,
+    )
     all_ids = all_id_pieces[:, 0, :id_count].reshape(tp_size * req_dev, steps, -1)
-    block_sums = every[..., :width]
-    block_max = every[..., width : width + HEADS]
-    block_totals = every[..., width + HEADS :]
+    block_max = every_stats[..., 0].reshape(seq_size, req_dev, steps, HEADS)
+    block_totals = every_stats[..., 64].reshape(seq_size, req_dev, steps, HEADS)
     overall = jnp.max(block_max, axis=0)
     factors = jnp.exp(block_max - overall[None])
     numer = jnp.sum(jnp.repeat(factors, head_size, axis=-1) * block_sums, axis=0)

time: 79.2 us -> 77 us (0.972)
  matrix products: 11.4 us -> 2.7 us
  Pallas kernels: 54.6 us -> 59.6 us
  other arithmetic: 4.48 us -> 5.36 us
    dot_general x3 -> x0, matrix products: 9.4 us -> none  [the longest x1 4.9 us: body(): jnp.einsum('rqd,rpd->rqp', q_wide, key_cache, preferred_element_type=jnp....]
    pallas_call x1, Pallas kernels: 37.8 us -> 41.1 us  [run_experts(): pl.pallas_call(functools.partial(expert_kernel, seq_size, tp_size, slices...]
    pallas_call x1, Pallas kernels: 16.8 us -> 18.5 us  [exchange(): pl.pallas_call(functools.partial(exchange_kernel, seq_size, tp_size, scal...]
    pad x0 -> x3, local copies, waits for them, and re-layouts: none -> 1.46 us  [the longest x1 0.82 us: body(): fresh_value = jnp.pad(new_value, ((0, 0), (0, 128 - steps), (0, 0)))]
    unnamed x15 -> x17, local copies, waits for them, and re-layouts: 0.14 us -> 1.3 us
    pallas_call x1 -> x0, local copies, waits for them, and re-layouts: 1.05 us -> none  [exchange(): pl.pallas_call(functools.partial(exchange_kernel, seq_size, tp_size), out...]
    lt x1 -> x0, other arithmetic: 0.87 us -> none  [body(): usable = (positions[None, :] < lengths[:, None])[:, None, :]]
    reduce_sum x1, other arithmetic: 0.15 us -> 1 us  [body(): jnp.sum(jnp.repeat(factors, head_size, axis=-1) * block_sums, axis=0)]
where the time goes in v9:
time: 77 us; the launch traced here: 76.7 us
  Pallas kernels  59.6 us (77%)
  local copies, waits for them, and re-layouts  7.97 us (10%)
  other arithmetic  5.36 us (7%)
  matrix products  2.7 us (4%)
  between operations  1.07 us (1%)
    pallas_call x1, Pallas kernels, run_experts(): pl.pallas_call(functools.partial(expert_kernel, seq_size, tp_size, slices...  41.1 us
    pallas_call x1, Pallas kernels, exchange(): pl.pallas_call(functools.partial(exchange_kernel, seq_size, tp_size, scal...  18.5 us

profile of v9, /device:TPU:1, one launch (start us, length us, event | category | flops | bytes accessed | tf_op | source)
XLA Modules:
  0.0 76.7 jit_solution(5882425450423827580)
XLA Ops:
  0.7 0.9 %bitcast_select_fusion.query_ref = bf16[3,64,1024]{2,1,0:T(8,128)(2,1)S(1)} fusion(pred[64,1024]{1,0:T(8,128)(4,1)S(1)} %bitcast.35, bf16[3,4,1024]{2,1,0:T(4,128)(2,1)} %param.15), kind=kLoop, calls=%fused_computation.4 | loop fusion | flops 196608 | bytes 483328 | tf_op jit(solution)/shard_map/jit(_where)/select_n | solution.py:400
  1.7 0.7 compare_convert_fusion
  2.5 1.0 %fusion.2 = f32[3,64,4]{2,1,0:T(8,128)S(1)} fusion(bf16[3,64,1024]{2,1,0:T(8,128)(2,1)S(1)} %bitcast_select_fusion.query_ref, bf16[3,4,1024]{2,1,0:T(4,128)(2,1)} %param.16, pred[64,4]{1,0:T(8,128)(4,1)S(1)} %get-tuple-element.17), kind=kOutput, calls=%fused_computation.3 | convolution fusion | flops 1574400 | bytes 421120 | tf_op jit(solution)/shard_map/rqd,rsd->rqs/dot_general | solution.py:407
  3.5 0.6 pad.28.fresh_ok_ref
  4.2 0.8 %pad.29.fresh_value_ref = bf16[3,128,1024]{2,1,0:T(8,128)(2,1)S(1)} pad(bf16[3,4,1024]{2,1,0:T(4,128)(2,1)} %param.17, bf16[]{:T(256)} %constant.126.clone.1), padding=0_0x0_124x0_0 | pad | bytes 811010 | tf_op jit(solution)/shard_map/jit(_pad)/pad | solution.py:420
  5.0 0.1 copy.42
  5.2 0.9 %copy-done.1 = f32[3,64,128]{2,1,0:T(8,128)S(1)} copy-done((f32[3,64,128]{2,1,0:T(8,128)S(1)}, f32[3,64,128]{2,1,0:T(8,128)}, u32[]{:S(2)}) %copy-start.1) | copy-done | bytes 98328
  6.1 18.5 %shard_map.149 = (f32[4,3,4,1024]{3,2,1,0:T(4,128)S(1)}, f32[4,3,64,128]{3,2,1,0:T(8,128)S(1)}, s32[32,8,128]{2,1,0:T(8,128)S(1)}) custom-call(bf16[3,64,1024]{2,1,0:T(8,128)(2,1)S(1)} %bitcast_select_fusion.query_ref, bf16[3,1024,1024]{2,1,0:T(8,128)(2,1)} %key_hbm.1, bf16[3,1024,1024]{2,1,0:T(8,128)(2,1)} %value_hbm.1, ...), custom_call_target="tpu_custom_call" | custom-call | tf_op jit(solution)/shard_map/pallas_call | solution.py:148
  24.6 0.1 slice_reduce_fusion.1
  24.7 0.3 multiply_reduce_fusion
  25.0 0.2 copy-done.2
  25.3 0.2 copy.43
  25.7 0.2 broadcast_in_dim.123
  25.9 0.2 reshape.215
  26.1 1.0 %multiply_reduce_fusion.1 = f32[3,4,1024]{2,1,0:T(4,128)S(1)} fusion(f32[4,3,4,1024]{3,2,1,0:T(4,128)S(1)} %reshape.215, f32[4,3,4,1024]{3,2,1,0:T(4,128)} %copy-done.2), kind=kLoop, calls=%fused_computation.13 | loop fusion | flops 86016 | bytes 442368 | tf_op jit(solution)/shard_map/reduce_sum | solution.py:433
  27.2 0.1 reshape.216
  27.4 0.5 multiply_reduce_fusion.2
  27.9 0.6 dynamic-slice_convert_fusion
  28.6 0.1 fusion.9
  28.7 0.2 select_reduce_fusion.2
  29.0 1.0 %slice_reduce_fusion = s32[32,24]{1,0:T(8,128)S(1)} fusion(s32[32,8,128]{2,1,0:T(8,128)} %copy-done.3), kind=kLoop, calls=%fused_computation.29 | loop fusion | bytes 6144 | tf_op jit(solution)/shard_map/slice | solution.py:428
  30.0 0.1 eq.110
  30.3 0.1 copy.46
  30.4 0.1 fusion.18
  31.0 0.6 pad.31.piece_ref
  32.0 0.1 copy.55
  32.2 0.7 copy.56
  33.0 0.1 copy.59
  33.2 0.7 pad_convert_fusion.pick_out_ref
  33.8 41.1 %shard_map.150 = bf16[32,16,128]{2,1,0:T(8,128)(2,1)} custom-call(bf16[16,1024]{1,0:T(8,128)(2,1)} %pad.31.piece_ref, bf16[64,512]{1,0:T(8,128)(2,1)} %bitcast.34, bf16[352,1024]{1,0:T(8,128)(2,1)} %gate_ref.1, bf16[352,1024]{1,0:T(8,128)(2,1)} %up_ref.1, bf16[352,1024]{1,0:T(8,128)(2,1)} %down_ref.1, bf16[32,16,64]{2,1,0:T(8,128)(2,1)} %pad_convert_fusion.pick_out_ref), custom_call_target="tpu_custom_call" | custom-call | tf_op jit(solution)/shard_map/pallas_call | solution.py:349
  74.9 1.1 %fusion.7 = f32[12,1,2,128]{3,1,2,0:T(1,128)S(1)} fusion(f32[12,16,1,1]{1,2,3,0:T(1,128)S(1)} %bitcast.38, bf16[16,2,12,128]{3,2,1,0:T(8,128)(2,1)} %bitcast.33), kind=kOutput, calls=%fused_computation.14 | convolution fusion | flops 589824 | bytes 111360 | tf_op jit(solution)/shard_map/ia,ahif->ihf/dot_general | solution.py:494
  76.0 0.6 add_convert_fusion
  (57 shorter events, 2.0 us)
Async XLA Ops:
  0.6 26.7 %copy-start = (bf16[1024,1024]{1,0:T(8,128)(2,1)S(1)}, bf16[1024,1024]{1,0:T(8,128)(2,1)}, u32[]{:S(2)}) copy-start(bf16[1024,1024]{1,0:T(8,128)(2,1)} %param.21) | copy-start | bytes 6291460
  0.6 4.3 %copy-start.4 = (s32[3,4,2]{1,2,0:T(2,128)S(1)}, s32[3,4,2]{1,2,0:T(2,128)}, u32[]{:S(2)}) copy-start(s32[3,4,2]{1,2,0:T(2,128)} %param.24) | copy-start | bytes 292
  5.2 0.9 %copy-start.1 = (f32[3,64,128]{2,1,0:T(8,128)S(1)}, f32[3,64,128]{2,1,0:T(8,128)}, u32[]{:S(2)}) copy-start(f32[3,64,128]{2,1,0:T(8,128)} %pad.28.fresh_ok_ref) | copy-start | bytes 294916
  24.6 0.7 copy-start.2
  24.6 0.7 copy-start.3
  24.6 2.8 %copy-start.5 = (bf16[3,4,1024]{2,1,0:T(4,128)(2,1)S(1)}, bf16[3,4,1024]{2,1,0:T(4,128)(2,1)}, u32[]{:S(2)}) copy-start(bf16[3,4,1024]{2,1,0:T(4,128)(2,1)} %param.14) | copy-start | bytes 73732
  25.5 3.0 %copy-start.6 = (f32[1024]{0:T(1024)S(1)}, f32[1024]{0:T(1024)}, u32[]{:S(2)}) copy-start(f32[1024]{0:T(1024)} %param.22) | copy-start | bytes 12292
  25.7 2.9 %copy-start.7 = (bf16[1024,16]{0,1:T(8,128)(2,1)S(1)}, bf16[1024,16]{0,1:T(8,128)(2,1)}, u32[]{:S(2)}) copy-start(bf16[1024,16]{0,1:T(8,128)(2,1)} %param.23) | copy-start | bytes 98308

commit v10 on v9

--- a/solution.py
+++ b/solution.py
@@ -15,9 +15,9 @@
 
 
 def exchange_kernel(seq_size, tp_size, scale, query_ref, key_hbm, value_hbm, usable_ref,
-                    fresh_ref, fresh_ok_ref, fresh_value_ref, ids_ref, sums_out, stats_out,
-                    ids_out, keys, values, sums, stats, sums_land, stats_land, ids_land,
-                    load_sem, send_a, recv_a, send_c, recv_c, send_b, recv_b):
+                    fresh_ref, fresh_ok_ref, fresh_value_ref, ids_ref, sums_out,
+                    ids_out, keys, values, sums, sums_land, ids_land,
+                    load_sem, send_a, recv_a, send_b, recv_b):
     mesh_type = pl.DeviceIdType.MESH
     s = lax.axis_index("seq")
     t = lax.axis_index("tp")
@@ -44,7 +44,10 @@
     head_of = lax.broadcasted_iota(jnp.int32, (rows, width), 1) // (width // heads)
     row_head = lax.broadcasted_iota(jnp.int32, (rows, width), 0) % heads
     own_head = head_of == row_head
-    lane = lax.broadcasted_iota(jnp.int32, (rows, 128), 1)
+    spread = (
+        lax.broadcasted_iota(jnp.int32, (rows // heads, rows), 1) // heads
+        == lax.broadcasted_iota(jnp.int32, (rows // heads, rows), 0)
+    ).astype(jnp.float32)
     contract = (((1,), (1,)), ((), ()))
     for r in range(req_dev):
         loads[2 * r].wait()
@@ -71,8 +74,17 @@
             preferred_element_type=jnp.float32,
         )
         wide = jnp.where(own_head, wide, 0.0)
-        sums[r] = jnp.sum(wide.reshape(rows // heads, heads, width), axis=1)
-        stats[r] = jnp.where(lane < 64, top, total)
+        steps = rows // heads
+        sums[r, 0:steps, :] = jnp.sum(wide.reshape(steps, heads, width), axis=1)
+        sums[r, steps : 2 * steps, :] = jnp.dot(
+            spread, jnp.where(own_head, top, 0.0),
+            precision=lax.Precision.HIGHEST, preferred_element_type=jnp.float32,
+        )
+        sums[r, 2 * steps : 3 * steps, :] = jnp.dot(
+            spread, jnp.where(own_head, total, 0.0),
+            precision=lax.Precision.HIGHEST, preferred_element_type=jnp.float32,
+        )
+        sums[r, 3 * steps :, :] = jnp.zeros((sums.shape[1] - 3 * steps, width), jnp.float32)
 
     pl.semaphore_wait(barrier, seq_size - 1 + tp_size - 1)
 
@@ -82,12 +94,6 @@
             device_id=(u, t), device_id_type=mesh_type,
         )
 
-    def stats_copy(u, slot):
-        return pltpu.make_async_remote_copy(
-            stats, stats_land.at[slot], send_c.at[u], recv_c.at[slot],
-            device_id=(u, t), device_id_type=mesh_type,
-        )
-
     def along_tp(u, slot):
         return pltpu.make_async_remote_copy(
             ids_ref, ids_land.at[slot], send_b.at[u], recv_b.at[slot],
@@ -98,12 +104,10 @@
         @pl.when(s == u)
         def _():
             pltpu.make_async_copy(sums, sums_land.at[u], recv_a.at[u]).start()
-            pltpu.make_async_copy(stats, stats_land.at[u], recv_c.at[u]).start()
 
         @pl.when(s != u)
         def _():
             sums_copy(u, s).start()
-            stats_copy(u, s).start()
     for u in range(tp_size):
         @pl.when(t == u)
         def _():
@@ -117,14 +121,11 @@
         @pl.when(s == u)
         def _():
             pltpu.make_async_copy(sums, sums_land.at[u], recv_a.at[u]).wait()
-            pltpu.make_async_copy(stats, stats_land.at[u], recv_c.at[u]).wait()
 
         @pl.when(s != u)
         def _():
             sums_copy(u, s).wait_send()
             sums_copy(u, u).wait_recv()
-            stats_copy(u, s).wait_send()
-            stats_copy(u, u).wait_recv()
     for u in range(tp_size):
         @pl.when(t == u)
         def _():
@@ -136,7 +137,6 @@
             along_tp(u, u).wait_recv()
 
     sums_out[...] = sums_land[...]
-    stats_out[...] = stats_land[...]
     ids_out[...] = ids_land[...]
 
 
@@ -148,24 +148,19 @@
     return pl.pallas_call(
         functools.partial(exchange_kernel, seq_size, tp_size, scale),
         out_shape=(
-            jax.ShapeDtypeStruct((seq_size, req_dev, steps, width), jnp.float32),
-            jax.ShapeDtypeStruct((seq_size, req_dev, rows, 128), jnp.float32),
+            jax.ShapeDtypeStruct((seq_size, req_dev, 4 * steps, width), jnp.float32),
             jax.ShapeDtypeStruct((tp_size,) + ids.shape, ids.dtype),
         ),
         in_specs=[vmem, pl.BlockSpec(memory_space=pl.ANY), pl.BlockSpec(memory_space=pl.ANY)]
         + [vmem] * 5,
-        out_specs=(vmem, vmem, vmem),
+        out_specs=(vmem, vmem),
         scratch_shapes=[
             pltpu.VMEM(key_cache.shape, key_cache.dtype),
             pltpu.VMEM(value_cache.shape, value_cache.dtype),
-            pltpu.VMEM((req_dev, steps, width), jnp.float32),
-            pltpu.VMEM((req_dev, rows, 128), jnp.float32),
-            pltpu.VMEM((seq_size, req_dev, steps, width), jnp.float32),
-            pltpu.VMEM((seq_size, req_dev, rows, 128), jnp.float32),
+            pltpu.VMEM((req_dev, 4 * steps, width), jnp.float32),
+            pltpu.VMEM((seq_size, req_dev, 4 * steps, width), jnp.float32),
             pltpu.VMEM((tp_size,) + ids.shape, ids.dtype),
             pltpu.SemaphoreType.DMA((2, req_dev)),
-            pltpu.SemaphoreType.DMA((seq_size,)),
-            pltpu.SemaphoreType.DMA((seq_size,)),
             pltpu.SemaphoreType.DMA((seq_size,)),
             pltpu.SemaphoreType.DMA((seq_size,)),
             pltpu.SemaphoreType.DMA((tp_size,)),
@@ -177,8 +172,9 @@
     )(query, key_cache, value_cache, usable, fresh, fresh_ok, fresh_value, ids)
 
 
-def expert_kernel(seq_size, tp_size, slices, piece_ref, pick_in_ref, gate_ref, up_ref,
-                  down_ref, pick_out_ref, out_ref, everyone, part, recv, middle, outgoing,
+def expert_kernel(seq_size, tp_size, slices, sums_ref, hidden_ref, out_weight_ref, gain_ref,
+                  pick_in_ref, gate_ref, up_ref, down_ref, pick_out_ref, out_ref, attn_ref,
+                  normed_ref, piece_ref, context, everyone, part, recv, middle, outgoing,
                   landing, send0, recv0, send1, recv1, send3, recv3):
     mesh_type = pl.DeviceIdType.MESH
     s = lax.axis_index("seq")
@@ -210,6 +206,35 @@
             pl.semaphore_signal(
                 barrier, inc=1, device_id=(src_seq, g * slices + k), device_id_type=mesh_type
             )
+    req_dev = sums_ref.shape[1]
+    steps = sums_ref.shape[2] // 4
+    context[...] = jnp.zeros_like(context)
+    for r in range(req_dev):
+        block_sums = [sums_ref[b, r, 0:steps, :] for b in range(seq_size)]
+        block_max = [sums_ref[b, r, steps : 2 * steps, :] for b in range(seq_size)]
+        block_totals = [sums_ref[b, r, 2 * steps : 3 * steps, :] for b in range(seq_size)]
+        overall = block_max[0]
+        for b in range(1, seq_size):
+            overall = jnp.maximum(overall, block_max[b])
+        numer = jnp.zeros_like(overall)
+        denom = jnp.zeros_like(overall)
+        for b in range(seq_size):
+            factor = jnp.exp(block_max[b] - overall)
+            numer = numer + factor * block_sums[b]
+            denom = denom + factor * block_totals[b]
+        context[r * steps : (r + 1) * steps, :] = numer / denom
+    attention = jnp.dot(
+        context[...].astype(jnp.bfloat16), out_weight_ref[...], preferred_element_type=jnp.float32
+    )
+    attn_ref[...] = attention
+    residual = hidden_ref[...] + attention
+    mean_square = jnp.mean(residual * residual, axis=1, keepdims=True)
+    normed = (residual * lax.rsqrt(mean_square + norm_epsilon) * gain_ref[...]).astype(
+        jnp.bfloat16
+    )
+    piece_ref[...] = normed
+    normed_ref[...] = normed
+
     far = (seq_size - 1) * halves
     near = tp_size - 1 + far
 
@@ -341,17 +366,24 @@
     out_ref[...] = landing[...]
 
 
-def run_experts(piece, pick_in, gate_weight, up_weight, down_weight, pick_out, seq_size,
-                tp_size, slices):
-    tokens, width = piece.shape
+def run_experts(sums, hidden, out_weight, gain, pick_in, gate_weight, up_weight, down_weight,
+                pick_out, seq_size, tp_size, slices):
+    tokens, width = hidden.shape
     rows = pick_in.shape[0]
     chunk = width // slices
+    vmem = pl.BlockSpec(memory_space=pltpu.VMEM)
     return pl.pallas_call(
         functools.partial(expert_kernel, seq_size, tp_size, slices),
-        out_shape=jax.ShapeDtypeStruct((tp_size, tokens, chunk), jnp.bfloat16),
-        in_specs=[pl.BlockSpec(memory_space=pltpu.VMEM)] * 6,
-        out_specs=pl.BlockSpec(memory_space=pltpu.VMEM),
+        out_shape=(
+            jax.ShapeDtypeStruct((tp_size, tokens, chunk), jnp.bfloat16),
+            jax.ShapeDtypeStruct((tokens, width), jnp.float32),
+            jax.ShapeDtypeStruct((tokens, width), jnp.bfloat16),
+        ),
+        in_specs=[vmem] * 9,
+        out_specs=(vmem, vmem, vmem),
         scratch_shapes=[
+            pltpu.VMEM((tokens, width), jnp.bfloat16),
+            pltpu.VMEM((tokens, width), jnp.float32),
             pltpu.VMEM((tp_size, tokens, width), jnp.bfloat16),
             pltpu.VMEM((rows, width), jnp.float32),
             pltpu.VMEM((slices, rows, chunk), jnp.float32),
@@ -365,8 +397,10 @@
             pltpu.SemaphoreType.DMA((tp_size,)),
             pltpu.SemaphoreType.DMA((tp_size,)),
         ],
-        compiler_params=pltpu.CompilerParams(collective_id=1, has_side_effects=True),
-    )(piece, pick_in, gate_weight, up_weight, down_weight, pick_out)
+        compiler_params=pltpu.CompilerParams(
+            collective_id=1, has_side_effects=True, vmem_limit_bytes=48 * 1024 * 1024
+        ),
+    )(sums, hidden, out_weight, gain, pick_in, gate_weight, up_weight, down_weight, pick_out)
 
 
 def body(
@@ -421,30 +455,12 @@
     id_count = expert_ids.size
     id_rows = 8
     id_piece = jnp.pad(expert_ids.reshape(1, id_count), ((0, id_rows - 1), (0, 128 - id_count)))
-    block_sums, every_stats, all_id_pieces = exchange(
+    block_sums, all_id_pieces = exchange(
         q_wide, key_cache, value_cache, usable, fresh_scores, fresh_ok, fresh_value, id_piece,
         seq_size, tp_size, scale,
     )
     all_ids = all_id_pieces[:, 0, :id_count].reshape(tp_size * req_dev, steps, -1)
-    block_max = every_stats[..., 0].reshape(seq_size, req_dev, steps, HEADS)
-    block_totals = every_stats[..., 64].reshape(seq_size, req_dev, steps, HEADS)
-    overall = jnp.max(block_max, axis=0)
-    factors = jnp.exp(block_max - overall[None])
-    numer = jnp.sum(jnp.repeat(factors, head_size, axis=-1) * block_sums, axis=0)
-    denom = jnp.sum(factors * block_totals, axis=0)
-    context = (numer / jnp.repeat(denom, head_size, axis=-1)).astype(jnp.bfloat16)
-    attention = jnp.einsum("rtd,de->rte", context, out_weight, preferred_element_type=jnp.float32)
     feature_block = width // seq_size
-    attn_out = lax.dynamic_slice_in_dim(
-        attention, seq_index * feature_block, feature_block, 2
-    ).astype(jnp.bfloat16)
-    residual = hidden_in.astype(jnp.float32) + attention
-    normed = (
-        residual
-        * lax.rsqrt(jnp.mean(residual * residual, axis=-1, keepdims=True) + norm_epsilon)
-        * norm_gain
-    ).astype(jnp.bfloat16)
-
     experts = router_weight.shape[1]
     topk = expert_ids.shape[2]
     requests = req_dev * tp_size
@@ -473,10 +489,19 @@
     pick_in = rows_for(mine).reshape(tp_size * tokens, padded).T
     held = ((tp_index % slices) // halves) * groups + tp_index // slices
     pick_out = rows_for(held)
-    piece = jnp.pad(normed.reshape(own, width), ((0, tokens - own), (0, 0)))
-    landed = run_experts(
-        piece, pick_in, gate_weight, up_weight, down_weight, pick_out, seq_size, tp_size, slices
-    )
+    hidden = jnp.pad(
+        hidden_in.astype(jnp.float32).reshape(own, width), ((0, tokens - own), (0, 0))
+    )
+    landed, attention, normed = run_experts(
+        block_sums, hidden, out_weight, norm_gain.reshape(1, width), pick_in, gate_weight,
+        up_weight, down_weight, pick_out, seq_size, tp_size, slices,
+    )
+    attention = attention[:own].reshape(req_dev, steps, width)
+    normed = normed[:own].reshape(req_dev, steps, width)
+    attn_out = lax.dynamic_slice_in_dim(
+        attention, seq_index * feature_block, feature_block, 2
+    ).astype(jnp.bfloat16)
+    residual = hidden_in.astype(jnp.float32) + attention
 
     logits = jnp.einsum("rtd,de->rte", normed, router_weight, preferred_element_type=jnp.float32)
     own_hot = expert_ids[..., None] == expert_range

time: 77 us -> 78.3 us (1.017)
  local copies, waits for them, and re-layouts: 7.97 us -> 12.2 us
  other arithmetic: 5.36 us -> 3.09 us
  matrix products: 2.7 us -> 1.3 us
    unnamed x17 -> x25, local copies, waits for them, and re-layouts: 1.3 us -> 7.67 us
    pallas_call x1, Pallas kernels: 18.5 us -> 20.7 us  [exchange(): pl.pallas_call(functools.partial(exchange_kernel, seq_size, tp_size, scal...]
    pallas_call x1, Pallas kernels: 41.1 us -> 39.5 us  [run_experts(): pl.pallas_call(functools.partial(expert_kernel, seq_size, tp_size, slices...]
    reduce_sum x2 -> x0, other arithmetic: 1.28 us -> none  [the longest x1 1 us: body(): jnp.sum(jnp.repeat(factors, head_size, axis=-1) * block_sums, axis=0)]
    dot_general x1, matrix products: 1.09 us -> 0.19 us  [body(): jnp.einsum('ia,ahif->ihf', per_slot, landed[:, :, :own], precision=lax.Pr...]
where the time goes in v10:
time: 78.3 us; the launch traced here: 77.8 us
  Pallas kernels  60.2 us (77%)
  local copies, waits for them, and re-layouts  12.2 us (16%)
  other arithmetic  3.09 us (4%)
  matrix products  1.3 us (2%)
  between operations  1.03 us (1%)
    pallas_call x1, Pallas kernels, run_experts(): pl.pallas_call(functools.partial(expert_kernel, seq_size, tp_size, slices...  39.5 us
    pallas_call x1, Pallas kernels, exchange(): pl.pallas_call(functools.partial(exchange_kernel, seq_size, tp_size, scal...  20.7 us
    unnamed x25, local copies, waits for them, and re-layouts  7.67 us

profile of v10, /device:TPU:1, one launch (start us, length us, event | category | flops | bytes accessed | tf_op | source)
XLA Modules:
  0.0 77.8 jit_solution(16330258177297748763)
XLA Ops:
  0.7 0.8 %bitcast_select_fusion.query_ref = bf16[3,64,1024]{2,1,0:T(8,128)(2,1)S(1)} fusion(pred[64,1024]{1,0:T(8,128)(4,1)S(1)} %bitcast.30, bf16[3,4,1024]{2,1,0:T(4,128)(2,1)} %param.15), kind=kLoop, calls=%fused_computation.2 | loop fusion | flops 196608 | bytes 483328 | tf_op jit(solution)/shard_map/jit(_where)/select_n | solution.py:434
  1.5 0.7 compare_convert_fusion
  2.4 1.0 %fusion = f32[3,64,4]{2,1,0:T(8,128)S(1)} fusion(bf16[3,64,1024]{2,1,0:T(8,128)(2,1)S(1)} %bitcast_select_fusion.query_ref, bf16[3,4,1024]{2,1,0:T(4,128)(2,1)} %param.16, pred[64,4]{1,0:T(8,128)(4,1)S(1)} %get-tuple-element.17), kind=kOutput, calls=%fused_computation.1 | convolution fusion | flops 1574400 | bytes 421120 | tf_op jit(solution)/shard_map/rqd,rsd->rqs/dot_general | solution.py:441
  3.4 0.6 pad.28.fresh_ok_ref
  4.0 0.8 %pad.29.fresh_value_ref = bf16[3,128,1024]{2,1,0:T(8,128)(2,1)S(1)} pad(bf16[3,4,1024]{2,1,0:T(4,128)(2,1)} %param.17, bf16[]{:T(256)} %constant.122.clone.1), padding=0_0x0_124x0_0 | pad | bytes 811010 | tf_op jit(solution)/shard_map/jit(_pad)/pad | solution.py:454
  4.8 0.8 %copy.38 = s32[3,4,2]{2,1,0:T(4,128)S(1)} copy(s32[3,4,2]{1,2,0:T(2,128)} %param.24) | data formatting | bytes 192 | tf_op args[10]
  5.7 0.9 %copy-done.7 = f32[3,64,128]{2,1,0:T(8,128)S(1)} copy-done((f32[3,64,128]{2,1,0:T(8,128)S(1)}, f32[3,64,128]{2,1,0:T(8,128)}, u32[]{:S(2)}) %copy-start.7) | copy-done | bytes 98328
  6.6 20.7 %shard_map.149 = (f32[4,3,16,1024]{3,2,1,0:T(8,128)S(1)}, s32[32,8,128]{2,1,0:T(8,128)S(1)}) custom-call(bf16[3,64,1024]{2,1,0:T(8,128)(2,1)S(1)} %bitcast_select_fusion.query_ref, bf16[3,1024,1024]{2,1,0:T(8,128)(2,1)} %key_hbm.1, bf16[3,1024,1024]{2,1,0:T(8,128)(2,1)} %value_hbm.1, f32[3,8,1024]{2,1,0:T(8,128)S(1)} %broadcast_in_dim.110.usable_ref, ...), custom_call_target="tpu_custom_call" | custom-call | tf_op jit(solution)/shard_map/pallas_call | solution.py:148
  27.3 0.9 %copy-done.2 = f32[4,3,16,1024]{3,2,1,0:T(8,128)} copy-done((f32[4,3,16,1024]{3,2,1,0:T(8,128)}, f32[4,3,16,1024]{3,2,1,0:T(8,128)S(1)}, u32[]{:S(2)}) %copy-start.2) | copy-done | bytes 786456
  28.2 0.6 copy-done.9
  28.9 0.9 %slice_reduce_fusion = s32[32,24]{1,0:T(8,128)S(1)} fusion(s32[32,8,128]{2,1,0:T(8,128)} %copy-done.9), kind=kLoop, calls=%fused_computation.20 | loop fusion | bytes 6144 | tf_op jit(solution)/shard_map/slice | solution.py:462
  29.8 0.1 reshape_squeeze.3
  30.0 0.1 copy.40
  30.1 0.1 copy.41
  30.2 0.1 fusion.18
  30.6 0.1 copy.39
  30.8 0.1 fusion.4
  30.9 0.1 copy.46
  31.2 0.1 copy.47
  31.3 0.1 copy.50
  31.6 1.1 %copy-done.3 = f32[4,3,16,1024]{3,2,1,0:T(8,128)S(1)} copy-done((f32[4,3,16,1024]{3,2,1,0:T(8,128)S(1)}, f32[4,3,16,1024]{3,2,1,0:T(8,128)}, u32[]{:S(2)}) %copy-start.3) | copy-done | bytes 786456
  32.7 1.1 %copy-done.4 = bf16[352,1024]{1,0:T(8,128)(2,1)S(1)} copy-done((bf16[352,1024]{1,0:T(8,128)(2,1)S(1)}, bf16[352,1024]{1,0:T(8,128)(2,1)}, u32[]{:S(2)}) %copy-start.4) | copy-done | bytes 720920
  33.8 1.1 %copy-done.5 = bf16[352,1024]{1,0:T(8,128)(2,1)S(1)} copy-done((bf16[352,1024]{1,0:T(8,128)(2,1)S(1)}, bf16[352,1024]{1,0:T(8,128)(2,1)}, u32[]{:S(2)}) %copy-start.5) | copy-done | bytes 720920
  34.9 1.1 %copy-done.6 = bf16[352,1024]{1,0:T(8,128)(2,1)S(1)} copy-done((bf16[352,1024]{1,0:T(8,128)(2,1)S(1)}, bf16[352,1024]{1,0:T(8,128)(2,1)}, u32[]{:S(2)}) %copy-start.6) | copy-done | bytes 720920
  36.0 39.5 %shard_map.150 = (bf16[32,16,128]{2,1,0:T(8,128)(2,1)S(1)}, f32[16,1024]{1,0:T(8,128)S(1)}, bf16[16,1024]{1,0:T(8,128)(2,1)S(1)}) custom-call(f32[4,3,16,1024]{3,2,1,0:T(8,128)S(1)} %copy-done.3, f32[16,1024]{1,0:T(8,128)S(1)} %pad.31.hidden_ref, bf16[1024,1024]{1,0:T(8,128)(2,1)S(1)} %copy-done.1, f32[1,1024]{1,0:T(1,128)S(1)} %bitcast.28, ...), custom_call_target="tpu_custom_call" | custom-call | tf_op jit(solution)/shard_map/pallas_call | solution.py:375
  75.6 0.6 dynamic-slice_convert_fusion
  76.2 0.1 fusion.7
  76.3 0.2 select_reduce_fusion.2
  76.5 0.1 copy.51
  76.7 0.1 copy.53
  76.9 0.2 fusion.5
  77.2 0.6 fusion.11
  (52 shorter events, 1.1 us)
Async XLA Ops:
  0.6 75.6 %copy-start = (bf16[1024,16]{0,1:T(8,128)(2,1)S(1)}, bf16[1024,16]{0,1:T(8,128)(2,1)}, u32[]{:S(2)}) copy-start(bf16[1024,16]{0,1:T(8,128)(2,1)} %param.23) | copy-start | bytes 98308
  5.7 0.9 %copy-start.7 = (f32[3,64,128]{2,1,0:T(8,128)S(1)}, f32[3,64,128]{2,1,0:T(8,128)}, u32[]{:S(2)}) copy-start(f32[3,64,128]{2,1,0:T(8,128)} %pad.28.fresh_ok_ref) | copy-start | bytes 294916
  6.6 22.2 %copy-start.10 = (bf16[3,4,1024]{2,1,0:T(4,128)(2,1)S(1)}, bf16[3,4,1024]{2,1,0:T(4,128)(2,1)}, u32[]{:S(2)}) copy-start(bf16[3,4,1024]{2,1,0:T(4,128)(2,1)} %param.14) | copy-start | bytes 73732
  6.6 24.9 %copy-start.1 = (bf16[1024,1024]{1,0:T(8,128)(2,1)S(1)}, bf16[1024,1024]{1,0:T(8,128)(2,1)}, u32[]{:S(2)}) copy-start(bf16[1024,1024]{1,0:T(8,128)(2,1)} %out_weight_ref.1) | copy-start | bytes 6291460
  6.6 24.9 %copy-start.8 = (f32[1024]{0:T(1024)S(1)}, f32[1024]{0:T(1024)}, u32[]{:S(2)}) copy-start(f32[1024]{0:T(1024)} %param.22) | copy-start | bytes 12292
  27.3 0.9 %copy-start.2 = (f32[4,3,16,1024]{3,2,1,0:T(8,128)}, f32[4,3,16,1024]{3,2,1,0:T(8,128)S(1)}, u32[]{:S(2)}) copy-start(f32[4,3,16,1024]{3,2,1,0:T(8,128)S(1)} %get-tuple-element.7.sums_ref) | copy-start | bytes 2359300
  28.2 0.6 copy-start.9
  28.8 47.5 %copy-start.11 = (s32[3,4,2]{1,2,0:T(2,128)S(1)}, s32[3,4,2]{1,2,0:T(2,128)}, u32[]{:S(2)}) copy-start(s32[3,4,2]{1,2,0:T(2,128)} %param.24) | copy-start | bytes 292
  31.5 1.1 %copy-start.3 = (f32[4,3,16,1024]{3,2,1,0:T(8,128)S(1)}, f32[4,3,16,1024]{3,2,1,0:T(8,128)}, u32[]{:S(2)}) copy-start(f32[4,3,16,1024]{3,2,1,0:T(8,128)} %copy-done.2) | copy-start | bytes 2359300
  32.7 1.1 %copy-start.4 = (bf16[352,1024]{1,0:T(8,128)(2,1)S(1)}, bf16[352,1024]{1,0:T(8,128)(2,1)}, u32[]{:S(2)}) copy-start(bf16[352,1024]{1,0:T(8,128)(2,1)} %gate_ref.1) | copy-start | bytes 2162692
  33.8 1.1 %copy-start.5 = (bf16[352,1024]{1,0:T(8,128)(2,1)S(1)}, bf16[352,1024]{1,0:T(8,128)(2,1)}, u32[]{:S(2)}) copy-start(bf16[352,1024]{1,0:T(8,128)(2,1)} %up_ref.1) | copy-start | bytes 2162692
  34.9 1.1 %copy-start.6 = (bf16[352,1024]{1,0:T(8,128)(2,1)S(1)}, bf16[352,1024]{1,0:T(8,128)(2,1)}, u32[]{:S(2)}) copy-start(bf16[352,1024]{1,0:T(8,128)(2,1)} %down_ref.1) | copy-start | bytes 2162692

commit v11 on v10

--- a/solution.py
+++ b/solution.py
@@ -167,15 +167,16 @@
             pltpu.SemaphoreType.DMA((tp_size,)),
         ],
         compiler_params=pltpu.CompilerParams(
-            collective_id=0, has_side_effects=True, vmem_limit_bytes=48 * 1024 * 1024
+            collective_id=0, has_side_effects=True
         ),
     )(query, key_cache, value_cache, usable, fresh, fresh_ok, fresh_value, ids)
 
 
-def expert_kernel(seq_size, tp_size, slices, sums_ref, hidden_ref, out_weight_ref, gain_ref,
-                  pick_in_ref, gate_ref, up_ref, down_ref, pick_out_ref, out_ref, attn_ref,
-                  normed_ref, piece_ref, context, everyone, part, recv, middle, outgoing,
-                  landing, send0, recv0, send1, recv1, send3, recv3):
+def expert_kernel(seq_size, tp_size, slices, sums_ref, hidden_ref, out_weight_hbm, gain_ref,
+                  pick_in_ref, gate_hbm, up_hbm, down_hbm, pick_out_ref, out_ref, attn_ref,
+                  normed_ref, out_weight_ref, gate_ref, up_ref, down_ref, load_sem, piece_ref,
+                  context, everyone, part, recv, middle, outgoing, landing, send0, recv0,
+                  send1, recv1, send3, recv3):
     mesh_type = pl.DeviceIdType.MESH
     s = lax.axis_index("seq")
     t = lax.axis_index("tp")
@@ -206,6 +207,16 @@
             pl.semaphore_signal(
                 barrier, inc=1, device_id=(src_seq, g * slices + k), device_id_type=mesh_type
             )
+    loads = [
+        pltpu.make_async_copy(src_hbm, dst, load_sem.at[n])
+        for n, (src_hbm, dst) in enumerate(
+            [(out_weight_hbm, out_weight_ref), (gate_hbm, gate_ref), (up_hbm, up_ref),
+             (down_hbm, down_ref)]
+        )
+    ]
+    for copy in loads:
+        copy.start()
+
     req_dev = sums_ref.shape[1]
     steps = sums_ref.shape[2] // 4
     context[...] = jnp.zeros_like(context)
@@ -223,6 +234,7 @@
             numer = numer + factor * block_sums[b]
             denom = denom + factor * block_totals[b]
         context[r * steps : (r + 1) * steps, :] = numer / denom
+    loads[0].wait()
     attention = jnp.dot(
         context[...].astype(jnp.bfloat16), out_weight_ref[...], preferred_element_type=jnp.float32
     )
@@ -271,6 +283,8 @@
             gather(u, t).wait_send()
             gather(u, u).wait_recv()
 
+    for copy in loads[1:]:
+        copy.wait()
     rows_in = everyone[...].reshape(-1, everyone.shape[2])
     buffer = jnp.dot(pick_in_ref[...], rows_in, preferred_element_type=jnp.float32).astype(
         jnp.bfloat16
@@ -372,6 +386,7 @@
     rows = pick_in.shape[0]
     chunk = width // slices
     vmem = pl.BlockSpec(memory_space=pltpu.VMEM)
+    hbm = pl.BlockSpec(memory_space=pl.ANY)
     return pl.pallas_call(
         functools.partial(expert_kernel, seq_size, tp_size, slices),
         out_shape=(
@@ -379,9 +394,14 @@
             jax.ShapeDtypeStruct((tokens, width), jnp.float32),
             jax.ShapeDtypeStruct((tokens, width), jnp.bfloat16),
         ),
-        in_specs=[vmem] * 9,
+        in_specs=[vmem, vmem, hbm, vmem, vmem, hbm, hbm, hbm, vmem],
         out_specs=(vmem, vmem, vmem),
         scratch_shapes=[
+            pltpu.VMEM(out_weight.shape, out_weight.dtype),
+            pltpu.VMEM(gate_weight.shape, gate_weight.dtype),
+            pltpu.VMEM(up_weight.shape, up_weight.dtype),
+            pltpu.VMEM(down_weight.shape, down_weight.dtype),
+            pltpu.SemaphoreType.DMA((4,)),
             pltpu.VMEM((tokens, width), jnp.bfloat16),
             pltpu.VMEM((tokens, width), jnp.float32),
             pltpu.VMEM((tp_size, tokens, width), jnp.bfloat16),
@@ -398,7 +418,7 @@
             pltpu.SemaphoreType.DMA((tp_size,)),
         ],
         compiler_params=pltpu.CompilerParams(
-            collective_id=1, has_side_effects=True, vmem_limit_bytes=48 * 1024 * 1024
+            collective_id=1, has_side_effects=True
         ),
     )(sums, hidden, out_weight, gain, pick_in, gate_weight, up_weight, down_weight, pick_out)
 

time: 78.3 us -> 82.5 us (1.054)
  Pallas kernels: 60.2 us -> 64.2 us
  local copies, waits for them, and re-layouts: 12.2 us -> 10.9 us
  matrix products: 1.3 us -> 2.2 us
    unnamed x25 -> x9, local copies, waits for them, and re-layouts: 7.67 us -> 0.81 us
    pallas_call x1, Pallas kernels: 20.7 us -> 22.8 us  [exchange(): pl.pallas_call(functools.partial(exchange_kernel, seq_size, tp_size, scal...]
    pallas_call x1, Pallas kernels: 39.5 us -> 41.3 us  [run_experts(): pl.pallas_call(functools.partial(expert_kernel, seq_size, tp_size, slices...]
    pad x1, local copies, waits for them, and re-layouts: 0.82 us -> 1.73 us  [body(): fresh_value = jnp.pad(new_value, ((0, 0), (0, 128 - steps), (0, 0)))]
    dot_general x1, matrix products: 0.19 us -> 1.09 us  [body(): jnp.einsum('ia,ahif->ihf', per_slot, landed[:, :, :own], precision=lax.Pr...]
    reshape x1, local copies, waits for them, and re-layouts: 0.02 us -> 0.86 us  [body(): attention = attention[:own].reshape(req_dev, steps, width)]
where the time goes in v11:
time: 82.5 us; the launch traced here: 82 us
  Pallas kernels  64.2 us (78%)
  local copies, waits for them, and re-layouts  10.9 us (13%)
  other arithmetic  3.78 us (5%)
  matrix products  2.2 us (3%)
  between operations  0.94 us (1%)
    pallas_call x1, Pallas kernels, run_experts(): pl.pallas_call(functools.partial(expert_kernel, seq_size, tp_size, slices...  41.3 us
    pallas_call x1, Pallas kernels, exchange(): pl.pallas_call(functools.partial(exchange_kernel, seq_size, tp_size, scal...  22.8 us
    pad x1, local copies, waits for them, and re-layouts, body(): fresh_value = jnp.pad(new_value, ((0, 0), (0, 128 - steps), (0, 0)))  1.73 us

profile of v11, /device:TPU:1, one launch (start us, length us, event | category | flops | bytes accessed | tf_op | source)
XLA Modules:
  0.0 82.0 jit_solution(6415495516091206944)
XLA Ops:
  0.7 0.8 bitcast_select_fusion.query_ref
  1.5 0.8 compare_convert_fusion
  2.3 0.6 broadcast_in_dim.110.usable_ref
  3.0 1.0 %fusion = f32[3,64,4]{2,1,0:T(8,128)S(1)} fusion(bf16[3,64,1024]{2,1,0:T(8,128)(2,1)S(1)} %bitcast_select_fusion.query_ref, bf16[3,4,1024]{2,1,0:T(4,128)(2,1)} %param.16, pred[64,4]{1,0:T(8,128)(4,1)S(1)} %get-tuple-element.17), kind=kOutput, calls=%fused_computation.1 | convolution fusion | flops 1574400 | bytes 421120 | tf_op jit(solution)/shard_map/rqd,rsd->rqs/dot_general | solution.py:461
  4.0 0.6 pad.27.fresh_ref
  4.7 0.6 pad.28.fresh_ok_ref
  5.3 1.7 %pad.29.fresh_value_ref = bf16[3,128,1024]{2,1,0:T(8,128)(2,1)} pad(bf16[3,4,1024]{2,1,0:T(4,128)(2,1)} %param.17, bf16[]{:T(256)} %constant.122.clone.1), padding=0_0x0_124x0_0 | pad | bytes 811010 | tf_op jit(solution)/shard_map/jit(_pad)/pad | solution.py:474
  7.0 0.8 copy.38
  7.9 0.6 pad.30.ids_ref
  8.5 22.8 %shard_map.149 = (f32[4,3,16,1024]{3,2,1,0:T(8,128)}, s32[32,8,128]{2,1,0:T(8,128)}) custom-call(bf16[3,64,1024]{2,1,0:T(8,128)(2,1)} %copy-done.1, bf16[3,1024,1024]{2,1,0:T(8,128)(2,1)} %key_hbm.1, bf16[3,1024,1024]{2,1,0:T(8,128)(2,1)} %value_hbm.1, f32[3,8,1024]{2,1,0:T(8,128)} %broadcast_in_dim.110.usable_ref, f32[3,64,128]{2,1,0:T(8,128)} %pad.27.fresh_ref, ...), custom_call_target="tpu_custom_call" | custom-call | tf_op jit(solution)/shard_map/pallas_call | solution.py:148
  31.4 0.6 pad.31.hidden_ref
  32.0 0.9 %slice_reduce_fusion = s32[32,24]{1,0:T(8,128)S(1)} fusion(s32[32,8,128]{2,1,0:T(8,128)} %get-tuple-element.8), kind=kLoop, calls=%fused_computation.20 | loop fusion | bytes 6144 | tf_op jit(solution)/shard_map/slice | solution.py:482
  33.0 0.1 reshape_squeeze.3
  33.1 0.1 copy.40
  33.3 0.1 copy.41
  33.4 0.1 fusion.18
  33.8 0.1 copy.39
  34.0 0.1 fusion.4
  34.1 0.1 copy.46
  34.3 0.7 copy.47
  35.0 0.1 copy.50
  35.2 0.7 pad_convert_fusion.pick_out_ref
  35.9 41.3 %shard_map.150 = (bf16[32,16,128]{2,1,0:T(8,128)(2,1)}, f32[16,1024]{1,0:T(8,128)}, bf16[16,1024]{1,0:T(8,128)(2,1)}) custom-call(f32[4,3,16,1024]{3,2,1,0:T(8,128)} %get-tuple-element.7.sums_ref, f32[16,1024]{1,0:T(8,128)} %pad.31.hidden_ref, bf16[1024,1024]{1,0:T(8,128)(2,1)} %out_weight_hbm.1, f32[1,1024]{1,0:T(1,128)} %bitcast.33, ...), custom_call_target="tpu_custom_call" | custom-call | tf_op jit(solution)/shard_map/pallas_call | solution.py:390
  77.3 0.9 %reshape.208 = f32[3,4,1024]{2,1,0:T(4,128)S(1)} reshape(f32[12,1024]{1,0:T(8,128)} %bitcast.28) | data formatting | bytes 98304 | tf_op jit(solution)/shard_map/reshape | solution.py:519
  78.1 0.6 dynamic-slice_convert_fusion
  78.8 0.8 reshape.209
  79.5 0.1 fusion.7
  79.7 0.2 select_reduce_fusion.2
  79.8 0.1 copy.51
  80.1 0.1 copy.53
  80.3 1.1 %fusion.5 = f32[12,1,2,128]{3,1,2,0:T(1,128)S(1)} fusion(f32[12,16,1,1]{1,2,3,0:T(1,128)S(1)} %bitcast.32, bf16[16,2,12,128]{3,2,1,0:T(8,128)(2,1)} %bitcast.27), kind=kOutput, calls=%fused_computation.10 | convolution fusion | flops 589824 | bytes 111360 | tf_op jit(solution)/shard_map/ia,ahif->ihf/dot_general | solution.py:539
  81.4 0.6 fusion.11
  (36 shorter events, 0.9 us)
Async XLA Ops:
  0.6 78.9 %copy-start = (bf16[1024,16]{0,1:T(8,128)(2,1)S(1)}, bf16[1024,16]{0,1:T(8,128)(2,1)}, u32[]{:S(2)}) copy-start(bf16[1024,16]{0,1:T(8,128)(2,1)} %param.23) | copy-start | bytes 98308
  1.5 7.0 %copy-start.1 = (bf16[3,64,1024]{2,1,0:T(8,128)(2,1)}, bf16[3,64,1024]{2,1,0:T(8,128)(2,1)S(1)}, u32[]{:S(2)}) copy-start(bf16[3,64,1024]{2,1,0:T(8,128)(2,1)S(1)} %bitcast_select_fusion.query_ref) | copy-start | bytes 1179652
  8.5 22.8 %copy-start.2 = (bf16[3,4,1024]{2,1,0:T(4,128)(2,1)S(1)}, bf16[3,4,1024]{2,1,0:T(4,128)(2,1)}, u32[]{:S(2)}) copy-start(bf16[3,4,1024]{2,1,0:T(4,128)(2,1)} %param.14) | copy-start | bytes 73732
  31.4 48.3 %copy-start.3 = (s32[3,4,2]{1,2,0:T(2,128)S(1)}, s32[3,4,2]{1,2,0:T(2,128)}, u32[]{:S(2)}) copy-start(s32[3,4,2]{1,2,0:T(2,128)} %param.24) | copy-start | bytes 292

commit v12 on v11

--- a/solution.py
+++ b/solution.py
@@ -167,7 +167,7 @@
             pltpu.SemaphoreType.DMA((tp_size,)),
         ],
         compiler_params=pltpu.CompilerParams(
-            collective_id=0, has_side_effects=True
+            collective_id=0, has_side_effects=True, vmem_limit_bytes=48 * 1024 * 1024
         ),
     )(query, key_cache, value_cache, usable, fresh, fresh_ok, fresh_value, ids)
 

time: 82.5 us -> 76.9 us (0.932)
  local copies, waits for them, and re-layouts: 10.9 us -> 7.47 us
  Pallas kernels: 64.2 us -> 62 us
    pallas_call x1, Pallas kernels: 22.8 us -> 20.6 us  [exchange(): pl.pallas_call(functools.partial(exchange_kernel, seq_size, tp_size, scal...]
    pad x1, local copies, waits for them, and re-layouts: 1.73 us -> 0.82 us  [body(): fresh_value = jnp.pad(new_value, ((0, 0), (0, 128 - steps), (0, 0)))]
    slice x1, local copies, waits for them, and re-layouts: 0.95 us -> 0.04 us  [body(): all_id_pieces[:, 0, :id_count].reshape(tp_size * req_dev, steps, -1)]
    unnamed x9, local copies, waits for them, and re-layouts: 0.81 us -> 1.67 us
where the time goes in v12:
time: 76.9 us; the launch traced here: 76.4 us
  Pallas kernels  62 us (81%)
  local copies, waits for them, and re-layouts  7.47 us (10%)
  other arithmetic  3.74 us (5%)
  matrix products  2.2 us (3%)
  between operations  0.98 us (1%)
    pallas_call x1, Pallas kernels, run_experts(): pl.pallas_call(functools.partial(expert_kernel, seq_size, tp_size, slices...  41.4 us
    pallas_call x1, Pallas kernels, exchange(): pl.pallas_call(functools.partial(exchange_kernel, seq_size, tp_size, scal...  20.6 us
    unnamed x9, local copies, waits for them, and re-layouts  1.67 us

profile of v12, /device:TPU:1, one launch (start us, length us, event | category | flops | bytes accessed | tf_op | source)
XLA Modules:
  0.0 76.4 jit_solution(8537602821618138163)
XLA Ops:
  0.7 0.8 %bitcast_select_fusion.query_ref = bf16[3,64,1024]{2,1,0:T(8,128)(2,1)S(1)} fusion(pred[64,1024]{1,0:T(8,128)(4,1)S(1)} %bitcast.26, bf16[3,4,1024]{2,1,0:T(4,128)(2,1)} %param.15), kind=kLoop, calls=%fused_computation.2 | loop fusion | flops 196608 | bytes 483328 | tf_op jit(solution)/shard_map/jit(_where)/select_n | solution.py:454
  1.5 0.7 compare_convert_fusion
  2.3 0.1 fusion.17
  2.4 1.0 %fusion = f32[3,64,4]{2,1,0:T(8,128)S(1)} fusion(bf16[3,64,1024]{2,1,0:T(8,128)(2,1)S(1)} %bitcast_select_fusion.query_ref, bf16[3,4,1024]{2,1,0:T(4,128)(2,1)} %param.16, pred[64,4]{1,0:T(8,128)(4,1)S(1)} %get-tuple-element.17), kind=kOutput, calls=%fused_computation.1 | convolution fusion | flops 1574400 | bytes 421120 | tf_op jit(solution)/shard_map/rqd,rsd->rqs/dot_general | solution.py:461
  3.4 0.8 %pad.29.fresh_value_ref = bf16[3,128,1024]{2,1,0:T(8,128)(2,1)S(1)} pad(bf16[3,4,1024]{2,1,0:T(4,128)(2,1)} %param.17, bf16[]{:T(256)} %constant.122.clone.1), padding=0_0x0_124x0_0 | pad | bytes 811010 | tf_op jit(solution)/shard_map/jit(_pad)/pad | solution.py:474
  4.2 0.8 %copy.38 = s32[3,4,2]{2,1,0:T(4,128)S(1)} copy(s32[3,4,2]{1,2,0:T(2,128)} %param.24) | data formatting | bytes 192 | tf_op args[10]
  5.0 0.1 reshape.202
  5.1 20.6 %shard_map.149 = (f32[4,3,16,1024]{3,2,1,0:T(8,128)S(1)}, s32[32,8,128]{2,1,0:T(8,128)S(1)}) custom-call(bf16[3,64,1024]{2,1,0:T(8,128)(2,1)S(1)} %bitcast_select_fusion.query_ref, bf16[3,1024,1024]{2,1,0:T(8,128)(2,1)} %key_hbm.1, bf16[3,1024,1024]{2,1,0:T(8,128)(2,1)} %value_hbm.1, f32[3,8,1024]{2,1,0:T(8,128)S(1)} %broadcast_in_dim.110.usable_ref, ...), custom_call_target="tpu_custom_call" | custom-call | tf_op jit(solution)/shard_map/pallas_call | solution.py:148
  25.8 0.9 %copy-done.1 = f32[4,3,16,1024]{3,2,1,0:T(8,128)} copy-done((f32[4,3,16,1024]{3,2,1,0:T(8,128)}, f32[4,3,16,1024]{3,2,1,0:T(8,128)S(1)}, u32[]{:S(2)}) %copy-start.1) | copy-done | bytes 786456
  26.6 0.6 pad.31.hidden_ref
  27.3 0.1 reshape_squeeze.3
  27.5 0.1 copy.40
  27.6 0.1 copy.41
  27.7 0.1 fusion.18
  27.9 0.1 copy.43
  28.1 0.1 copy.39
  28.3 0.1 fusion.4
  28.4 0.1 copy.46
  28.7 0.7 copy.47
  29.4 0.1 copy.50
  29.6 0.7 pad_convert_fusion.pick_out_ref
  30.3 41.4 %shard_map.150 = (bf16[32,16,128]{2,1,0:T(8,128)(2,1)}, f32[16,1024]{1,0:T(8,128)}, bf16[16,1024]{1,0:T(8,128)(2,1)}) custom-call(f32[4,3,16,1024]{3,2,1,0:T(8,128)} %copy-done.1, f32[16,1024]{1,0:T(8,128)} %pad.31.hidden_ref, bf16[1024,1024]{1,0:T(8,128)(2,1)} %out_weight_hbm.1, f32[1,1024]{1,0:T(1,128)} %bitcast.33, bf16[64,512]{1,0:T(8,128)(2,1)} %bitcast.25, ...), custom_call_target="tpu_custom_call" | custom-call | tf_op jit(solution)/shard_map/pallas_call | solution.py:390
  71.7 0.9 %reshape.208 = f32[3,4,1024]{2,1,0:T(4,128)S(1)} reshape(f32[12,1024]{1,0:T(8,128)} %bitcast.28) | data formatting | bytes 98304 | tf_op jit(solution)/shard_map/reshape | solution.py:519
  72.6 0.6 dynamic-slice_convert_fusion
  73.2 0.8 %reshape.209 = bf16[3,4,1024]{2,1,0:T(4,128)(2,1)S(1)} reshape(bf16[12,1024]{1,0:T(8,128)(2,1)} %bitcast.31) | data formatting | bytes 49152 | tf_op jit(solution)/shard_map/reshape | solution.py:520
  74.0 0.1 fusion.7
  74.1 0.2 select_reduce_fusion.2
  74.3 0.1 copy.51
  74.5 0.1 copy.53
  74.6 0.1 select_reduce_fusion.1
  74.7 1.1 %fusion.5 = f32[12,1,2,128]{3,1,2,0:T(1,128)S(1)} fusion(f32[12,16,1,1]{1,2,3,0:T(1,128)S(1)} %bitcast.32, bf16[16,2,12,128]{3,2,1,0:T(8,128)(2,1)} %bitcast.27), kind=kOutput, calls=%fused_computation.10 | convolution fusion | flops 589824 | bytes 111360 | tf_op jit(solution)/shard_map/ia,ahif->ihf/dot_general | solution.py:539
  75.8 0.6 fusion.11
  (36 shorter events, 0.7 us)
Async XLA Ops:
  0.6 73.3 %copy-start = (bf16[1024,16]{0,1:T(8,128)(2,1)S(1)}, bf16[1024,16]{0,1:T(8,128)(2,1)}, u32[]{:S(2)}) copy-start(bf16[1024,16]{0,1:T(8,128)(2,1)} %param.23) | copy-start | bytes 98308
  5.1 21.5 %copy-start.2 = (bf16[3,4,1024]{2,1,0:T(4,128)(2,1)S(1)}, bf16[3,4,1024]{2,1,0:T(4,128)(2,1)}, u32[]{:S(2)}) copy-start(bf16[3,4,1024]{2,1,0:T(4,128)(2,1)} %param.14) | copy-start | bytes 73732
  25.7 0.9 %copy-start.1 = (f32[4,3,16,1024]{3,2,1,0:T(8,128)}, f32[4,3,16,1024]{3,2,1,0:T(8,128)S(1)}, u32[]{:S(2)}) copy-start(f32[4,3,16,1024]{3,2,1,0:T(8,128)S(1)} %get-tuple-element.7.sums_ref) | copy-start | bytes 2359300
  26.6 47.5 %copy-start.3 = (s32[3,4,2]{1,2,0:T(2,128)S(1)}, s32[3,4,2]{1,2,0:T(2,128)}, u32[]{:S(2)}) copy-start(s32[3,4,2]{1,2,0:T(2,128)} %param.24) | copy-start | bytes 292

commit v13 on v12

--- a/solution.py
+++ b/solution.py
@@ -238,14 +238,16 @@
     attention = jnp.dot(
         context[...].astype(jnp.bfloat16), out_weight_ref[...], preferred_element_type=jnp.float32
     )
-    attn_ref[...] = attention
+    for r in range(req_dev):
+        attn_ref[r] = attention[r * steps : (r + 1) * steps, :]
     residual = hidden_ref[...] + attention
     mean_square = jnp.mean(residual * residual, axis=1, keepdims=True)
     normed = (residual * lax.rsqrt(mean_square + norm_epsilon) * gain_ref[...]).astype(
         jnp.bfloat16
     )
     piece_ref[...] = normed
-    normed_ref[...] = normed
+    for r in range(req_dev):
+        normed_ref[r] = normed[r * steps : (r + 1) * steps, :]
 
     far = (seq_size - 1) * halves
     near = tp_size - 1 + far
@@ -391,8 +393,8 @@
         functools.partial(expert_kernel, seq_size, tp_size, slices),
         out_shape=(
             jax.ShapeDtypeStruct((tp_size, tokens, chunk), jnp.bfloat16),
-            jax.ShapeDtypeStruct((tokens, width), jnp.float32),
-            jax.ShapeDtypeStruct((tokens, width), jnp.bfloat16),
+            jax.ShapeDtypeStruct((sums.shape[1], sums.shape[2] // 4, width), jnp.float32),
+            jax.ShapeDtypeStruct((sums.shape[1], sums.shape[2] // 4, width), jnp.bfloat16),
         ),
         in_specs=[vmem, vmem, hbm, vmem, vmem, hbm, hbm, hbm, vmem],
         out_specs=(vmem, vmem, vmem),
@@ -516,8 +518,6 @@
         block_sums, hidden, out_weight, norm_gain.reshape(1, width), pick_in, gate_weight,
         up_weight, down_weight, pick_out, seq_size, tp_size, slices,
     )
-    attention = attention[:own].reshape(req_dev, steps, width)
-    normed = normed[:own].reshape(req_dev, steps, width)
     attn_out = lax.dynamic_slice_in_dim(
         attention, seq_index * feature_block, feature_block, 2
     ).astype(jnp.bfloat16)

time: 76.9 us -> 77.5 us (level)
  local copies, waits for them, and re-layouts: 7.47 us -> 6.54 us
    reshape x2 -> x0, local copies, waits for them, and re-layouts: 1.63 us -> none  [the longest x1 0.86 us: body(): attention = attention[:own].reshape(req_dev, steps, width)]
where the time goes in v13:
time: 77.5 us; the launch traced here: 76.9 us
  Pallas kernels  62 us (80%)
  local copies, waits for them, and re-layouts  6.54 us (8%)
  other arithmetic  4.44 us (6%)
  matrix products  2.94 us (4%)
  between operations  0.97 us (1%)
    pallas_call x1, Pallas kernels, run_experts(): pl.pallas_call(functools.partial(expert_kernel, seq_size, tp_size, slices...  41.4 us
    pallas_call x1, Pallas kernels, exchange(): pl.pallas_call(functools.partial(exchange_kernel, seq_size, tp_size, scal...  20.6 us
    unnamed x9, local copies, waits for them, and re-layouts  1.67 us

profile of v13, /device:TPU:1, one launch (start us, length us, event | category | flops | bytes accessed | tf_op | source)
XLA Modules:
  0.0 76.9 jit_solution(18228752129378054808)
XLA Ops:
  0.7 0.8 %bitcast_select_fusion.query_ref = bf16[3,64,1024]{2,1,0:T(8,128)(2,1)S(1)} fusion(pred[64,1024]{1,0:T(8,128)(4,1)S(1)} %bitcast.24, bf16[3,4,1024]{2,1,0:T(4,128)(2,1)} %param.15), kind=kLoop, calls=%fused_computation.2 | loop fusion | flops 196608 | bytes 483328 | tf_op jit(solution)/shard_map/jit(_where)/select_n | solution.py:456
  1.5 0.7 compare_convert_fusion
  2.3 0.1 fusion.17
  2.4 1.0 %fusion = f32[3,64,4]{2,1,0:T(8,128)S(1)} fusion(bf16[3,64,1024]{2,1,0:T(8,128)(2,1)S(1)} %bitcast_select_fusion.query_ref, bf16[3,4,1024]{2,1,0:T(4,128)(2,1)} %param.16, pred[64,4]{1,0:T(8,128)(4,1)S(1)} %get-tuple-element.17), kind=kOutput, calls=%fused_computation.1 | convolution fusion | flops 1574400 | bytes 421120 | tf_op jit(solution)/shard_map/rqd,rsd->rqs/dot_general | solution.py:463
  3.4 0.8 %pad.29.fresh_value_ref = bf16[3,128,1024]{2,1,0:T(8,128)(2,1)S(1)} pad(bf16[3,4,1024]{2,1,0:T(4,128)(2,1)} %param.17, bf16[]{:T(256)} %constant.122.clone.1), padding=0_0x0_124x0_0 | pad | bytes 811010 | tf_op jit(solution)/shard_map/jit(_pad)/pad | solution.py:476
  4.2 0.8 %copy.38 = s32[3,4,2]{2,1,0:T(4,128)S(1)} copy(s32[3,4,2]{1,2,0:T(2,128)} %param.24) | data formatting | bytes 192 | tf_op args[10]
  5.0 0.1 reshape.196
  5.1 20.6 %shard_map.149 = (f32[4,3,16,1024]{3,2,1,0:T(8,128)S(1)}, s32[32,8,128]{2,1,0:T(8,128)S(1)}) custom-call(bf16[3,64,1024]{2,1,0:T(8,128)(2,1)S(1)} %bitcast_select_fusion.query_ref, bf16[3,1024,1024]{2,1,0:T(8,128)(2,1)} %key_hbm.1, bf16[3,1024,1024]{2,1,0:T(8,128)(2,1)} %value_hbm.1, f32[3,8,1024]{2,1,0:T(8,128)S(1)} %broadcast_in_dim.110.usable_ref, ...), custom_call_target="tpu_custom_call" | custom-call | tf_op jit(solution)/shard_map/pallas_call | solution.py:148
  25.8 0.9 %copy-done.1 = f32[4,3,16,1024]{3,2,1,0:T(8,128)} copy-done((f32[4,3,16,1024]{3,2,1,0:T(8,128)}, f32[4,3,16,1024]{3,2,1,0:T(8,128)S(1)}, u32[]{:S(2)}) %copy-start.1) | copy-done | bytes 786456
  26.6 0.6 pad.31.hidden_ref
  27.3 0.1 reshape_squeeze.3
  27.5 0.1 copy.40
  27.6 0.1 copy.41
  27.7 0.1 fusion.18
  27.9 0.1 copy.43
  28.0 0.1 broadcast_add_fusion
  28.1 0.1 copy.39
  28.3 0.1 fusion.4
  28.4 0.1 copy.46
  28.7 0.7 copy.47
  29.4 0.1 copy.50
  29.6 0.7 pad_convert_fusion.pick_out_ref
  30.3 41.4 %shard_map.150 = (bf16[32,16,128]{2,1,0:T(8,128)(2,1)}, f32[3,4,1024]{2,1,0:T(4,128)}, bf16[3,4,1024]{2,1,0:T(4,128)(2,1)}) custom-call(f32[4,3,16,1024]{3,2,1,0:T(8,128)} %copy-done.1, f32[16,1024]{1,0:T(8,128)} %pad.31.hidden_ref, bf16[1024,1024]{1,0:T(8,128)(2,1)} %out_weight_hbm.1, f32[1,1024]{1,0:T(1,128)} %bitcast.29, bf16[64,512]{1,0:T(8,128)(2,1)} %bitcast.23, ...), custom_call_target="tpu_custom_call" | custom-call | tf_op jit(solution)/shard_map/pallas_call | solution.py:392
  71.7 1.3 %dynamic-slice_convert_fusion = bf16[3,4,256]{2,1,0:T(4,128)(2,1)} fusion(f32[3,4,1024]{2,1,0:T(4,128)} %get-tuple-element.9, s32[]{:T(128)S(6)} %select_n.96), kind=kLoop, calls=%fused_computation.28 | loop fusion | bytes 12292 | tf_op jit(solution)/shard_map/convert_element_type | solution.py:523
  73.0 0.9 %fusion.7 = f32[3,4,16]{2,1,0:T(4,128)S(1)} fusion(bf16[3,4,1024]{2,1,0:T(4,128)(2,1)} %get-tuple-element.10, bf16[1024,16]{0,1:T(8,128)(2,1)S(1)} %copy-done), kind=kOutput, calls=%fused_computation.16 | convolution fusion | flops 393216 | bytes 58112 | tf_op jit(solution)/shard_map/rtd,de->rte/dot_general | solution.py:526
  73.9 0.2 select_reduce_fusion.2
  74.1 0.1 copy.51
  74.2 0.1 compare_select_fusion
  74.3 0.1 copy.53
  74.4 0.1 select_reduce_fusion.1
  74.5 1.1 %fusion.5 = f32[12,1,2,128]{3,1,2,0:T(1,128)S(1)} fusion(f32[12,16,1,1]{1,2,3,0:T(1,128)S(1)} %bitcast.28, bf16[16,2,12,128]{3,2,1,0:T(8,128)(2,1)} %bitcast.25), kind=kOutput, calls=%fused_computation.10 | convolution fusion | flops 589824 | bytes 111360 | tf_op jit(solution)/shard_map/ia,ahif->ihf/dot_general | solution.py:539
  75.6 1.3 %fusion.11 = bf16[3,4,256]{2,1,0:T(4,128)(2,1)} fusion(f32[3,4,256]{2,1,0:T(4,128)S(1)} %reshape.204, f32[3,4,1024]{2,1,0:T(4,128)S(1)} %convert_element_type.42, s32[]{:T(128)S(6)} %select_n.96, f32[3,4,1024]{2,1,0:T(4,128)} %get-tuple-element.9), kind=kLoop, calls=%fused_computation.24 | loop fusion | flops 9216 | bytes 43012 | tf_op jit(solution)/shard_map/convert_element_type | solution.py:543
  (34 shorter events, 0.5 us)
Async XLA Ops:
  0.6 72.4 %copy-start = (bf16[1024,16]{0,1:T(8,128)(2,1)S(1)}, bf16[1024,16]{0,1:T(8,128)(2,1)}, u32[]{:S(2)}) copy-start(bf16[1024,16]{0,1:T(8,128)(2,1)} %param.23) | copy-start | bytes 98308
  5.1 21.5 %copy-start.2 = (bf16[3,4,1024]{2,1,0:T(4,128)(2,1)S(1)}, bf16[3,4,1024]{2,1,0:T(4,128)(2,1)}, u32[]{:S(2)}) copy-start(bf16[3,4,1024]{2,1,0:T(4,128)(2,1)} %param.14) | copy-start | bytes 73732
  25.7 0.9 %copy-start.1 = (f32[4,3,16,1024]{3,2,1,0:T(8,128)}, f32[4,3,16,1024]{3,2,1,0:T(8,128)S(1)}, u32[]{:S(2)}) copy-start(f32[4,3,16,1024]{3,2,1,0:T(8,128)S(1)} %get-tuple-element.7.sums_ref) | copy-start | bytes 2359300
  26.6 47.3 %copy-start.3 = (s32[3,4,2]{1,2,0:T(2,128)S(1)}, s32[3,4,2]{1,2,0:T(2,128)}, u32[]{:S(2)}) copy-start(s32[3,4,2]{1,2,0:T(2,128)} %param.24) | copy-start | bytes 292

commit v14 on v12

--- a/solution.py
+++ b/solution.py
@@ -293,7 +293,9 @@
     gate = lax.dot_general(buffer, gate_ref[...], contract, preferred_element_type=jnp.float32)
     upward = lax.dot_general(buffer, up_ref[...], contract, preferred_element_type=jnp.float32)
     inner = (jax.nn.gelu(gate) * upward).astype(jnp.bfloat16)
-    part[...] = jnp.dot(inner, down_ref[...], preferred_element_type=jnp.float32)
+    part[...] = jnp.dot(inner, down_ref[...], preferred_element_type=jnp.float32).astype(
+        part.dtype
+    )
 
     def stage1(i):
         return pltpu.make_async_remote_copy(
@@ -337,9 +339,9 @@
                 device_id_type=mesh_type,
             ).wait_recv()
 
-    total = recv[0]
+    total = recv[0].astype(jnp.float32)
     for k in range(1, slices):
-        total = total + recv[k]
+        total = total + recv[k].astype(jnp.float32)
     middle[...] = total.astype(middle.dtype)
 
     picked = jnp.dot(
@@ -405,8 +407,8 @@
             pltpu.VMEM((tokens, width), jnp.bfloat16),
             pltpu.VMEM((tokens, width), jnp.float32),
             pltpu.VMEM((tp_size, tokens, width), jnp.bfloat16),
-            pltpu.VMEM((rows, width), jnp.float32),
-            pltpu.VMEM((slices, rows, chunk), jnp.float32),
+            pltpu.VMEM((rows, width), jnp.bfloat16),
+            pltpu.VMEM((slices, rows, chunk), jnp.bfloat16),
             pltpu.VMEM((rows, chunk), jnp.bfloat16),
             pltpu.VMEM((tp_size, tokens, chunk), jnp.bfloat16),
             pltpu.VMEM((tp_size, tokens, chunk), jnp.bfloat16),

time: 76.9 us -> 75.6 us (0.983)
  Pallas kernels: 62 us -> 60.7 us
    pallas_call x1, Pallas kernels: 41.4 us -> 40.1 us  [run_experts(): pl.pallas_call(functools.partial(expert_kernel, seq_size, tp_size, slices...]
where the time goes in v14:
time: 75.6 us; the launch traced here: 75.1 us
  Pallas kernels  60.7 us (80%)
  local copies, waits for them, and re-layouts  7.47 us (10%)
  other arithmetic  3.74 us (5%)
  matrix products  2.2 us (3%)
  between operations  0.98 us (1%)
    pallas_call x1, Pallas kernels, run_experts(): pl.pallas_call(functools.partial(expert_kernel, seq_size, tp_size, slices...  40.1 us
    pallas_call x1, Pallas kernels, exchange(): pl.pallas_call(functools.partial(exchange_kernel, seq_size, tp_size, scal...  20.6 us
    unnamed x9, local copies, waits for them, and re-layouts  1.67 us

profile of v14, /device:TPU:1, one launch (start us, length us, event | category | flops | bytes accessed | tf_op | source)
XLA Modules:
  0.0 75.1 jit_solution(8455071704187364530)
XLA Ops:
  0.7 0.8 %bitcast_select_fusion.query_ref = bf16[3,64,1024]{2,1,0:T(8,128)(2,1)S(1)} fusion(pred[64,1024]{1,0:T(8,128)(4,1)S(1)} %bitcast.26, bf16[3,4,1024]{2,1,0:T(4,128)(2,1)} %param.15), kind=kLoop, calls=%fused_computation.2 | loop fusion | flops 196608 | bytes 483328 | tf_op jit(solution)/shard_map/jit(_where)/select_n | solution.py:456
  1.5 0.7 compare_convert_fusion
  2.3 0.1 fusion.17
  2.4 1.0 %fusion = f32[3,64,4]{2,1,0:T(8,128)S(1)} fusion(bf16[3,64,1024]{2,1,0:T(8,128)(2,1)S(1)} %bitcast_select_fusion.query_ref, bf16[3,4,1024]{2,1,0:T(4,128)(2,1)} %param.16, pred[64,4]{1,0:T(8,128)(4,1)S(1)} %get-tuple-element.17), kind=kOutput, calls=%fused_computation.1 | convolution fusion | flops 1574400 | bytes 421120 | tf_op jit(solution)/shard_map/rqd,rsd->rqs/dot_general | solution.py:463
  3.4 0.8 %pad.29.fresh_value_ref = bf16[3,128,1024]{2,1,0:T(8,128)(2,1)S(1)} pad(bf16[3,4,1024]{2,1,0:T(4,128)(2,1)} %param.17, bf16[]{:T(256)} %constant.122.clone.1), padding=0_0x0_124x0_0 | pad | bytes 811010 | tf_op jit(solution)/shard_map/jit(_pad)/pad | solution.py:476
  4.2 0.8 %copy.38 = s32[3,4,2]{2,1,0:T(4,128)S(1)} copy(s32[3,4,2]{1,2,0:T(2,128)} %param.24) | data formatting | bytes 192 | tf_op args[10]
  5.0 0.1 reshape.202
  5.1 20.6 %shard_map.149 = (f32[4,3,16,1024]{3,2,1,0:T(8,128)S(1)}, s32[32,8,128]{2,1,0:T(8,128)S(1)}) custom-call(bf16[3,64,1024]{2,1,0:T(8,128)(2,1)S(1)} %bitcast_select_fusion.query_ref, bf16[3,1024,1024]{2,1,0:T(8,128)(2,1)} %key_hbm.1, bf16[3,1024,1024]{2,1,0:T(8,128)(2,1)} %value_hbm.1, f32[3,8,1024]{2,1,0:T(8,128)S(1)} %broadcast_in_dim.110.usable_ref, ...), custom_call_target="tpu_custom_call" | custom-call | tf_op jit(solution)/shard_map/pallas_call | solution.py:148
  25.8 0.9 %copy-done.1 = f32[4,3,16,1024]{3,2,1,0:T(8,128)} copy-done((f32[4,3,16,1024]{3,2,1,0:T(8,128)}, f32[4,3,16,1024]{3,2,1,0:T(8,128)S(1)}, u32[]{:S(2)}) %copy-start.1) | copy-done | bytes 786456
  26.6 0.6 pad.31.hidden_ref
  27.3 0.1 reshape_squeeze.3
  27.5 0.1 copy.40
  27.6 0.1 copy.41
  27.7 0.1 fusion.18
  27.9 0.1 copy.43
  28.1 0.1 copy.39
  28.3 0.1 fusion.4
  28.4 0.1 copy.46
  28.7 0.7 copy.47
  29.4 0.1 copy.50
  29.6 0.7 pad_convert_fusion.pick_out_ref
  30.3 40.1 %shard_map.150 = (bf16[32,16,128]{2,1,0:T(8,128)(2,1)}, f32[16,1024]{1,0:T(8,128)}, bf16[16,1024]{1,0:T(8,128)(2,1)}) custom-call(f32[4,3,16,1024]{3,2,1,0:T(8,128)} %copy-done.1, f32[16,1024]{1,0:T(8,128)} %pad.31.hidden_ref, bf16[1024,1024]{1,0:T(8,128)(2,1)} %out_weight_hbm.1, f32[1,1024]{1,0:T(1,128)} %bitcast.33, bf16[64,512]{1,0:T(8,128)(2,1)} %bitcast.25, ...), custom_call_target="tpu_custom_call" | custom-call | tf_op jit(solution)/shard_map/pallas_call | solution.py:392
  70.4 0.9 %reshape.208 = f32[3,4,1024]{2,1,0:T(4,128)S(1)} reshape(f32[12,1024]{1,0:T(8,128)} %bitcast.28) | data formatting | bytes 98304 | tf_op jit(solution)/shard_map/reshape | solution.py:521
  71.3 0.6 dynamic-slice_convert_fusion
  71.9 0.8 %reshape.209 = bf16[3,4,1024]{2,1,0:T(4,128)(2,1)S(1)} reshape(bf16[12,1024]{1,0:T(8,128)(2,1)} %bitcast.31) | data formatting | bytes 49152 | tf_op jit(solution)/shard_map/reshape | solution.py:522
  72.7 0.1 fusion.7
  72.8 0.2 select_reduce_fusion.2
  73.0 0.1 copy.51
  73.2 0.1 copy.53
  73.3 0.1 select_reduce_fusion.1
  73.4 1.1 %fusion.5 = f32[12,1,2,128]{3,1,2,0:T(1,128)S(1)} fusion(f32[12,16,1,1]{1,2,3,0:T(1,128)S(1)} %bitcast.32, bf16[16,2,12,128]{3,2,1,0:T(8,128)(2,1)} %bitcast.27), kind=kOutput, calls=%fused_computation.10 | convolution fusion | flops 589824 | bytes 111360 | tf_op jit(solution)/shard_map/ia,ahif->ihf/dot_general | solution.py:541
  74.5 0.6 fusion.11
  (36 shorter events, 0.7 us)
Async XLA Ops:
  0.6 72.0 %copy-start = (bf16[1024,16]{0,1:T(8,128)(2,1)S(1)}, bf16[1024,16]{0,1:T(8,128)(2,1)}, u32[]{:S(2)}) copy-start(bf16[1024,16]{0,1:T(8,128)(2,1)} %param.23) | copy-start | bytes 98308
  5.1 21.5 %copy-start.2 = (bf16[3,4,1024]{2,1,0:T(4,128)(2,1)S(1)}, bf16[3,4,1024]{2,1,0:T(4,128)(2,1)}, u32[]{:S(2)}) copy-start(bf16[3,4,1024]{2,1,0:T(4,128)(2,1)} %param.14) | copy-start | bytes 73732
  25.7 0.9 %copy-start.1 = (f32[4,3,16,1024]{3,2,1,0:T(8,128)}, f32[4,3,16,1024]{3,2,1,0:T(8,128)S(1)}, u32[]{:S(2)}) copy-start(f32[4,3,16,1024]{3,2,1,0:T(8,128)S(1)} %get-tuple-element.7.sums_ref) | copy-start | bytes 2359300
  26.6 46.2 %copy-start.3 = (s32[3,4,2]{1,2,0:T(2,128)S(1)}, s32[3,4,2]{1,2,0:T(2,128)}, u32[]{:S(2)}) copy-start(s32[3,4,2]{1,2,0:T(2,128)} %param.24) | copy-start | bytes 292

commit v15 on v14

--- a/solution.py
+++ b/solution.py
@@ -264,24 +264,15 @@
             device_id=(s, u), device_id_type=mesh_type,
         )
 
-    for u in range(tp_size):
-        @pl.when(t == u)
-        def _():
-            pltpu.make_async_copy(piece_ref, everyone.at[u], recv0.at[u]).start()
-
-        @pl.when(t != u)
-        def _():
-            gather(u, t).start()
-
-    for u in range(tp_size):
-        @pl.when(t == u)
-        def _():
-            pltpu.make_async_copy(piece_ref, everyone.at[u], recv0.at[u]).wait()
-
-        @pl.when(t != u)
-        def _():
-            gather(u, t).wait_send()
-            gather(u, u).wait_recv()
+    pltpu.make_async_copy(piece_ref, everyone.at[t], recv0.at[t]).start()
+    for k in range(1, tp_size):
+        gather((t + k) % tp_size, t).start()
+
+    pltpu.make_async_copy(piece_ref, everyone.at[t], recv0.at[t]).wait()
+    for k in range(1, tp_size):
+        u = (t + k) % tp_size
+        gather(u, t).wait_send()
+        gather(u, u).wait_recv()
 
     for copy in loads[1:]:
         copy.wait()
@@ -357,27 +348,18 @@
             device_id=(s, u), device_id_type=mesh_type,
         )
 
-    for u in range(tp_size):
-        @pl.when(t == u)
-        def _():
-            pltpu.make_async_copy(outgoing.at[u], landing.at[u], recv3.at[u]).start()
-
-        @pl.when(t != u)
-        def _():
-            stage3(u).start()
-
-    for u in range(tp_size):
-        @pl.when(t == u)
-        def _():
-            pltpu.make_async_copy(outgoing.at[u], landing.at[u], recv3.at[u]).wait()
-
-        @pl.when(t != u)
-        def _():
-            stage3(u).wait_send()
-            pltpu.make_async_remote_copy(
-                outgoing.at[u], landing.at[u], send3.at[u], recv3.at[u],
-                device_id=(s, u), device_id_type=mesh_type,
-            ).wait_recv()
+    pltpu.make_async_copy(outgoing.at[t], landing.at[t], recv3.at[t]).start()
+    for k in range(1, tp_size):
+        stage3((t + k) % tp_size).start()
+
+    pltpu.make_async_copy(outgoing.at[t], landing.at[t], recv3.at[t]).wait()
+    for k in range(1, tp_size):
+        u = (t + k) % tp_size
+        stage3(u).wait_send()
+        pltpu.make_async_remote_copy(
+            outgoing.at[u], landing.at[u], send3.at[u], recv3.at[u],
+            device_id=(s, u), device_id_type=mesh_type,
+        ).wait_recv()
 
     out_ref[...] = landing[...]
 

time: 75.6 us -> 71.9 us (0.951)
  Pallas kernels: 60.7 us -> 57 us
    pallas_call x1, Pallas kernels: 40.1 us -> 36.4 us  [run_experts(): pl.pallas_call(functools.partial(expert_kernel, seq_size, tp_size, slices...]
where the time goes in v15:
time: 71.9 us; the launch traced here: 71.4 us
  Pallas kernels  57 us (79%)
  local copies, waits for them, and re-layouts  7.47 us (10%)
  other arithmetic  3.74 us (5%)
  matrix products  2.2 us (3%)
  between operations  0.98 us (1%)
    pallas_call x1, Pallas kernels, run_experts(): pl.pallas_call(functools.partial(expert_kernel, seq_size, tp_size, slices...  36.4 us
    pallas_call x1, Pallas kernels, exchange(): pl.pallas_call(functools.partial(exchange_kernel, seq_size, tp_size, scal...  20.6 us
    unnamed x9, local copies, waits for them, and re-layouts  1.67 us

profile of v15, /device:TPU:1, one launch (start us, length us, event | category | flops | bytes accessed | tf_op | source)
XLA Modules:
  0.0 71.4 jit_solution(7673820508899386407)
XLA Ops:
  0.7 0.8 %bitcast_select_fusion.query_ref = bf16[3,64,1024]{2,1,0:T(8,128)(2,1)S(1)} fusion(pred[64,1024]{1,0:T(8,128)(4,1)S(1)} %bitcast.26, bf16[3,4,1024]{2,1,0:T(4,128)(2,1)} %param.15), kind=kLoop, calls=%fused_computation.2 | loop fusion | flops 196608 | bytes 483328 | tf_op jit(solution)/shard_map/jit(_where)/select_n | solution.py:438
  1.5 0.7 %compare_convert_fusion = f32[3,1024]{1,0:T(4,128)S(1)} fusion(s32[1024]{0:T(1024)S(1)} %iota_add_fusion, s32[3]{0:T(128)} %param.20), kind=kLoop, calls=%fused_computation.21 | loop fusion | flops 6144 | bytes 16396 | tf_op jit(solution)/shard_map/convert_element_type | solution.py:442
  2.3 0.1 fusion.17
  2.4 1.0 %fusion = f32[3,64,4]{2,1,0:T(8,128)S(1)} fusion(bf16[3,64,1024]{2,1,0:T(8,128)(2,1)S(1)} %bitcast_select_fusion.query_ref, bf16[3,4,1024]{2,1,0:T(4,128)(2,1)} %param.16, pred[64,4]{1,0:T(8,128)(4,1)S(1)} %get-tuple-element.17), kind=kOutput, calls=%fused_computation.1 | convolution fusion | flops 1574400 | bytes 421120 | tf_op jit(solution)/shard_map/rqd,rsd->rqs/dot_general | solution.py:445
  3.4 0.8 %pad.29.fresh_value_ref = bf16[3,128,1024]{2,1,0:T(8,128)(2,1)S(1)} pad(bf16[3,4,1024]{2,1,0:T(4,128)(2,1)} %param.17, bf16[]{:T(256)} %constant.122.clone.1), padding=0_0x0_124x0_0 | pad | bytes 811010 | tf_op jit(solution)/shard_map/jit(_pad)/pad | solution.py:458
  4.2 0.8 %copy.38 = s32[3,4,2]{2,1,0:T(4,128)S(1)} copy(s32[3,4,2]{1,2,0:T(2,128)} %param.24) | data formatting | bytes 192 | tf_op args[10]
  5.0 0.1 reshape.202
  5.1 20.6 %shard_map.149 = (f32[4,3,16,1024]{3,2,1,0:T(8,128)S(1)}, s32[32,8,128]{2,1,0:T(8,128)S(1)}) custom-call(bf16[3,64,1024]{2,1,0:T(8,128)(2,1)S(1)} %bitcast_select_fusion.query_ref, bf16[3,1024,1024]{2,1,0:T(8,128)(2,1)} %key_hbm.1, bf16[3,1024,1024]{2,1,0:T(8,128)(2,1)} %value_hbm.1, f32[3,8,1024]{2,1,0:T(8,128)S(1)} %broadcast_in_dim.110.usable_ref, ...), custom_call_target="tpu_custom_call" | custom-call | tf_op jit(solution)/shard_map/pallas_call | solution.py:148
  25.8 0.9 %copy-done.1 = f32[4,3,16,1024]{3,2,1,0:T(8,128)} copy-done((f32[4,3,16,1024]{3,2,1,0:T(8,128)}, f32[4,3,16,1024]{3,2,1,0:T(8,128)S(1)}, u32[]{:S(2)}) %copy-start.1) | copy-done | bytes 786456
  26.6 0.6 pad.31.hidden_ref
  27.3 0.1 reshape_squeeze.3
  27.5 0.1 copy.40
  27.6 0.1 copy.41
  27.7 0.1 fusion.18
  27.9 0.1 copy.43
  28.1 0.1 copy.39
  28.3 0.1 fusion.4
  28.4 0.1 copy.46
  28.7 0.7 %copy.47 = bf16[512,64]{0,1:T(8,128)(2,1)} copy(bf16[512,64]{1,0:T(8,128)(2,1)S(1)} %bitcast.24) | data formatting | bytes 131072 | tf_op jit(solution)/shard_map/transpose | solution.py:493
  29.4 0.1 copy.50
  29.6 0.7 pad_convert_fusion.pick_out_ref
  30.3 36.4 %shard_map.150 = (bf16[32,16,128]{2,1,0:T(8,128)(2,1)}, f32[16,1024]{1,0:T(8,128)}, bf16[16,1024]{1,0:T(8,128)(2,1)}) custom-call(f32[4,3,16,1024]{3,2,1,0:T(8,128)} %copy-done.1, f32[16,1024]{1,0:T(8,128)} %pad.31.hidden_ref, bf16[1024,1024]{1,0:T(8,128)(2,1)} %out_weight_hbm.1, f32[1,1024]{1,0:T(1,128)} %bitcast.33, bf16[64,512]{1,0:T(8,128)(2,1)} %bitcast.25, ...), custom_call_target="tpu_custom_call" | custom-call | tf_op jit(solution)/shard_map/pallas_call | solution.py:374
  66.7 0.9 %reshape.208 = f32[3,4,1024]{2,1,0:T(4,128)S(1)} reshape(f32[12,1024]{1,0:T(8,128)} %bitcast.28) | data formatting | bytes 98304 | tf_op jit(solution)/shard_map/reshape | solution.py:503
  67.6 0.6 dynamic-slice_convert_fusion
  68.2 0.8 %reshape.209 = bf16[3,4,1024]{2,1,0:T(4,128)(2,1)S(1)} reshape(bf16[12,1024]{1,0:T(8,128)(2,1)} %bitcast.31) | data formatting | bytes 49152 | tf_op jit(solution)/shard_map/reshape | solution.py:504
  68.9 0.1 fusion.7
  69.1 0.2 select_reduce_fusion.2
  69.2 0.1 copy.51
  69.5 0.1 copy.53
  69.6 0.1 select_reduce_fusion.1
  69.7 1.1 %fusion.5 = f32[12,1,2,128]{3,1,2,0:T(1,128)S(1)} fusion(f32[12,16,1,1]{1,2,3,0:T(1,128)S(1)} %bitcast.32, bf16[16,2,12,128]{3,2,1,0:T(8,128)(2,1)} %bitcast.27), kind=kOutput, calls=%fused_computation.10 | convolution fusion | flops 589824 | bytes 111360 | tf_op jit(solution)/shard_map/ia,ahif->ihf/dot_general | solution.py:523
  70.8 0.6 fusion.11
  (36 shorter events, 0.7 us)
Async XLA Ops:
  0.6 68.3 %copy-start = (bf16[1024,16]{0,1:T(8,128)(2,1)S(1)}, bf16[1024,16]{0,1:T(8,128)(2,1)}, u32[]{:S(2)}) copy-start(bf16[1024,16]{0,1:T(8,128)(2,1)} %param.23) | copy-start | bytes 98308
  5.1 21.5 %copy-start.2 = (bf16[3,4,1024]{2,1,0:T(4,128)(2,1)S(1)}, bf16[3,4,1024]{2,1,0:T(4,128)(2,1)}, u32[]{:S(2)}) copy-start(bf16[3,4,1024]{2,1,0:T(4,128)(2,1)} %param.14) | copy-start | bytes 73732
  25.7 0.9 %copy-start.1 = (f32[4,3,16,1024]{3,2,1,0:T(8,128)}, f32[4,3,16,1024]{3,2,1,0:T(8,128)S(1)}, u32[]{:S(2)}) copy-start(f32[4,3,16,1024]{3,2,1,0:T(8,128)S(1)} %get-tuple-element.7.sums_ref) | copy-start | bytes 2359300
  26.6 42.5 %copy-start.3 = (s32[3,4,2]{1,2,0:T(2,128)S(1)}, s32[3,4,2]{1,2,0:T(2,128)}, u32[]{:S(2)}) copy-start(s32[3,4,2]{1,2,0:T(2,128)} %param.24) | copy-start | bytes 292

commit v16 on v15

--- a/solution.py
+++ b/solution.py
@@ -100,41 +100,23 @@
             device_id=(s, u), device_id_type=mesh_type,
         )
 
-    for u in range(seq_size):
-        @pl.when(s == u)
-        def _():
-            pltpu.make_async_copy(sums, sums_land.at[u], recv_a.at[u]).start()
-
-        @pl.when(s != u)
-        def _():
-            sums_copy(u, s).start()
-    for u in range(tp_size):
-        @pl.when(t == u)
-        def _():
-            pltpu.make_async_copy(ids_ref, ids_land.at[u], recv_b.at[u]).start()
-
-        @pl.when(t != u)
-        def _():
-            along_tp(u, t).start()
-
-    for u in range(seq_size):
-        @pl.when(s == u)
-        def _():
-            pltpu.make_async_copy(sums, sums_land.at[u], recv_a.at[u]).wait()
-
-        @pl.when(s != u)
-        def _():
-            sums_copy(u, s).wait_send()
-            sums_copy(u, u).wait_recv()
-    for u in range(tp_size):
-        @pl.when(t == u)
-        def _():
-            pltpu.make_async_copy(ids_ref, ids_land.at[u], recv_b.at[u]).wait()
-
-        @pl.when(t != u)
-        def _():
-            along_tp(u, t).wait_send()
-            along_tp(u, u).wait_recv()
+    pltpu.make_async_copy(sums, sums_land.at[s], recv_a.at[s]).start()
+    for k in range(1, seq_size):
+        sums_copy((s + k) % seq_size, s).start()
+    pltpu.make_async_copy(ids_ref, ids_land.at[t], recv_b.at[t]).start()
+    for k in range(1, tp_size):
+        along_tp((t + k) % tp_size, t).start()
+
+    pltpu.make_async_copy(sums, sums_land.at[s], recv_a.at[s]).wait()
+    for k in range(1, seq_size):
+        u = (s + k) % seq_size
+        sums_copy(u, s).wait_send()
+        sums_copy(u, u).wait_recv()
+    pltpu.make_async_copy(ids_ref, ids_land.at[t], recv_b.at[t]).wait()
+    for k in range(1, tp_size):
+        u = (t + k) % tp_size
+        along_tp(u, t).wait_send()
+        along_tp(u, u).wait_recv()
 
     sums_out[...] = sums_land[...]
     ids_out[...] = ids_land[...]

time: 71.9 us -> 72.2 us (level)
  no operation moved by 1% of the time
where the time goes in v16:
time: 72.2 us; the launch traced here: 71.7 us
  Pallas kernels  57.3 us (79%)
  local copies, waits for them, and re-layouts  7.47 us (10%)
  other arithmetic  3.74 us (5%)
  matrix products  2.2 us (3%)
  between operations  0.98 us (1%)
    pallas_call x1, Pallas kernels, run_experts(): pl.pallas_call(functools.partial(expert_kernel, seq_size, tp_size, slices...  36.6 us
    pallas_call x1, Pallas kernels, exchange(): pl.pallas_call(functools.partial(exchange_kernel, seq_size, tp_size, scal...  20.6 us
    unnamed x9, local copies, waits for them, and re-layouts  1.67 us

profile of v16, /device:TPU:1, one launch (start us, length us, event | category | flops | bytes accessed | tf_op | source)
XLA Modules:
  0.0 71.7 jit_solution(597498730128033960)
XLA Ops:
  0.7 0.8 %bitcast_select_fusion.query_ref = bf16[3,64,1024]{2,1,0:T(8,128)(2,1)S(1)} fusion(pred[64,1024]{1,0:T(8,128)(4,1)S(1)} %bitcast.26, bf16[3,4,1024]{2,1,0:T(4,128)(2,1)} %param.15), kind=kLoop, calls=%fused_computation.2 | loop fusion | flops 196608 | bytes 483328 | tf_op jit(solution)/shard_map/jit(_where)/select_n | solution.py:420
  1.5 0.7 %compare_convert_fusion = f32[3,1024]{1,0:T(4,128)S(1)} fusion(s32[1024]{0:T(1024)S(1)} %iota_add_fusion, s32[3]{0:T(128)} %param.20), kind=kLoop, calls=%fused_computation.21 | loop fusion | flops 6144 | bytes 16396 | tf_op jit(solution)/shard_map/convert_element_type | solution.py:424
  2.3 0.1 fusion.17
  2.4 1.0 %fusion = f32[3,64,4]{2,1,0:T(8,128)S(1)} fusion(bf16[3,64,1024]{2,1,0:T(8,128)(2,1)S(1)} %bitcast_select_fusion.query_ref, bf16[3,4,1024]{2,1,0:T(4,128)(2,1)} %param.16, pred[64,4]{1,0:T(8,128)(4,1)S(1)} %get-tuple-element.17), kind=kOutput, calls=%fused_computation.1 | convolution fusion | flops 1574400 | bytes 421120 | tf_op jit(solution)/shard_map/rqd,rsd->rqs/dot_general | solution.py:427
  3.4 0.8 %pad.29.fresh_value_ref = bf16[3,128,1024]{2,1,0:T(8,128)(2,1)S(1)} pad(bf16[3,4,1024]{2,1,0:T(4,128)(2,1)} %param.17, bf16[]{:T(256)} %constant.122.clone.1), padding=0_0x0_124x0_0 | pad | bytes 811010 | tf_op jit(solution)/shard_map/jit(_pad)/pad | solution.py:440
  4.2 0.8 %copy.38 = s32[3,4,2]{2,1,0:T(4,128)S(1)} copy(s32[3,4,2]{1,2,0:T(2,128)} %param.24) | data formatting | bytes 192 | tf_op args[10]
  5.0 0.1 reshape.202
  5.1 20.6 %shard_map.149 = (f32[4,3,16,1024]{3,2,1,0:T(8,128)S(1)}, s32[32,8,128]{2,1,0:T(8,128)S(1)}) custom-call(bf16[3,64,1024]{2,1,0:T(8,128)(2,1)S(1)} %bitcast_select_fusion.query_ref, bf16[3,1024,1024]{2,1,0:T(8,128)(2,1)} %key_hbm.1, bf16[3,1024,1024]{2,1,0:T(8,128)(2,1)} %value_hbm.1, f32[3,8,1024]{2,1,0:T(8,128)S(1)} %broadcast_in_dim.110.usable_ref, ...), custom_call_target="tpu_custom_call" | custom-call | tf_op jit(solution)/shard_map/pallas_call | solution.py:130
  25.8 0.9 %copy-done.1 = f32[4,3,16,1024]{3,2,1,0:T(8,128)} copy-done((f32[4,3,16,1024]{3,2,1,0:T(8,128)}, f32[4,3,16,1024]{3,2,1,0:T(8,128)S(1)}, u32[]{:S(2)}) %copy-start.1) | copy-done | bytes 786456
  26.7 0.6 pad.31.hidden_ref
  27.3 0.1 reshape_squeeze.3
  27.5 0.1 copy.40
  27.6 0.1 copy.41
  27.8 0.1 fusion.18
  27.9 0.1 copy.43
  28.1 0.1 copy.39
  28.3 0.1 fusion.4
  28.4 0.1 copy.46
  28.7 0.7 copy.47
  29.4 0.1 copy.50
  29.6 0.7 pad_convert_fusion.pick_out_ref
  30.3 36.6 %shard_map.150 = (bf16[32,16,128]{2,1,0:T(8,128)(2,1)}, f32[16,1024]{1,0:T(8,128)}, bf16[16,1024]{1,0:T(8,128)(2,1)}) custom-call(f32[4,3,16,1024]{3,2,1,0:T(8,128)} %copy-done.1, f32[16,1024]{1,0:T(8,128)} %pad.31.hidden_ref, bf16[1024,1024]{1,0:T(8,128)(2,1)} %out_weight_hbm.1, f32[1,1024]{1,0:T(1,128)} %bitcast.33, bf16[64,512]{1,0:T(8,128)(2,1)} %bitcast.25, ...), custom_call_target="tpu_custom_call" | custom-call | tf_op jit(solution)/shard_map/pallas_call | solution.py:356
  67.0 0.9 %reshape.208 = f32[3,4,1024]{2,1,0:T(4,128)S(1)} reshape(f32[12,1024]{1,0:T(8,128)} %bitcast.28) | data formatting | bytes 98304 | tf_op jit(solution)/shard_map/reshape | solution.py:485
  67.8 0.6 dynamic-slice_convert_fusion
  68.4 0.8 %reshape.209 = bf16[3,4,1024]{2,1,0:T(4,128)(2,1)S(1)} reshape(bf16[12,1024]{1,0:T(8,128)(2,1)} %bitcast.31) | data formatting | bytes 49152 | tf_op jit(solution)/shard_map/reshape | solution.py:486
  69.2 0.1 fusion.7
  69.4 0.2 select_reduce_fusion.2
  69.5 0.1 copy.51
  69.7 0.1 copy.53
  69.8 0.1 select_reduce_fusion.1
  69.9 1.1 %fusion.5 = f32[12,1,2,128]{3,1,2,0:T(1,128)S(1)} fusion(f32[12,16,1,1]{1,2,3,0:T(1,128)S(1)} %bitcast.32, bf16[16,2,12,128]{3,2,1,0:T(8,128)(2,1)} %bitcast.27), kind=kOutput, calls=%fused_computation.10 | convolution fusion | flops 589824 | bytes 111360 | tf_op jit(solution)/shard_map/ia,ahif->ihf/dot_general | solution.py:505
  71.1 0.6 fusion.11
  (36 shorter events, 0.7 us)
Async XLA Ops:
  0.6 68.6 %copy-start = (bf16[1024,16]{0,1:T(8,128)(2,1)S(1)}, bf16[1024,16]{0,1:T(8,128)(2,1)}, u32[]{:S(2)}) copy-start(bf16[1024,16]{0,1:T(8,128)(2,1)} %param.23) | copy-start | bytes 98308
  5.1 21.5 %copy-start.2 = (bf16[3,4,1024]{2,1,0:T(4,128)(2,1)S(1)}, bf16[3,4,1024]{2,1,0:T(4,128)(2,1)}, u32[]{:S(2)}) copy-start(bf16[3,4,1024]{2,1,0:T(4,128)(2,1)} %param.14) | copy-start | bytes 73732
  25.8 0.9 %copy-start.1 = (f32[4,3,16,1024]{3,2,1,0:T(8,128)}, f32[4,3,16,1024]{3,2,1,0:T(8,128)S(1)}, u32[]{:S(2)}) copy-start(f32[4,3,16,1024]{3,2,1,0:T(8,128)S(1)} %get-tuple-element.7.sums_ref) | copy-start | bytes 2359300
  26.6 42.7 %copy-start.3 = (s32[3,4,2]{1,2,0:T(2,128)S(1)}, s32[3,4,2]{1,2,0:T(2,128)}, u32[]{:S(2)}) copy-start(s32[3,4,2]{1,2,0:T(2,128)} %param.24) | copy-start | bytes 292

commit v17 on v16

--- a/solution.py
+++ b/solution.py
@@ -272,7 +272,7 @@
 
     def stage1(i):
         return pltpu.make_async_remote_copy(
-            part.at[:, pl.ds(i * chunk, chunk)],
+            part.at[:, pl.ds(pl.multiple_of(i * chunk, chunk), chunk)],
             recv.at[j],
             send1.at[i],
             recv1.at[j],
@@ -280,10 +280,14 @@
             device_id_type=mesh_type,
         )
 
-    for i in range(slices):
+    for k in range(slices):
+        i = (j + k) % slices
+
         @pl.when(is_self(i))
         def _():
-            pltpu.make_async_copy(part.at[:, pl.ds(i * chunk, chunk)], recv.at[j], recv1.at[j]).start()
+            pltpu.make_async_copy(
+                part.at[:, pl.ds(pl.multiple_of(i * chunk, chunk), chunk)], recv.at[j], recv1.at[j]
+            ).start()
 
         @pl.when(jnp.logical_not(is_self(i)))
         def _():

time: 72.2 us -> 72.8 us (level)
  no operation moved by 1% of the time
where the time goes in v17:
time: 72.8 us; the launch traced here: 72.3 us
  Pallas kernels  57.9 us (80%)
  local copies, waits for them, and re-layouts  7.47 us (10%)
  other arithmetic  3.74 us (5%)
  matrix products  2.2 us (3%)
  between operations  0.98 us (1%)
    pallas_call x1, Pallas kernels, run_experts(): pl.pallas_call(functools.partial(expert_kernel, seq_size, tp_size, slices...  37.2 us
    pallas_call x1, Pallas kernels, exchange(): pl.pallas_call(functools.partial(exchange_kernel, seq_size, tp_size, scal...  20.6 us
    unnamed x9, local copies, waits for them, and re-layouts  1.67 us

profile of v17, /device:TPU:1, one launch (start us, length us, event | category | flops | bytes accessed | tf_op | source)
XLA Modules:
  0.0 72.3 jit_solution(9546540214169063788)
XLA Ops:
  0.7 0.8 %bitcast_select_fusion.query_ref = bf16[3,64,1024]{2,1,0:T(8,128)(2,1)S(1)} fusion(pred[64,1024]{1,0:T(8,128)(4,1)S(1)} %bitcast.26, bf16[3,4,1024]{2,1,0:T(4,128)(2,1)} %param.15), kind=kLoop, calls=%fused_computation.2 | loop fusion | flops 196608 | bytes 483328 | tf_op jit(solution)/shard_map/jit(_where)/select_n | solution.py:424
  1.5 0.7 %compare_convert_fusion = f32[3,1024]{1,0:T(4,128)S(1)} fusion(s32[1024]{0:T(1024)S(1)} %iota_add_fusion, s32[3]{0:T(128)} %param.20), kind=kLoop, calls=%fused_computation.21 | loop fusion | flops 6144 | bytes 16396 | tf_op jit(solution)/shard_map/convert_element_type | solution.py:428
  2.3 0.1 fusion.17
  2.4 1.0 %fusion = f32[3,64,4]{2,1,0:T(8,128)S(1)} fusion(bf16[3,64,1024]{2,1,0:T(8,128)(2,1)S(1)} %bitcast_select_fusion.query_ref, bf16[3,4,1024]{2,1,0:T(4,128)(2,1)} %param.16, pred[64,4]{1,0:T(8,128)(4,1)S(1)} %get-tuple-element.17), kind=kOutput, calls=%fused_computation.1 | convolution fusion | flops 1574400 | bytes 421120 | tf_op jit(solution)/shard_map/rqd,rsd->rqs/dot_general | solution.py:431
  3.4 0.8 %pad.29.fresh_value_ref = bf16[3,128,1024]{2,1,0:T(8,128)(2,1)S(1)} pad(bf16[3,4,1024]{2,1,0:T(4,128)(2,1)} %param.17, bf16[]{:T(256)} %constant.122.clone.1), padding=0_0x0_124x0_0 | pad | bytes 811010 | tf_op jit(solution)/shard_map/jit(_pad)/pad | solution.py:444
  4.2 0.8 %copy.38 = s32[3,4,2]{2,1,0:T(4,128)S(1)} copy(s32[3,4,2]{1,2,0:T(2,128)} %param.24) | data formatting | bytes 192 | tf_op args[10]
  5.0 0.1 reshape.202
  5.1 20.6 %shard_map.149 = (f32[4,3,16,1024]{3,2,1,0:T(8,128)S(1)}, s32[32,8,128]{2,1,0:T(8,128)S(1)}) custom-call(bf16[3,64,1024]{2,1,0:T(8,128)(2,1)S(1)} %bitcast_select_fusion.query_ref, bf16[3,1024,1024]{2,1,0:T(8,128)(2,1)} %key_hbm.1, bf16[3,1024,1024]{2,1,0:T(8,128)(2,1)} %value_hbm.1, f32[3,8,1024]{2,1,0:T(8,128)S(1)} %broadcast_in_dim.110.usable_ref, ...), custom_call_target="tpu_custom_call" | custom-call | tf_op jit(solution)/shard_map/pallas_call | solution.py:130
  25.8 0.9 %copy-done.1 = f32[4,3,16,1024]{3,2,1,0:T(8,128)} copy-done((f32[4,3,16,1024]{3,2,1,0:T(8,128)}, f32[4,3,16,1024]{3,2,1,0:T(8,128)S(1)}, u32[]{:S(2)}) %copy-start.1) | copy-done | bytes 786456
  26.7 0.6 pad.31.hidden_ref
  27.3 0.1 reshape_squeeze.3
  27.5 0.1 copy.40
  27.6 0.1 copy.41
  27.8 0.1 fusion.18
  27.9 0.1 copy.43
  28.1 0.1 copy.39
  28.3 0.1 fusion.4
  28.4 0.1 copy.46
  28.7 0.7 copy.47
  29.4 0.1 copy.50
  29.6 0.7 pad_convert_fusion.pick_out_ref
  30.3 37.2 %shard_map.150 = (bf16[32,16,128]{2,1,0:T(8,128)(2,1)}, f32[16,1024]{1,0:T(8,128)}, bf16[16,1024]{1,0:T(8,128)(2,1)}) custom-call(f32[4,3,16,1024]{3,2,1,0:T(8,128)} %copy-done.1, f32[16,1024]{1,0:T(8,128)} %pad.31.hidden_ref, bf16[1024,1024]{1,0:T(8,128)(2,1)} %out_weight_hbm.1, f32[1,1024]{1,0:T(1,128)} %bitcast.33, bf16[64,512]{1,0:T(8,128)(2,1)} %bitcast.25, ...), custom_call_target="tpu_custom_call" | custom-call | tf_op jit(solution)/shard_map/pallas_call | solution.py:360
  67.6 0.9 %reshape.208 = f32[3,4,1024]{2,1,0:T(4,128)S(1)} reshape(f32[12,1024]{1,0:T(8,128)} %bitcast.28) | data formatting | bytes 98304 | tf_op jit(solution)/shard_map/reshape | solution.py:489
  68.4 0.6 dynamic-slice_convert_fusion
  69.0 0.8 %reshape.209 = bf16[3,4,1024]{2,1,0:T(4,128)(2,1)S(1)} reshape(bf16[12,1024]{1,0:T(8,128)(2,1)} %bitcast.31) | data formatting | bytes 49152 | tf_op jit(solution)/shard_map/reshape | solution.py:490
  69.8 0.1 fusion.7
  70.0 0.2 select_reduce_fusion.2
  70.1 0.1 copy.51
  70.3 0.1 copy.53
  70.4 0.1 select_reduce_fusion.1
  70.5 1.1 %fusion.5 = f32[12,1,2,128]{3,1,2,0:T(1,128)S(1)} fusion(f32[12,16,1,1]{1,2,3,0:T(1,128)S(1)} %bitcast.32, bf16[16,2,12,128]{3,2,1,0:T(8,128)(2,1)} %bitcast.27), kind=kOutput, calls=%fused_computation.10 | convolution fusion | flops 589824 | bytes 111360 | tf_op jit(solution)/shard_map/ia,ahif->ihf/dot_general | solution.py:509
  71.7 0.6 fusion.11
  (36 shorter events, 0.7 us)
Async XLA Ops:
  0.6 69.2 %copy-start = (bf16[1024,16]{0,1:T(8,128)(2,1)S(1)}, bf16[1024,16]{0,1:T(8,128)(2,1)}, u32[]{:S(2)}) copy-start(bf16[1024,16]{0,1:T(8,128)(2,1)} %param.23) | copy-start | bytes 98308
  5.1 21.5 %copy-start.2 = (bf16[3,4,1024]{2,1,0:T(4,128)(2,1)S(1)}, bf16[3,4,1024]{2,1,0:T(4,128)(2,1)}, u32[]{:S(2)}) copy-start(bf16[3,4,1024]{2,1,0:T(4,128)(2,1)} %param.14) | copy-start | bytes 73732
  25.8 0.9 %copy-start.1 = (f32[4,3,16,1024]{3,2,1,0:T(8,128)}, f32[4,3,16,1024]{3,2,1,0:T(8,128)S(1)}, u32[]{:S(2)}) copy-start(f32[4,3,16,1024]{3,2,1,0:T(8,128)S(1)} %get-tuple-element.7.sums_ref) | copy-start | bytes 2359300
  26.6 43.3 %copy-start.3 = (s32[3,4,2]{1,2,0:T(2,128)S(1)}, s32[3,4,2]{1,2,0:T(2,128)}, u32[]{:S(2)}) copy-start(s32[3,4,2]{1,2,0:T(2,128)} %param.24) | copy-start | bytes 292

commit v18 on v16

--- a/solution.py
+++ b/solution.py
@@ -472,7 +472,12 @@
         return jnp.pad(chosen_rows, ((0, 0), (0, tokens - own), (0, 0))).astype(jnp.bfloat16)
 
     mine = (seq_index * tp_size + tp_index) // slices
-    pick_in = rows_for(mine).reshape(tp_size * tokens, padded).T
+    mine_hit = (all_ids == mine) & (all_slots < capacity)
+    pick_in = jnp.any(
+        mine_hit[None] & (row_of[None] == jnp.arange(padded)[:, None, None, None]), axis=3
+    ).reshape(padded, tp_size, own)
+    pick_in = jnp.pad(pick_in, ((0, 0), (0, 0), (0, tokens - own))).astype(jnp.bfloat16)
+    pick_in = pick_in.reshape(padded, tp_size * tokens)
     held = ((tp_index % slices) // halves) * groups + tp_index // slices
     pick_out = rows_for(held)
     hidden = jnp.pad(

time: 72.2 us -> 72.2 us (level)
    reshape x0 -> x2, local copies, waits for them, and re-layouts: none -> 0.76 us  [the longest x1 0.71 us: body(): pick_in = pick_in.reshape(padded, tp_size * tokens)]
where the time goes in v18:
time: 72.2 us; the launch traced here: 71.7 us
  Pallas kernels  57.3 us (79%)
  local copies, waits for them, and re-layouts  7.47 us (10%)
  other arithmetic  3.75 us (5%)
  matrix products  2.2 us (3%)
  between operations  0.97 us (1%)
    pallas_call x1, Pallas kernels, run_experts(): pl.pallas_call(functools.partial(expert_kernel, seq_size, tp_size, slices...  36.6 us
    pallas_call x1, Pallas kernels, exchange(): pl.pallas_call(functools.partial(exchange_kernel, seq_size, tp_size, scal...  20.6 us
    unnamed x9, local copies, waits for them, and re-layouts  1.67 us

profile of v18, /device:TPU:1, one launch (start us, length us, event | category | flops | bytes accessed | tf_op | source)
XLA Modules:
  0.0 71.7 jit_solution(3148184263496474015)
XLA Ops:
  0.7 0.8 %bitcast_select_fusion.query_ref = bf16[3,64,1024]{2,1,0:T(8,128)(2,1)S(1)} fusion(pred[64,1024]{1,0:T(8,128)(4,1)S(1)} %bitcast.26, bf16[3,4,1024]{2,1,0:T(4,128)(2,1)} %param.15), kind=kLoop, calls=%fused_computation.2 | loop fusion | flops 196608 | bytes 483328 | tf_op jit(solution)/shard_map/jit(_where)/select_n | solution.py:420
  1.5 0.7 %compare_convert_fusion = f32[3,1024]{1,0:T(4,128)S(1)} fusion(s32[1024]{0:T(1024)S(1)} %iota_add_fusion, s32[3]{0:T(128)} %param.20), kind=kLoop, calls=%fused_computation.22 | loop fusion | flops 6144 | bytes 16396 | tf_op jit(solution)/shard_map/convert_element_type | solution.py:424
  2.3 0.1 fusion.17
  2.4 1.0 %fusion = f32[3,64,4]{2,1,0:T(8,128)S(1)} fusion(bf16[3,64,1024]{2,1,0:T(8,128)(2,1)S(1)} %bitcast_select_fusion.query_ref, bf16[3,4,1024]{2,1,0:T(4,128)(2,1)} %param.16, pred[64,4]{1,0:T(8,128)(4,1)S(1)} %get-tuple-element.15), kind=kOutput, calls=%fused_computation.1 | convolution fusion | flops 1574400 | bytes 421120 | tf_op jit(solution)/shard_map/rqd,rsd->rqs/dot_general | solution.py:427
  3.4 0.8 %pad.30.fresh_value_ref = bf16[3,128,1024]{2,1,0:T(8,128)(2,1)S(1)} pad(bf16[3,4,1024]{2,1,0:T(4,128)(2,1)} %param.17, bf16[]{:T(256)} %constant.123.clone.1), padding=0_0x0_124x0_0 | pad | bytes 811010 | tf_op jit(solution)/shard_map/jit(_pad)/pad | solution.py:440
  4.2 0.8 %copy.38 = s32[3,4,2]{2,1,0:T(4,128)S(1)} copy(s32[3,4,2]{1,2,0:T(2,128)} %param.24) | data formatting | bytes 192 | tf_op args[10]
  5.0 0.1 reshape.207
  5.1 20.6 %shard_map.149 = (f32[4,3,16,1024]{3,2,1,0:T(8,128)S(1)}, s32[32,8,128]{2,1,0:T(8,128)S(1)}) custom-call(bf16[3,64,1024]{2,1,0:T(8,128)(2,1)S(1)} %bitcast_select_fusion.query_ref, bf16[3,1024,1024]{2,1,0:T(8,128)(2,1)} %key_hbm.1, bf16[3,1024,1024]{2,1,0:T(8,128)(2,1)} %value_hbm.1, f32[3,8,1024]{2,1,0:T(8,128)S(1)} %broadcast_in_dim.110.usable_ref, ...), custom_call_target="tpu_custom_call" | custom-call | tf_op jit(solution)/shard_map/pallas_call | solution.py:130
  25.8 0.9 %copy-done.1 = f32[4,3,16,1024]{3,2,1,0:T(8,128)} copy-done((f32[4,3,16,1024]{3,2,1,0:T(8,128)}, f32[4,3,16,1024]{3,2,1,0:T(8,128)S(1)}, u32[]{:S(2)}) %copy-start.1) | copy-done | bytes 786456
  26.7 0.6 pad.32.hidden_ref
  27.3 0.1 reshape_squeeze.3
  27.5 0.1 copy.40
  27.6 0.1 copy.41
  27.8 0.1 fusion.18
  27.9 0.1 copy.43
  28.1 0.1 copy.39
  28.4 0.1 copy.46
  28.6 0.7 copy.50.pick_in_ref
  29.4 0.1 copy.49
  29.6 0.7 pad_convert_fusion.pick_out_ref
  30.3 36.6 %shard_map.150 = (bf16[32,16,128]{2,1,0:T(8,128)(2,1)}, f32[16,1024]{1,0:T(8,128)}, bf16[16,1024]{1,0:T(8,128)(2,1)}) custom-call(f32[4,3,16,1024]{3,2,1,0:T(8,128)} %copy-done.1, f32[16,1024]{1,0:T(8,128)} %pad.32.hidden_ref, bf16[1024,1024]{1,0:T(8,128)(2,1)} %out_weight_hbm.1, f32[1,1024]{1,0:T(1,128)} %bitcast.33, bf16[64,512]{1,0:T(8,128)(2,1)} %copy.50.pick_in_ref, ...), custom_call_target="tpu_custom_call" | custom-call | tf_op jit(solution)/shard_map/pallas_call | solution.py:356
  67.0 0.9 %reshape.214 = f32[3,4,1024]{2,1,0:T(4,128)S(1)} reshape(f32[12,1024]{1,0:T(8,128)} %bitcast.28) | data formatting | bytes 98304 | tf_op jit(solution)/shard_map/reshape | solution.py:490
  67.8 0.6 dynamic-slice_convert_fusion
  68.4 0.8 %reshape.215 = bf16[3,4,1024]{2,1,0:T(4,128)(2,1)S(1)} reshape(bf16[12,1024]{1,0:T(8,128)(2,1)} %bitcast.31) | data formatting | bytes 49152 | tf_op jit(solution)/shard_map/reshape | solution.py:491
  69.2 0.1 fusion.7
  69.4 0.2 select_reduce_fusion.2
  69.5 0.1 copy.51
  69.6 0.1 compare_select_fusion
  69.7 0.1 copy.53
  69.8 0.1 select_reduce_fusion.1
  69.9 1.1 %fusion.5 = f32[12,1,2,128]{3,1,2,0:T(1,128)S(1)} fusion(f32[12,16,1,1]{1,2,3,0:T(1,128)S(1)} %bitcast.32, bf16[16,2,12,128]{3,2,1,0:T(8,128)(2,1)} %bitcast.27), kind=kOutput, calls=%fused_computation.11 | convolution fusion | flops 589824 | bytes 111360 | tf_op jit(solution)/shard_map/ia,ahif->ihf/dot_general | solution.py:510
  71.1 0.6 fusion.11
  (37 shorter events, 0.7 us)
Async XLA Ops:
  0.6 68.6 %copy-start = (bf16[1024,16]{0,1:T(8,128)(2,1)S(1)}, bf16[1024,16]{0,1:T(8,128)(2,1)}, u32[]{:S(2)}) copy-start(bf16[1024,16]{0,1:T(8,128)(2,1)} %param.23) | copy-start | bytes 98308
  5.1 21.5 %copy-start.2 = (bf16[3,4,1024]{2,1,0:T(4,128)(2,1)S(1)}, bf16[3,4,1024]{2,1,0:T(4,128)(2,1)}, u32[]{:S(2)}) copy-start(bf16[3,4,1024]{2,1,0:T(4,128)(2,1)} %param.14) | copy-start | bytes 73732
  25.8 0.9 %copy-start.1 = (f32[4,3,16,1024]{3,2,1,0:T(8,128)}, f32[4,3,16,1024]{3,2,1,0:T(8,128)S(1)}, u32[]{:S(2)}) copy-start(f32[4,3,16,1024]{3,2,1,0:T(8,128)S(1)} %get-tuple-element.7.sums_ref) | copy-start | bytes 2359300
  26.6 42.7 %copy-start.3 = (s32[3,4,2]{1,2,0:T(2,128)S(1)}, s32[3,4,2]{1,2,0:T(2,128)}, u32[]{:S(2)}) copy-start(s32[3,4,2]{1,2,0:T(2,128)} %param.24) | copy-start | bytes 292

commit v19 on v16

--- a/solution.py
+++ b/solution.py
@@ -84,7 +84,6 @@
             spread, jnp.where(own_head, total, 0.0),
             precision=lax.Precision.HIGHEST, preferred_element_type=jnp.float32,
         )
-        sums[r, 3 * steps :, :] = jnp.zeros((sums.shape[1] - 3 * steps, width), jnp.float32)
 
     pl.semaphore_wait(barrier, seq_size - 1 + tp_size - 1)
 
@@ -130,7 +129,7 @@
     return pl.pallas_call(
         functools.partial(exchange_kernel, seq_size, tp_size, scale),
         out_shape=(
-            jax.ShapeDtypeStruct((seq_size, req_dev, 4 * steps, width), jnp.float32),
+            jax.ShapeDtypeStruct((seq_size, req_dev, 3 * steps, width), jnp.float32),
             jax.ShapeDtypeStruct((tp_size,) + ids.shape, ids.dtype),
         ),
         in_specs=[vmem, pl.BlockSpec(memory_space=pl.ANY), pl.BlockSpec(memory_space=pl.ANY)]
@@ -139,8 +138,8 @@
         scratch_shapes=[
             pltpu.VMEM(key_cache.shape, key_cache.dtype),
             pltpu.VMEM(value_cache.shape, value_cache.dtype),
-            pltpu.VMEM((req_dev, 4 * steps, width), jnp.float32),
-            pltpu.VMEM((seq_size, req_dev, 4 * steps, width), jnp.float32),
+            pltpu.VMEM((req_dev, 3 * steps, width), jnp.float32),
+            pltpu.VMEM((seq_size, req_dev, 3 * steps, width), jnp.float32),
             pltpu.VMEM((tp_size,) + ids.shape, ids.dtype),
             pltpu.SemaphoreType.DMA((2, req_dev)),
             pltpu.SemaphoreType.DMA((seq_size,)),
@@ -200,7 +199,7 @@
         copy.start()
 
     req_dev = sums_ref.shape[1]
-    steps = sums_ref.shape[2] // 4
+    steps = sums_ref.shape[2] // 3
     context[...] = jnp.zeros_like(context)
     for r in range(req_dev):
         block_sums = [sums_ref[b, r, 0:steps, :] for b in range(seq_size)]

time: 72.2 us -> 72.2 us (level)
  no operation moved by 1% of the time
where the time goes in v19:
time: 72.2 us; the launch traced here: 71.7 us
  Pallas kernels  57.3 us (79%)
  local copies, waits for them, and re-layouts  7.47 us (10%)
  other arithmetic  3.74 us (5%)
  matrix products  2.2 us (3%)
  between operations  0.98 us (1%)
    pallas_call x1, Pallas kernels, run_experts(): pl.pallas_call(functools.partial(expert_kernel, seq_size, tp_size, slices...  36.6 us
    pallas_call x1, Pallas kernels, exchange(): pl.pallas_call(functools.partial(exchange_kernel, seq_size, tp_size, scal...  20.6 us
    unnamed x9, local copies, waits for them, and re-layouts  1.67 us

profile of v19, /device:TPU:1, one launch (start us, length us, event | category | flops | bytes accessed | tf_op | source)
XLA Modules:
  0.0 71.7 jit_solution(16757203800832370613)
XLA Ops:
  0.7 0.8 %bitcast_select_fusion.query_ref = bf16[3,64,1024]{2,1,0:T(8,128)(2,1)S(1)} fusion(pred[64,1024]{1,0:T(8,128)(4,1)S(1)} %bitcast.26, bf16[3,4,1024]{2,1,0:T(4,128)(2,1)} %param.15), kind=kLoop, calls=%fused_computation.2 | loop fusion | flops 196608 | bytes 483328 | tf_op jit(solution)/shard_map/jit(_where)/select_n | solution.py:419
  1.5 0.7 %compare_convert_fusion = f32[3,1024]{1,0:T(4,128)S(1)} fusion(s32[1024]{0:T(1024)S(1)} %iota_add_fusion, s32[3]{0:T(128)} %param.20), kind=kLoop, calls=%fused_computation.21 | loop fusion | flops 6144 | bytes 16396 | tf_op jit(solution)/shard_map/convert_element_type | solution.py:423
  2.3 0.1 fusion.17
  2.4 1.0 %fusion = f32[3,64,4]{2,1,0:T(8,128)S(1)} fusion(bf16[3,64,1024]{2,1,0:T(8,128)(2,1)S(1)} %bitcast_select_fusion.query_ref, bf16[3,4,1024]{2,1,0:T(4,128)(2,1)} %param.16, pred[64,4]{1,0:T(8,128)(4,1)S(1)} %get-tuple-element.17), kind=kOutput, calls=%fused_computation.1 | convolution fusion | flops 1574400 | bytes 421120 | tf_op jit(solution)/shard_map/rqd,rsd->rqs/dot_general | solution.py:426
  3.4 0.8 %pad.29.fresh_value_ref = bf16[3,128,1024]{2,1,0:T(8,128)(2,1)S(1)} pad(bf16[3,4,1024]{2,1,0:T(4,128)(2,1)} %param.17, bf16[]{:T(256)} %constant.122.clone.1), padding=0_0x0_124x0_0 | pad | bytes 811010 | tf_op jit(solution)/shard_map/jit(_pad)/pad | solution.py:439
  4.2 0.8 %copy.38 = s32[3,4,2]{2,1,0:T(4,128)S(1)} copy(s32[3,4,2]{1,2,0:T(2,128)} %param.24) | data formatting | bytes 192 | tf_op args[10]
  5.0 0.1 reshape.202
  5.1 20.6 %shard_map.149 = (f32[4,3,12,1024]{3,2,1,0:T(8,128)S(1)}, s32[32,8,128]{2,1,0:T(8,128)S(1)}) custom-call(bf16[3,64,1024]{2,1,0:T(8,128)(2,1)S(1)} %bitcast_select_fusion.query_ref, bf16[3,1024,1024]{2,1,0:T(8,128)(2,1)} %key_hbm.1, bf16[3,1024,1024]{2,1,0:T(8,128)(2,1)} %value_hbm.1, f32[3,8,1024]{2,1,0:T(8,128)S(1)} %broadcast_in_dim.110.usable_ref, ...), custom_call_target="tpu_custom_call" | custom-call | tf_op jit(solution)/shard_map/pallas_call | solution.py:129
  25.8 0.9 %copy-done.1 = f32[4,3,12,1024]{3,2,1,0:T(8,128)} copy-done((f32[4,3,12,1024]{3,2,1,0:T(8,128)}, f32[4,3,12,1024]{3,2,1,0:T(8,128)S(1)}, u32[]{:S(2)}) %copy-start.1) | copy-done | bytes 589848
  26.7 0.6 pad.31.hidden_ref
  27.3 0.1 reshape_squeeze.3
  27.5 0.1 copy.40
  27.6 0.1 copy.41
  27.8 0.1 fusion.18
  27.9 0.1 copy.43
  28.1 0.1 copy.39
  28.3 0.1 fusion.4
  28.4 0.1 copy.46
  28.7 0.7 copy.47
  29.4 0.1 copy.50
  29.6 0.7 pad_convert_fusion.pick_out_ref
  30.3 36.6 %shard_map.150 = (bf16[32,16,128]{2,1,0:T(8,128)(2,1)}, f32[16,1024]{1,0:T(8,128)}, bf16[16,1024]{1,0:T(8,128)(2,1)}) custom-call(f32[4,3,12,1024]{3,2,1,0:T(8,128)} %copy-done.1, f32[16,1024]{1,0:T(8,128)} %pad.31.hidden_ref, bf16[1024,1024]{1,0:T(8,128)(2,1)} %out_weight_hbm.1, f32[1,1024]{1,0:T(1,128)} %bitcast.33, bf16[64,512]{1,0:T(8,128)(2,1)} %bitcast.25, ...), custom_call_target="tpu_custom_call" | custom-call | tf_op jit(solution)/shard_map/pallas_call | solution.py:355
  67.0 0.9 %reshape.208 = f32[3,4,1024]{2,1,0:T(4,128)S(1)} reshape(f32[12,1024]{1,0:T(8,128)} %bitcast.28) | data formatting | bytes 98304 | tf_op jit(solution)/shard_map/reshape | solution.py:484
  67.8 0.6 dynamic-slice_convert_fusion
  68.4 0.8 %reshape.209 = bf16[3,4,1024]{2,1,0:T(4,128)(2,1)S(1)} reshape(bf16[12,1024]{1,0:T(8,128)(2,1)} %bitcast.31) | data formatting | bytes 49152 | tf_op jit(solution)/shard_map/reshape | solution.py:485
  69.2 0.1 fusion.7
  69.4 0.2 select_reduce_fusion.2
  69.5 0.1 copy.51
  69.7 0.1 copy.53
  69.8 0.1 select_reduce_fusion.1
  69.9 1.1 %fusion.5 = f32[12,1,2,128]{3,1,2,0:T(1,128)S(1)} fusion(f32[12,16,1,1]{1,2,3,0:T(1,128)S(1)} %bitcast.32, bf16[16,2,12,128]{3,2,1,0:T(8,128)(2,1)} %bitcast.27), kind=kOutput, calls=%fused_computation.10 | convolution fusion | flops 589824 | bytes 111360 | tf_op jit(solution)/shard_map/ia,ahif->ihf/dot_general | solution.py:504
  71.1 0.6 fusion.11
  (36 shorter events, 0.7 us)
Async XLA Ops:
  0.6 68.6 %copy-start = (bf16[1024,16]{0,1:T(8,128)(2,1)S(1)}, bf16[1024,16]{0,1:T(8,128)(2,1)}, u32[]{:S(2)}) copy-start(bf16[1024,16]{0,1:T(8,128)(2,1)} %param.23) | copy-start | bytes 98308
  5.1 21.5 %copy-start.2 = (bf16[3,4,1024]{2,1,0:T(4,128)(2,1)S(1)}, bf16[3,4,1024]{2,1,0:T(4,128)(2,1)}, u32[]{:S(2)}) copy-start(bf16[3,4,1024]{2,1,0:T(4,128)(2,1)} %param.14) | copy-start | bytes 73732
  25.8 0.9 %copy-start.1 = (f32[4,3,12,1024]{3,2,1,0:T(8,128)}, f32[4,3,12,1024]{3,2,1,0:T(8,128)S(1)}, u32[]{:S(2)}) copy-start(f32[4,3,12,1024]{3,2,1,0:T(8,128)S(1)} %get-tuple-element.7.sums_ref) | copy-start | bytes 1769476
  26.6 42.7 %copy-start.3 = (s32[3,4,2]{1,2,0:T(2,128)S(1)}, s32[3,4,2]{1,2,0:T(2,128)}, u32[]{:S(2)}) copy-start(s32[3,4,2]{1,2,0:T(2,128)} %param.24) | copy-start | bytes 292
